TPU v7x, 32 devices: a whole 2x2x4 slice. The times are simulated.
32 devices in a mesh: shard: 2 (over core), dp: 16 (over z, y, x).
Axes of the slice: x: 2, y: 2, z: 4, core: 2. Of those that a mesh axis runs over, the one named last changes fastest.
Arguments:
- content: bfloat16 [2, 2048, 768], P(None, ('shard', 'dp')), may hold values from -6 to 6
- query_state: bfloat16 [2, 2048, 768], P(None, ('shard', 'dp')), may hold values from -6 to 6
- token_seg: int32 [2, 2048], P(None, ('shard', 'dp')), may hold values from 0 to 12, as said below
- positions: int32 [2, 2048], P(None, ('shard', 'dp')), may hold values from 0 to 383, as said below
- parent: int32 [2, 2, 13], P(None, 'shard'), may hold values from 0 to 4, as said below
- w_query: bfloat16 [768, 768], P('shard'), may hold values from -0.21875 to 0.21875
- w_key: bfloat16 [768, 768], P('shard'), may hold values from -0.21875 to 0.21875
- w_value: bfloat16 [768, 768], P('shard'), may hold values from -0.21875 to 0.21875
- w_out: bfloat16 [768, 768], P('shard'), may hold values from -0.875 to 0.875
- w_inner: bfloat16 [768, 3072], P('shard'), may hold values from -0.21875 to 0.21875
- w_outer: bfloat16 [3072, 768], P('shard'), may hold values from -0.109375 to 0.109375
- b_inner: bfloat16 [3072], P('shard'), may hold values from -1.75 to 1.75
- b_outer: bfloat16 [768], P('shard'), may hold values from -1.75 to 1.75
- gain_attn: bfloat16 [768], P('shard'), may hold values from 0.5 to 1.5
- bias_attn: bfloat16 [768], P('shard'), may hold values from -1.75 to 1.75
- gain_ffn: bfloat16 [768], P('shard'), may hold values from 0.5 to 1.5
- bias_ffn: bfloat16 [768], P('shard'), may hold values from -1.75 to 1.75
- bias_content: bfloat16 [768], P('shard'), may hold values from -3 to 3
- bias_segment: bfloat16 [768], P('shard'), may hold values from -3 to 3
- seg_embed: bfloat16 [2, 768], P(None, 'shard'), may hold values from -6 to 6
- rel_table: bfloat16 [16, 12], P('shard'), may hold values from -4 to 4
- cot_content: bfloat16 [2, 2048, 768], P(None, ('shard', 'dp')), may hold values from -6 to 6
- cot_query: bfloat16 [2, 2048, 768], P(None, ('shard', 'dp')), may hold values from -6 to 6
Outputs:
- out_content: bfloat16 [2, 2048, 768], P(None, ('shard', 'dp'))
- out_query: bfloat16 [2, 2048, 768], P(None, ('shard', 'dp'))
- grad_content: float32 [2, 2048, 768], P(None, ('shard', 'dp'))
- grad_query: float32 [2, 2048, 768], P(None, ('shard', 'dp'))
- grad_w_query: float32 [768, 768], P('shard')
- grad_w_key: float32 [768, 768], P('shard')
- grad_w_value: float32 [768, 768], P('shard')
- grad_w_out: float32 [768, 768], P('shard')
- grad_w_inner: float32 [768, 3072], P('shard')
- grad_w_outer: float32 [3072, 768], P('shard')
- grad_b_inner: float32 [3072], P('shard')
- grad_b_outer: float32 [768], P('shard')
- grad_gain_attn: float32 [768], P('shard')
- grad_bias_attn: float32 [768], P('shard')
- grad_gain_ffn: float32 [768], P('shard')
- grad_bias_ffn: float32 [768], P('shard')
- grad_bias_content: float32 [768], P('shard')
- grad_bias_segment: float32 [768], P('shard')
- grad_seg_embed: float32 [2, 768], P(None, 'shard')
- grad_rel_table: float32 [16, 12], P('shard')
Inputs may be any that keep to these rules, and one draw needn't show every extreme that they name: `token_seg`: each tree's 1024 tokens fall in 16 runs of 64 tokens; four runs carry segment 0 (the trunk), one run each carries segments 1 to 4 (branches) and 5 to 12 (leaves). Which run carries which segment is drawn for each tree. The trunk's runs hold positions 0 to 255, run after run in an order drawn for each tree; a branch's run holds 256 to 319 and a leaf's 5 * 64 to 383; positions rise by one along a run. Entry s is the parent segment of segment s: 0 for segment 0 and for the branches 1 to 4; each branch is the parent of exactly two leaves.
All inputs are finite; a program needn't handle non-finite values.
Results may differ from a plain program's by a relative error of at most 0.029.
Values may be sent and summed in bfloat16 or wider, within the bound.
No kernel may reach another device: no remote copies, remote signals or barrier semaphores. Data moves between devices by JAX's collectives and lax.ppermute only.
A program may use at most 192 MiB of HBM per device.

v0:
```python
import jax
import jax.numpy as jnp
from jax import lax
from jax.sharding import PartitionSpec as P

thresholds = (1, 2, 4, 8, 32, 128, 512)
norm_eps = 1e-05
masked_score = -1e30
highest = lax.Precision.HIGHEST


def layer_norm(inputs, norm_gain, norm_shift):
    row_mean = jnp.mean(inputs, axis=-1, keepdims=True)
    centred = inputs - row_mean
    spread = jnp.mean(centred * centred, axis=-1, keepdims=True)
    return centred * lax.rsqrt(spread + norm_eps) * norm_gain + norm_shift


def gelu_tanh(inputs):
    return jax.nn.gelu(inputs, approximate=True)


def bucket_of(query_pos, key_pos):
    offset = query_pos[:, None] - key_pos[None, :]
    magnitude = jnp.abs(offset)
    bucket = jnp.zeros(offset.shape, jnp.int32)
    for threshold in thresholds:
        bucket = bucket + (magnitude >= threshold).astype(jnp.int32)
    return bucket + 8 * (offset < 0).astype(jnp.int32)


def path_of(row_segment, parent_row):
    segment_ids = jnp.arange(parent_row.shape[0], dtype=jnp.int32)
    parent_one = jnp.sum(
        jnp.where(row_segment[:, None] == segment_ids[None, :], parent_row[None, :], 0), axis=1
    )
    parent_two = jnp.sum(
        jnp.where(parent_one[:, None] == segment_ids[None, :], parent_row[None, :], 0), axis=1
    )
    return (parent_one, parent_two)


def bucket_table(bucket, bucket_total):
    bucket_ids = jnp.arange(bucket_total, dtype=jnp.int32)
    return (bucket[None] == bucket_ids[:, None, None]).astype(jnp.bfloat16)


def shards(
    content,
    query_state,
    token_seg,
    positions,
    parent,
    w_query,
    w_key,
    w_value,
    w_out,
    w_inner,
    w_outer,
    b_inner,
    b_outer,
    gain_attn,
    bias_attn,
    gain_ffn,
    bias_ffn,
    bias_content,
    bias_segment,
    seg_embed,
    rel_table,
    cot_content,
    cot_query,
):
    micro_count = content.shape[0]
    row_count = content.shape[1]
    model_width = content.shape[2]
    head_count = rel_table.shape[1]
    bucket_total = rel_table.shape[0] * lax.axis_size("shard")
    head_size = model_width // head_count
    score_scale = head_size ** (-0.5)
    tree_tokens = row_count * lax.axis_size("dp")
    key_block = min(512, tree_tokens)
    block_count = tree_tokens // key_block
    dp_index = lax.axis_index("dp")
    both_count = 2 * row_count
    outputs_content = []
    outputs_query = []
    grads_content = []
    grads_query = []
    owned_shares = []
    for micro_index in range(micro_count):
        gathered = (
            lax.all_gather(w_query, "shard", axis=0, tiled=True),
            lax.all_gather(w_key, "shard", axis=0, tiled=True),
            lax.all_gather(w_value, "shard", axis=0, tiled=True),
            lax.all_gather(w_out, "shard", axis=0, tiled=True),
            lax.all_gather(w_inner, "shard", axis=0, tiled=True),
            lax.all_gather(w_outer, "shard", axis=0, tiled=True),
            lax.all_gather(b_inner, "shard", axis=0, tiled=True),
            lax.all_gather(b_outer, "shard", axis=0, tiled=True),
            lax.all_gather(gain_attn, "shard", axis=0, tiled=True),
            lax.all_gather(bias_attn, "shard", axis=0, tiled=True),
            lax.all_gather(gain_ffn, "shard", axis=0, tiled=True),
            lax.all_gather(bias_ffn, "shard", axis=0, tiled=True),
            lax.all_gather(bias_content, "shard", axis=0, tiled=True),
            lax.all_gather(bias_segment, "shard", axis=0, tiled=True),
            lax.all_gather(seg_embed, "shard", axis=1, tiled=True),
            lax.all_gather(rel_table, "shard", axis=0, tiled=True),
        )
        full_query, full_key, full_value, full_out, full_inner, full_outer = gathered[:6]
        reduced_table = gathered[15]
        (
            inner_bias,
            outer_bias,
            attn_gain,
            attn_shift,
            ffn_gain,
            ffn_shift,
            content_bias,
            segment_bias,
            segment_embed,
            bias_table,
        ) = [membership_mask.astype(jnp.float32) for membership_mask in gathered[6:]]
        content_rows = content[micro_index]
        query_rows = query_state[micro_index]
        row_segments = token_seg[micro_index]
        position_of_rows = positions[micro_index]
        parent_row = parent[micro_index, 0]
        both_rows = jnp.concatenate([content_rows, query_rows], axis=0)
        own_kv = jnp.concatenate(
            [
                jnp.dot(content_rows, full_key, preferred_element_type=jnp.float32),
                jnp.dot(content_rows, full_value, preferred_element_type=jnp.float32),
            ],
            axis=1,
        ).astype(jnp.bfloat16)
        tree_kv, key_segments, key_positions = (
            lax.all_gather(own_kv, "dp", axis=0, tiled=True),
            lax.all_gather(row_segments, "dp", axis=0, tiled=True),
            lax.all_gather(position_of_rows, "dp", axis=0, tiled=True),
        )
        query_raw = jnp.dot(both_rows, full_query, preferred_element_type=jnp.float32)
        query_low = (
            (query_raw + content_bias)
            .astype(jnp.bfloat16)
            .reshape(both_count, head_count, head_size)
        )
        query_segment = (query_raw + segment_bias).reshape(both_count, head_count, head_size)
        seg_heads = segment_embed.reshape(2, head_count, head_size)
        seg_score = jnp.einsum("qhd,chd->hqc", query_segment, seg_heads, precision=highest)
        score_other = seg_score[:, :, 0][:, :, None]
        score_same = seg_score[:, :, 1][:, :, None]
        row_segment = jnp.concatenate([row_segments, row_segments])
        row_pos = jnp.concatenate([position_of_rows, position_of_rows])
        own_index = dp_index * row_count + jnp.arange(row_count, dtype=jnp.int32)
        row_index = jnp.concatenate([own_index, own_index])
        row_query = jnp.arange(both_count, dtype=jnp.int32) >= row_count
        parent_one, parent_two = path_of(row_segment, parent_row)
        kv_blocks = tree_kv.reshape(block_count, key_block, 2 * model_width)
        seg_blocks = key_segments.reshape(block_count, key_block)
        pos_blocks = key_positions.reshape(block_count, key_block)
        block_starts = jnp.arange(block_count, dtype=jnp.int32) * key_block
        block_items = (kv_blocks, seg_blocks, pos_blocks, block_starts)

        def visible_of(block_seg, start):
            key_index = start + jnp.arange(key_block, dtype=jnp.int32)
            visible = (block_seg[None, :] == row_segment[:, None]) | (
                block_seg[None, :] == parent_one[:, None]
            )
            visible = visible | (block_seg[None, :] == parent_two[:, None])
            return visible & jnp.logical_not(
                row_query[:, None] & (key_index[None, :] == row_index[:, None])
            )

        def scores_of(block_kv, block_seg, block_pos, visible):
            key_heads = block_kv[:, :model_width].reshape(key_block, head_count, head_size)
            raw_scores = jnp.einsum(
                "qhd,khd->hqk", query_low, key_heads, preferred_element_type=jnp.float32
            )
            same_seg = block_seg[None, :] == row_segment[:, None]
            seg_term = jnp.where(same_seg[None], score_same, score_other)
            indicator_rows = bucket_table(bucket_of(row_pos, block_pos), bucket_total)
            rel_bias = jnp.einsum(
                "nar,nf->far", indicator_rows, reduced_table, preferred_element_type=jnp.float32
            )
            scores = (raw_scores + seg_term) * score_scale + rel_bias
            return (jnp.where(visible[None], scores, masked_score), same_seg, indicator_rows)

        def extent_step(state_in, element):
            block_kv, block_seg, block_pos, start = element
            visible = visible_of(block_seg, start)
            scores = scores_of(block_kv, block_seg, block_pos, visible)[0]
            row_peak = jnp.maximum(state_in[0], jnp.max(scores, axis=-1))
            row_mass = state_in[1] * jnp.exp(state_in[0] - row_peak)
            row_mass = row_mass + jnp.sum(jnp.exp(scores - row_peak[:, :, None]), axis=-1)
            result = (row_peak, row_mass)
            return (result, None)

        start_state = (
            jnp.full((head_count, both_count), masked_score, jnp.float32),
            jnp.zeros((head_count, both_count), jnp.float32),
        )
        (row_peak, row_mass), _ = lax.scan(extent_step, start_state, block_items)
        log_total = row_peak + jnp.log(row_mass)

        def output_step(state_in, element):
            block_kv, block_seg, block_pos, start = element
            visible = visible_of(block_seg, start)
            scores = scores_of(block_kv, block_seg, block_pos, visible)[0]
            probs_low = jnp.exp(scores - log_total[:, :, None]).astype(jnp.bfloat16)
            value_heads = block_kv[:, model_width:].reshape(key_block, head_count, head_size)
            result = state_in + jnp.einsum(
                "hqk,khd->qhd", probs_low, value_heads, preferred_element_type=jnp.float32
            )
            return (result, None)

        attended_heads, _ = lax.scan(
            output_step, jnp.zeros((both_count, head_count, head_size), jnp.float32), block_items
        )
        attended = attended_heads.reshape(both_count, model_width)
        att_low = attended.astype(jnp.bfloat16)
        branch = jnp.dot(att_low, full_out, preferred_element_type=jnp.float32)
        middle, norm_first = jax.vjp(
            layer_norm, branch + both_rows.astype(jnp.float32), attn_gain, attn_shift
        )
        middle_low = middle.astype(jnp.bfloat16)
        inner_pre = jnp.dot(middle_low, full_inner, preferred_element_type=jnp.float32) + inner_bias
        activated, gelu_back = jax.vjp(gelu_tanh, inner_pre)
        act_low = activated.astype(jnp.bfloat16)
        final_in = (
            jnp.dot(act_low, full_outer, preferred_element_type=jnp.float32) + outer_bias + middle
        )
        final_rows, norm_second = jax.vjp(layer_norm, final_in, ffn_gain, ffn_shift)
        outputs_content.append(final_rows[:row_count].astype(jnp.bfloat16))
        outputs_query.append(final_rows[row_count:].astype(jnp.bfloat16))
        d_final = jnp.concatenate(
            [cot_content[micro_index], cot_query[micro_index]], axis=0
        ).astype(jnp.float32)
        d_final_in, grad_gain_ffn, grad_bias_ffn = norm_second(d_final)
        d_outer = d_final_in.astype(jnp.bfloat16)
        grad_w_outer = jnp.einsum("rf,rd->fd", act_low, d_outer, preferred_element_type=jnp.float32)
        grad_b_outer = jnp.sum(d_outer.astype(jnp.float32), axis=0)
        d_act = jnp.einsum("rd,fd->rf", d_outer, full_outer, preferred_element_type=jnp.float32)
        d_inner = gelu_back(d_act)[0].astype(jnp.bfloat16)
        grad_w_inner = jnp.einsum(
            "rd,rf->df", middle_low, d_inner, preferred_element_type=jnp.float32
        )
        grad_b_inner = jnp.sum(d_inner.astype(jnp.float32), axis=0)
        d_middle = d_final_in + jnp.einsum(
            "rf,df->rd", d_inner, full_inner, preferred_element_type=jnp.float32
        )
        d_mid_in, grad_gain_attn, grad_bias_attn = norm_first(d_middle)
        d_branch = d_mid_in.astype(jnp.bfloat16)
        grad_w_out = jnp.einsum("rd,re->de", att_low, d_branch, preferred_element_type=jnp.float32)
        d_att = jnp.einsum("re,de->rd", d_branch, full_out, preferred_element_type=jnp.float32)
        d_att = d_att.astype(jnp.bfloat16).reshape(both_count, head_count, head_size)
        delta_row = jnp.transpose(jnp.sum(d_att.astype(jnp.float32) * attended_heads, axis=-1))

        def back_step(state_in, element):
            block_kv, block_seg, block_pos, start = element
            visible = visible_of(block_seg, start)
            scores, same_seg, indicator_rows = scores_of(block_kv, block_seg, block_pos, visible)
            key_heads = block_kv[:, :model_width].reshape(key_block, head_count, head_size)
            value_heads = block_kv[:, model_width:].reshape(key_block, head_count, head_size)
            probs = jnp.exp(scores - log_total[:, :, None])
            probs_low = probs.astype(jnp.bfloat16)
            d_probs = jnp.einsum(
                "qhd,khd->hqk", d_att, value_heads, preferred_element_type=jnp.float32
            )
            score_gradient = (probs * (d_probs - delta_row[:, :, None])).astype(jnp.bfloat16)
            d_exact = score_gradient.astype(jnp.float32)
            d_query_part = state_in[0] + jnp.einsum(
                "hqk,khd->qhd", score_gradient, key_heads, preferred_element_type=jnp.float32
            )
            d_same = state_in[1] + jnp.sum(jnp.where(same_seg[None], d_exact, 0.0), axis=-1)
            d_every = state_in[2] + jnp.sum(d_exact, axis=-1)
            d_table = state_in[3] + jnp.einsum(
                "wam,yam->yw", score_gradient, indicator_rows, preferred_element_type=jnp.float32
            )
            d_key = jnp.einsum(
                "hqk,qhd->khd", score_gradient, query_low, preferred_element_type=jnp.float32
            )
            d_value = jnp.einsum(
                "hqk,qhd->khd", probs_low, d_att, preferred_element_type=jnp.float32
            )
            block_grads = jnp.concatenate(
                [
                    d_key.reshape(key_block, model_width) * score_scale,
                    d_value.reshape(key_block, model_width),
                ],
                axis=1,
            )
            return ((d_query_part, d_same, d_every, d_table), block_grads)

        back_state = (
            jnp.zeros((both_count, head_count, head_size), jnp.float32),
            jnp.zeros((head_count, both_count), jnp.float32),
            jnp.zeros((head_count, both_count), jnp.float32),
            jnp.zeros(bias_table.shape, jnp.float32),
        )
        (d_query_content, d_same, d_every, grad_rel_table), key_grads = lax.scan(
            back_step, back_state, block_items
        )
        d_query_content = d_query_content * score_scale
        d_seg = jnp.stack([d_every - d_same, d_same], axis=-1) * score_scale
        d_query_seg = jnp.einsum("hqc,chd->qhd", d_seg, seg_heads, precision=highest)
        grad_seg_embed = jnp.einsum(
            "hqc,qhd->chd", d_seg, query_segment, precision=highest
        ).reshape(2, model_width)
        grad_bias_content = jnp.sum(d_query_content, axis=0).reshape(model_width)
        grad_bias_segment = jnp.sum(d_query_seg, axis=0).reshape(model_width)
        d_query = (
            (d_query_content + d_query_seg).reshape(both_count, model_width).astype(jnp.bfloat16)
        )
        own_kv_grads = lax.psum_scatter(
            key_grads.reshape(tree_tokens, 2 * model_width).astype(jnp.bfloat16),
            "dp",
            scatter_dimension=0,
            tiled=True,
        ).astype(jnp.float32)
        own_kv_grads = own_kv_grads.astype(jnp.bfloat16)
        d_keys = own_kv_grads[:, :model_width]
        d_values = own_kv_grads[:, model_width:]
        grad_w_query = jnp.einsum(
            "rd,re->de", both_rows, d_query, preferred_element_type=jnp.float32
        )
        grad_w_key = jnp.einsum(
            "rd,re->de", content_rows, d_keys, preferred_element_type=jnp.float32
        )
        grad_w_value = jnp.einsum(
            "rd,re->de", content_rows, d_values, preferred_element_type=jnp.float32
        )
        d_both = d_mid_in + jnp.einsum(
            "re,de->rd", d_query, full_query, preferred_element_type=jnp.float32
        )
        grad_rows = d_both[:row_count] + jnp.einsum(
            "re,de->rd", d_keys, full_key, preferred_element_type=jnp.float32
        )
        grad_rows = grad_rows + jnp.einsum(
            "re,de->rd", d_values, full_value, preferred_element_type=jnp.float32
        )
        grads_content.append(grad_rows)
        grads_query.append(d_both[row_count:])
        partial_gradients = [
            grad_w_query,
            grad_w_key,
            grad_w_value,
            grad_w_out,
            grad_w_inner,
            grad_w_outer,
            grad_b_inner,
            grad_b_outer,
            grad_gain_attn,
            grad_bias_attn,
            grad_gain_ffn,
            grad_bias_ffn,
            grad_bias_content,
            grad_bias_segment,
            grad_seg_embed,
            grad_rel_table,
        ]
        shares = (
            lax.psum_scatter(
                partial_gradients[0].astype(jnp.bfloat16), "shard", scatter_dimension=0, tiled=True
            ).astype(jnp.float32),
            lax.psum_scatter(
                partial_gradients[1].astype(jnp.bfloat16), "shard", scatter_dimension=0, tiled=True
            ).astype(jnp.float32),
            lax.psum_scatter(
                partial_gradients[2].astype(jnp.bfloat16), "shard", scatter_dimension=0, tiled=True
            ).astype(jnp.float32),
            lax.psum_scatter(
                partial_gradients[3].astype(jnp.bfloat16), "shard", scatter_dimension=0, tiled=True
            ).astype(jnp.float32),
            lax.psum_scatter(
                partial_gradients[4].astype(jnp.bfloat16), "shard", scatter_dimension=0, tiled=True
            ).astype(jnp.float32),
            lax.psum_scatter(
                partial_gradients[5].astype(jnp.bfloat16), "shard", scatter_dimension=0, tiled=True
            ).astype(jnp.float32),
            lax.psum_scatter(
                partial_gradients[6].astype(jnp.bfloat16), "shard", scatter_dimension=0, tiled=True
            ).astype(jnp.float32),
            lax.psum_scatter(
                partial_gradients[7].astype(jnp.bfloat16), "shard", scatter_dimension=0, tiled=True
            ).astype(jnp.float32),
            lax.psum_scatter(
                partial_gradients[8].astype(jnp.bfloat16), "shard", scatter_dimension=0, tiled=True
            ).astype(jnp.float32),
            lax.psum_scatter(
                partial_gradients[9].astype(jnp.bfloat16), "shard", scatter_dimension=0, tiled=True
            ).astype(jnp.float32),
            lax.psum_scatter(
                partial_gradients[10].astype(jnp.bfloat16), "shard", scatter_dimension=0, tiled=True
            ).astype(jnp.float32),
            lax.psum_scatter(
                partial_gradients[11].astype(jnp.bfloat16), "shard", scatter_dimension=0, tiled=True
            ).astype(jnp.float32),
            lax.psum_scatter(
                partial_gradients[12].astype(jnp.bfloat16), "shard", scatter_dimension=0, tiled=True
            ).astype(jnp.float32),
            lax.psum_scatter(
                partial_gradients[13].astype(jnp.bfloat16), "shard", scatter_dimension=0, tiled=True
            ).astype(jnp.float32),
            lax.psum_scatter(
                partial_gradients[14].astype(jnp.bfloat16), "shard", scatter_dimension=1, tiled=True
            ).astype(jnp.float32),
            lax.psum_scatter(
                partial_gradients[15].astype(jnp.bfloat16), "shard", scatter_dimension=0, tiled=True
            ).astype(jnp.float32),
        )
        if micro_index == 0:
            owned_shares = list(shares)
        else:
            owned_shares = [
                preceding_rows + later for preceding_rows, later in zip(owned_shares, shares)
            ]
    totals = (
        lax.psum(owned_shares[0].astype(jnp.bfloat16), "dp").astype(jnp.float32),
        lax.psum(owned_shares[1].astype(jnp.bfloat16), "dp").astype(jnp.float32),
        lax.psum(owned_shares[2].astype(jnp.bfloat16), "dp").astype(jnp.float32),
        lax.psum(owned_shares[3].astype(jnp.bfloat16), "dp").astype(jnp.float32),
        lax.psum(owned_shares[4].astype(jnp.bfloat16), "dp").astype(jnp.float32),
        lax.psum(owned_shares[5].astype(jnp.bfloat16), "dp").astype(jnp.float32),
        lax.psum(owned_shares[6].astype(jnp.bfloat16), "dp").astype(jnp.float32),
        lax.psum(owned_shares[7].astype(jnp.bfloat16), "dp").astype(jnp.float32),
        lax.psum(owned_shares[8].astype(jnp.bfloat16), "dp").astype(jnp.float32),
        lax.psum(owned_shares[9].astype(jnp.bfloat16), "dp").astype(jnp.float32),
        lax.psum(owned_shares[10].astype(jnp.bfloat16), "dp").astype(jnp.float32),
        lax.psum(owned_shares[11].astype(jnp.bfloat16), "dp").astype(jnp.float32),
        lax.psum(owned_shares[12].astype(jnp.bfloat16), "dp").astype(jnp.float32),
        lax.psum(owned_shares[13].astype(jnp.bfloat16), "dp").astype(jnp.float32),
        lax.psum(owned_shares[14].astype(jnp.bfloat16), "dp").astype(jnp.float32),
        lax.psum(owned_shares[15].astype(jnp.bfloat16), "dp").astype(jnp.float32),
    )
    return (
        jnp.stack(outputs_content),
        jnp.stack(outputs_query),
        jnp.stack(grads_content),
        jnp.stack(grads_query),
        totals[0],
        totals[1],
        totals[2],
        totals[3],
        totals[4],
        totals[5],
        totals[6],
        totals[7],
        totals[8],
        totals[9],
        totals[10],
        totals[11],
        totals[12],
        totals[13],
        totals[14],
        totals[15],
    )


def solution(mesh):
    placed = (
        P(None, ("shard", "dp"), None),
        P(None, ("shard", "dp"), None),
        P(None, ("shard", "dp")),
        P(None, ("shard", "dp")),
        P(None, "shard", None),
        P("shard", None),
        P("shard", None),
        P("shard", None),
        P("shard", None),
        P("shard", None),
        P("shard", None),
        P("shard"),
        P("shard"),
        P("shard"),
        P("shard"),
        P("shard"),
        P("shard"),
        P("shard"),
        P("shard"),
        P(None, "shard"),
        P("shard", None),
        P(None, ("shard", "dp"), None),
        P(None, ("shard", "dp"), None),
    )
    return jax.shard_map(
        shards,
        mesh=mesh,
        in_specs=placed,
        out_specs=(
            P(None, ("shard", "dp"), None),
            P(None, ("shard", "dp"), None),
            P(None, ("shard", "dp"), None),
            P(None, ("shard", "dp"), None),
            P("shard", None),
            P("shard", None),
            P("shard", None),
            P("shard", None),
            P("shard", None),
            P("shard", None),
            P("shard"),
            P("shard"),
            P("shard"),
            P("shard"),
            P("shard"),
            P("shard"),
            P("shard"),
            P("shard"),
            P(None, "shard"),
            P("shard", None),
        ),
        check_vma=False,
    )
```

profile of v0, /device:TPU:0, one launch (start us, length us, event | category | flops | bytes accessed | tf_op | source)
XLA Modules:
  0.0 1132.9 jit_solution(3056973957920240784)
XLA Ops:
  9.5 12.1 %all-gather.23.cloned.1.call-done = bf16[768,768]{1,0:T(8,128)(2,1)} async-done(((bf16[384,768]{1,0:T(8,128)(2,1)}), bf16[768,768]{1,0:T(8,128)(2,1)}) %all-gather.23.cloned.1.call-update) | async-done | bytes 1179664 | tf_op jit(solution)/shard_map/all_gather | solution.py:94
  23.1 10.4 all-gather.21.cloned.1.call-done
  45.9 77.8 %all-reduce.22 = (s32[1024]{0:T(1024)S(1)}, s32[1024]{0:T(1024)S(1)}, s32[1024]{0:T(1024)S(1)}, s32[1024]{0:T(1024)S(1)}) all-reduce(s32[1024]{0:T(1024)S(1)} %fusion.186, s32[1024]{0:T(1024)S(1)} %fusion.187, s32[1024]{0:T(1024)S(1)} %fusion.184, s32[1024]{0:T(1024)S(1)} %fusion.185), channel_id=4, replica_groups=mesh['shard'=2,'dp'=16] {'dp'}, use_global_device_ids=true, to_apply=%add.2 | all-reduce | flops 4096 | bytes 32768
  169.2 41.9 %while.88 = (s32[]{:T(128)}, f32[12,128]{1,0:T(8,128)}, f32[12,128]{1,0:T(8,128)}, s32[2,512]{1,0:T(2,128)}, s32[128]{0:T(128)}, /*index=5*/s32[128]{0:T(128)}, ...) while((s32[]{:T(128)}, f32[12,128]{1,0:T(8,128)}, ...), condition=%wide.region_17.18_spmd.clone, body=%wide.region_14.17_spmd.clone.sunk | while | flops 135405696 | bytes 26121736 | solution.py:202
  212.4 36.2 %while.89 = (s32[]{:T(128)}, f32[128,12,64]{0,2,1:T(8,128)}, bf16[2,512,1536]{1,2,0:T(8,128)(2,1)}, s32[2,512]{1,0:T(2,128)}, s32[128]{0:T(128)}, /*index=5*/s32...) while((s32[]{:T(128)}, f32[128,12,64]{0,2,1:T(8,128)}, ...), condition=%wide.region_19.20_spmd.clone, body=%wide.region_18.19_spmd.clone.sunk | while | flops 235471488 | bytes 22254920 | solution.py:216
  259.5 4.7 copy.220
  264.2 33.8 %while.86 = (s32[]{:T(128)}, f32[12,128]{1,0:T(8,128)S(1)}, f32[12,128]{1,0:T(8,128)S(1)}, s32[2,512]{1,0:T(2,128)S(1)}, s32[128]{0:T(128)}, /*index=5*/s32[128]...) while((s32[]{:T(128)}, f32[12,128]{1,0:T(8,128)S(1)}, ...), condition=%wide.region_5.6_spmd.clone, body=%wide.region_2.5_spmd.clone.sunk | while | flops 135405696 | bytes 25474372 | solution.py:202
  298.6 33.5 %while.87 = (s32[]{:T(128)}, f32[128,12,64]{0,2,1:T(8,128)}, bf16[2,512,1536]{1,2,0:T(8,128)(2,1)}, s32[2,512]{1,0:T(2,128)S(1)}, s32[128]{0:T(128)}, /*index=5*...) while((s32[]{:T(128)}, f32[128,12,64]{0,2,1:T(8,128)}, ...), condition=%wide.region_7.8_spmd.clone, body=%wide.region_6.7_spmd.clone.sunk | while | flops 235471488 | bytes 22254920 | solution.py:216
  361.8 61.9 %while.90 = (s32[]{:T(128)}, f32[128,12,64]{0,2,1:T(8,128)}, f32[12,128]{1,0:T(8,128)}, f32[12,128]{1,0:T(8,128)}, f32[16,12]{1,0:T(8,128)}, /*index=5*/bf16[2,5...) while((s32[]{:T(128)}, f32[128,12,64]{0,2,1:T(8,128)}, ...), condition=%wide.region_32.33_spmd.clone, body=%wide.region_29.32_spmd.clone.sunk | while | flops 573116416 | bytes 66162552 | solution.py:300
  429.1 61.8 %while.91 = (s32[]{:T(128)}, f32[128,12,64]{0,2,1:T(8,128)}, f32[12,128]{1,0:T(8,128)}, f32[12,128]{1,0:T(8,128)}, f32[16,12]{1,0:T(8,128)}, /*index=5*/bf16[2,5...) while((s32[]{:T(128)}, f32[128,12,64]{0,2,1:T(8,128)}, ...), condition=%wide.region_42.43_spmd.clone, body=%wide.region_39.42_spmd.clone.sunk | while | flops 573116416 | bytes 66187156 | solution.py:300
  501.2 52.5 %reduce-scatter.29.cloned.1.call-done = bf16[64,1536]{1,0:T(8,128)(2,1)} async-done(((bf16[1024,1536]{1,0:T(8,128)(2,1)}), bf16[64,1536]{1,0:T(8,128)(2,1)}) %reduce-scatter.29.cloned.1.call-update) | async-done | bytes 196624 | tf_op jit(solution)/shard_map/reduce_scatter | solution.py:314
  556.6 132.5 %reduce-scatter.31.cloned.1.call-done = bf16[64,1536]{1,0:T(8,128)(2,1)} async-done(((bf16[1024,1536]{1,0:T(8,128)(2,1)}), bf16[64,1536]{1,0:T(8,128)(2,1)}) %reduce-scatter.31.cloned.1.call-update) | async-done | bytes 196624 | tf_op jit(solution)/shard_map/reduce_scatter | solution.py:314
  723.4 12.1 %reduce-scatter.35.cloned.1.call-done = bf16[384,768]{1,0:T(8,128)(2,1)} async-done(((bf16[768,768]{1,0:T(8,128)(2,1)}), bf16[384,768]{1,0:T(8,128)(2,1)}) %reduce-scatter.35.cloned.1.call-update) | async-done | bytes 589840 | tf_op jit(solution)/shard_map/reduce_scatter | solution.py:362
  737.8 10.3 reduce-scatter.53.cloned.1.call-done
  749.4 11.3 reduce-scatter.55.cloned.1.call-done
  763.0 10.2 reduce-scatter.49.cloned.1.call-done
  774.6 11.3 reduce-scatter.51.cloned.1.call-done
  788.2 14.4 %reduce-scatter.43.cloned.1.call-done = bf16[384,3072]{1,0:T(8,128)(2,1)} async-done(((bf16[768,3072]{1,0:T(8,128)(2,1)}), bf16[384,3072]{1,0:T(8,128)(2,1)}) %reduce-scatter.43.cloned.1.call-update) | async-done | bytes 2359312 | tf_op jit(solution)/shard_map/reduce_scatter | solution.py:374
  802.6 16.6 %reduce-scatter.41.cloned.1.call-done = bf16[384,3072]{1,0:T(8,128)(2,1)} async-done(((bf16[768,3072]{1,0:T(8,128)(2,1)}), bf16[384,3072]{1,0:T(8,128)(2,1)}) %reduce-scatter.41.cloned.1.call-update) | async-done | bytes 2359312 | tf_op jit(solution)/shard_map/reduce_scatter | solution.py:374
  819.3 4.7 add_convert_fusion.1
  823.9 11.4 %reduce-scatter.47.cloned.1.call-done = bf16[1536,768]{1,0:T(8,128)(2,1)} async-done(((bf16[3072,768]{1,0:T(8,128)(2,1)}), bf16[1536,768]{1,0:T(8,128)(2,1)}) %reduce-scatter.47.cloned.1.call-update) | async-done | bytes 2359312 | tf_op jit(solution)/shard_map/reduce_scatter | solution.py:377
  835.4 16.2 %reduce-scatter.45.cloned.1.call-done = bf16[1536,768]{1,0:T(8,128)(2,1)} async-done(((bf16[3072,768]{1,0:T(8,128)(2,1)}), bf16[1536,768]{1,0:T(8,128)(2,1)}) %reduce-scatter.45.cloned.1.call-update) | async-done | bytes 2359312 | tf_op jit(solution)/shard_map/reduce_scatter | solution.py:377
  874.4 80.5 %all-reduce.23 = (bf16[1536]{0:T(1024)(128)(2,1)S(1)}, bf16[384]{0:T(512)(128)(2,1)S(1)}, bf16[384]{0:T(512)(128)(2,1)S(1)}, bf16[384]{0:T(512)(128)(2,1)S(1)}, ...) all-reduce(bf16[1536]{0:T(1024)(128)(2,1)S(1)} %add_convert_fusion., ...), channel_id=1, replica_groups=mesh['shard'=2,'dp'=16] {'dp'}, use_global_device_ids=true, to_apply=%region_66.67 | all-reduce | flops 5088 | bytes 20352 | tf_op jit(solution)/shard_map/psum | solution.py:424
  965.4 148.7 %all-reduce.28.cloned.1.call-done = (bf16[384,768]{0,1:T(8,128)(2,1)}, bf16[384,768]{0,1:T(8,128)(2,1)}, bf16[384,768]{1,0:T(8,128)(2,1)}, bf16[384,768]{1,0:T(8...) async-done(((bf16[384,768]{0,1:T(8,128)(2,1)}, bf16[384,768]{0,1:T(8,128)(2,1)}, bf16[384,768]{1,0:T(8,128)(2,1)}, bf16[384,768]{1,0:T(8,128)(2,1)}, ...) | async-done | bytes 7077904 | tf_op jit(solution)/shard_map/psum | solution.py:419
  (999 shorter events, 473.4 us)
Async XLA Ops:
  7.9 25.6 %all-gather.21.cloned.1.call-start = ((), (), s32[]{:S(2)}) async-start(), calls=%async_computation.16 | async-start | bytes 1769472 | tf_op jit(solution)/shard_map/all_gather | solution.py:93
  8.7 144.1 %all-gather.27.cloned.1.call-start = ((), (), s32[]{:S(2)}) async-start(), calls=%async_computation.19 | async-start | bytes 1769472 | tf_op jit(solution)/shard_map/all_gather | solution.py:92
  9.4 155.1 %all-gather.35.cloned.1.call-start = ((), (), s32[]{:S(2)}) async-start(), calls=%async_computation.23 | async-start | bytes 3342336 | tf_op jit(solution)/shard_map/all_gather | solution.py:137
  35.8 213.9 %all-gather.29.cloned.1.call-start = ((), (), s32[]{:S(2)}) async-start(), calls=%async_computation.20 | async-start | bytes 1769472 | tf_op jit(solution)/shard_map/all_gather | solution.py:95
  36.4 215.4 %all-gather.31.cloned.1.call-start = ((), (), s32[]{:S(2)}) async-start(), calls=%async_computation.21 | async-start | bytes 7077888 | tf_op jit(solution)/shard_map/all_gather | solution.py:96
  37.2 217.9 %all-gather.33.cloned.1.call-start = ((), (), s32[]{:S(2)}) async-start(), calls=%async_computation.22 | async-start | bytes 7077888 | tf_op jit(solution)/shard_map/all_gather | solution.py:97
  38.0 221.5 %all-gather.25.cloned.1.call-start = ((), (), s32[]{:S(2)}) async-start(), calls=%async_computation.18 | async-start | bytes 3342336 | tf_op jit(solution)/shard_map/all_gather | solution.py:137
  163.9 389.7 %reduce-scatter.29.cloned.1.call-start = ((), (), s32[]{:S(2)}) async-start(), calls=%async_computation.24 | async-start | bytes 3342336 | tf_op jit(solution)/shard_map/reduce_scatter | solution.py:314
  427.1 262.0 %reduce-scatter.31.cloned.1.call-start = ((), (), s32[]{:S(2)}) async-start(), calls=%async_computation.25 | async-start | bytes 3342336 | tf_op jit(solution)/shard_map/reduce_scatter | solution.py:314
  490.9 229.4 %reduce-scatter.37.cloned.1.call-start = ((), (), s32[]{:S(2)}) async-start(), calls=%async_computation.28 | async-start | bytes 1769472 | tf_op jit(solution)/shard_map/reduce_scatter | solution.py:371
  493.6 226.7 %reduce-scatter.39.cloned.1.call-start = ((), (), s32[]{:S(2)}) async-start(), calls=%async_computation.29 | async-start | bytes 1769472 | tf_op jit(solution)/shard_map/reduce_scatter | solution.py:371
  495.4 228.1 %reduce-scatter.33.cloned.1.call-start = ((), (), s32[]{:S(2)}) async-start(), calls=%async_computation.26 | async-start | bytes 1769472 | tf_op jit(solution)/shard_map/reduce_scatter | solution.py:362
  498.2 237.3 %reduce-scatter.35.cloned.1.call-start = ((), (), s32[]{:S(2)}) async-start(), calls=%async_computation.27 | async-start | bytes 1769472 | tf_op jit(solution)/shard_map/reduce_scatter | solution.py:362
  501.1 247.0 %reduce-scatter.53.cloned.1.call-start = ((), (), s32[]{:S(2)}) async-start(), calls=%async_computation.36 | async-start | bytes 1769472
  556.5 204.2 %reduce-scatter.55.cloned.1.call-start = ((), (), s32[]{:S(2)}) async-start(), calls=%async_computation.37 | async-start | bytes 1769472
  692.0 81.3 %reduce-scatter.49.cloned.1.call-start = ((), (), s32[]{:S(2)}) async-start(), calls=%async_computation.34 | async-start | bytes 1769472
  694.2 91.7 %reduce-scatter.51.cloned.1.call-start = ((), (), s32[]{:S(2)}) async-start(), calls=%async_computation.35 | async-start | bytes 1769472
  696.3 106.3 %reduce-scatter.43.cloned.1.call-start = ((), (), s32[]{:S(2)}) async-start(), calls=%async_computation.31 | async-start | bytes 7077888 | tf_op jit(solution)/shard_map/reduce_scatter | solution.py:374
  700.2 119.1 %reduce-scatter.41.cloned.1.call-start = ((), (), s32[]{:S(2)}) async-start(), calls=%async_computation.30 | async-start | bytes 7077888 | tf_op jit(solution)/shard_map/reduce_scatter | solution.py:374
  705.1 130.3 %reduce-scatter.47.cloned.1.call-start = ((), (), s32[]{:S(2)}) async-start(), calls=%async_computation.33 | async-start | bytes 7077888 | tf_op jit(solution)/shard_map/reduce_scatter | solution.py:377
  710.3 141.3 %reduce-scatter.45.cloned.1.call-start = ((), (), s32[]{:S(2)}) async-start(), calls=%async_computation.32 | async-start | bytes 7077888 | tf_op jit(solution)/shard_map/reduce_scatter | solution.py:377
  715.7 154.4 %reduce-scatter.57.cloned.1.call-start = ((), (), s32[]{:S(2)}) async-start(), calls=%async_computation.38 | async-start | bytes 294912
  718.3 155.2 %reduce-scatter.59.cloned.1.call-start = ((), (), s32[]{:S(2)}) async-start(), calls=%async_computation.39 | async-start | bytes 294912
  719.9 394.1 %all-reduce.28.cloned.1.call-start = ((), (), s32[]{:S(2)}) async-start(), calls=%async_computation.40 | async-start | bytes 14155776 | tf_op jit(solution)/shard_map/psum | solution.py:419
  (255 other events, 2553.5 us)
Sparse Core Ops, SparseCore 0:
  9.6 11.9 all-gather.22
  23.1 10.3 all-gather.20
  35.1 10.3 all-gather.26
  48.7 69.4 all-gather.34
  119.5 8.2 all-gather.28
  129.3 15.6 all-gather.30
  146.5 15.5 all-gather.32
  165.4 69.2 all-gather.24
  427.2 126.3 reduce-scatter.28
  559.0 130.0 reduce-scatter.30
  701.4 9.8 reduce-scatter.38
  713.6 9.8 reduce-scatter.32
  725.6 9.8 reduce-scatter.34
  738.2 9.8 reduce-scatter.52
  750.8 9.8 reduce-scatter.54
  763.4 9.8 reduce-scatter.48
  776.0 9.8 reduce-scatter.50
  788.8 13.7 reduce-scatter.42
  805.4 13.7 reduce-scatter.40
  821.6 13.7 reduce-scatter.46
  837.8 13.7 reduce-scatter.44
  853.8 8.7 reduce-scatter.56
  864.7 8.7 reduce-scatter.58
  881.0 233.0 all-reduce.27
  (1 shorter events, 7.8 us)
where the time goes:
time: 1140 us; the launch traced here: 1130 us
  waiting for transfers between devices  477 us (42%)
  blocking collectives  180 us (16%)
  local copies, waits for them, and re-layouts  178 us (16%)
  matrix products  165 us (14%)
  other arithmetic  109 us (10%)
  between operations  19.4 us (2%)
    reduce_scatter x2, waiting for transfers between devices, shards(): lax.psum_scatter(key_grads.reshape(tree_tokens, 2 * model_width).astype(j...  185 us
    psum x1, waiting for transfers between devices, shards(): lax.psum(owned_shares[1].astype(jnp.bfloat16), 'dp').astype(jnp.float32)  149 us
    unnamed x2, blocking collectives  81.4 us
    psum x1, blocking collectives, shards(): lax.psum(owned_shares[6].astype(jnp.bfloat16), 'dp').astype(jnp.float32)  80.5 us
    unnamed x31, waiting for transfers between devices  49.6 us
    dot_general x12, local copies, waits for them, and re-layouts, scores_of(): jnp.einsum('nar,nf->far', indicator_rows, reduced_table, preferred_elemen...  41.6 us
    unnamed x372, local copies, waits for them, and re-layouts  38.8 us
    dot_general x12, matrix products, scores_of(): jnp.einsum('nar,nf->far', indicator_rows, reduced_table, preferred_elemen...  33.7 us
  transfers between devices with their start and end apart: 25, of which 16 were waited for; matrix products, arithmetic and copies ran while one was open for 23% of the time, Pallas kernels for 0%

commit v1 on v0

v1 whole, which is shorter than its diff:
```python
import functools

import jax
import jax.numpy as jnp
from jax import lax
from jax.experimental import pallas as pl
from jax.experimental.pallas import tpu as pltpu
from jax.sharding import PartitionSpec as P

thresholds = (1, 2, 4, 8, 32, 128, 512)
norm_eps = 1e-05
masked_score = -1e30
path_runs = 6
trunk_runs = 4
tree_runs = 16
vmem_bytes = 60 * 1024 * 1024
low = jnp.bfloat16
f32 = jnp.float32
any_space = pl.BlockSpec(memory_space=pl.ANY)
smem_space = pl.BlockSpec(memory_space=pltpu.SMEM)
vmem_space = pl.BlockSpec(memory_space=pltpu.VMEM)


def mm(left, right):
    return lax.dot_general(left, right, (((1,), (0,)), ((), ())), preferred_element_type=f32)


def mm_nt(left, right):
    return lax.dot_general(left, right, (((1,), (1,)), ((), ())), preferred_element_type=f32)


def mm_tn(left, right):
    return lax.dot_general(left, right, (((0,), (0,)), ((), ())), preferred_element_type=f32)


def weight_copies(pieces, target, sems, first, shard):
    if len(pieces) == 1:
        return [pltpu.make_async_copy(pieces[0], target, sems.at[first])]
    half = pieces[0].shape[0]
    own = pl.multiple_of(shard * half, 16)
    other = pl.multiple_of((1 - shard) * half, 16)
    return [
        pltpu.make_async_copy(pieces[0], target.at[pl.ds(own, half)], sems.at[first]),
        pltpu.make_async_copy(pieces[1], target.at[pl.ds(other, half)], sems.at[first + 1]),
    ]


def scalar_at(scalars, slots, micro, entry):
    return scalars[2 + (3 + slots) * micro + entry]


def query_kernel(pieces, scalars, rows, vectors, *refs):
    weights = refs[:pieces]
    query_low, query_segment, full, sems = refs[pieces:]
    copies = weight_copies(weights, full, sems, 0, scalars[0])
    for copy in copies:
        copy.start()
    for copy in copies:
        copy.wait()
    raw = mm(rows[...], full[...])
    query_low[...] = (raw + vectors[9:10, :]).astype(low)
    query_segment[...] = (raw + vectors[10:11, :]).astype(low)


def keys_kernel(pieces, columns, run, slots, scalars, *refs):
    parts = refs[: len(columns)]
    refs = refs[len(columns) :]
    key_weights, value_weights = refs[:pieces], refs[pieces : 2 * pieces]
    path, keys, values, full_key, full_value, sems, path_sems = refs[2 * pieces :]
    shard = scalars[0]
    copies = weight_copies(key_weights, full_key, sems, 0, shard)
    copies = copies + weight_copies(value_weights, full_value, sems, pieces, shard)
    moves = []
    micro_count = path.shape[0]
    for micro in range(micro_count):
        for slot in range(slots):
            relative = scalar_at(scalars, slots, micro, 3 + slot)
            for part, (start, width) in enumerate(columns):
                index = (micro * slots + slot) * len(columns) + part
                moves.append(
                    pltpu.make_async_copy(
                        parts[part].at[relative, pl.ds(micro * run, run), :],
                        path.at[micro, pl.ds(slot * run, run), pl.ds(start, width)],
                        path_sems.at[index],
                    )
                )
    for copy in moves + copies:
        copy.start()
    for copy in moves + copies:
        copy.wait()
    for micro in range(micro_count):
        rows = path[micro]
        span = slots * run
        keys[micro * span : (micro + 1) * span, :] = mm(rows, full_key[...]).astype(low)
        values[micro * span : (micro + 1) * span, :] = mm(rows, full_value[...]).astype(low)


def head_masks():
    lane = lax.broadcasted_iota(jnp.int32, (1, 128), 1)
    first = lane < 64
    return first, first.astype(f32).astype(low), (1.0 - first.astype(f32)).astype(low)


def stack_query(query_low, query_segment, mask_a, mask_b):
    both = jnp.concatenate([query_low, query_segment], axis=1)
    wide_a = jnp.concatenate([mask_a, mask_a], axis=1)
    wide_b = jnp.concatenate([mask_b, mask_b], axis=1)
    return jnp.concatenate([both * wide_a, both * wide_b], axis=0)


def stack_keys(keys, vectors, lo):
    row = lax.broadcasted_iota(jnp.int32, (keys.shape[0], 1), 0)
    segment = jnp.where(row >= lo, vectors[12:13, :], vectors[11:12, :]).astype(low)
    return jnp.concatenate([keys, segment], axis=1)


def offsets_of(base, run, span):
    row = lax.broadcasted_iota(jnp.int32, (run, span), 0)
    column = lax.broadcasted_iota(jnp.int32, (run, span), 1)
    return base + row - column, column


def attend_kernel(run, slots, scalars, table, query_low, query_segment, keys, values, vectors, probs, attended):
    pair, micro = pl.program_id(0), pl.program_id(1)
    base, lo, hi = (scalar_at(scalars, slots, micro, entry) for entry in range(3))
    span = slots * run
    first, mask_a, mask_b = head_masks()
    left = stack_query(query_low[...], query_segment[...], mask_a, mask_b)
    right = stack_keys(keys[...], vectors[...], lo)
    raw = mm_nt(left, right)
    delta, column = offsets_of(base, run, span)
    visible = column < hi
    biases = []
    for head in range(2):
        at = 2 * pair + head
        bias = jnp.full((run, span), table[0, at], f32)
        for step, threshold in enumerate(thresholds):
            if threshold < span:
                bias = jnp.where(delta >= threshold, table[1 + step, at], bias)
                bias = jnp.where(delta <= -threshold, table[9 + step, at], bias)
        bias = jnp.where(visible, bias, masked_score)
        biases.append(bias)
        biases.append(jnp.where(delta == 0, masked_score, bias))
    scores = raw * 0.125 + jnp.concatenate(biases, axis=0)
    peak = jnp.max(scores, axis=-1, keepdims=True)
    mass = jnp.exp(scores - peak)
    total = jnp.sum(mass, axis=-1, keepdims=True)
    probs_low = (mass * (1.0 / total)).astype(low)
    probs[0] = probs_low
    heads = mm(probs_low, values[...])
    attended[...] = jnp.where(first, heads[: 2 * run], heads[2 * run :])


def norm_forward(inputs):
    centred = inputs - jnp.mean(inputs, axis=-1, keepdims=True)
    scale = lax.rsqrt(jnp.mean(centred * centred, axis=-1, keepdims=True) + norm_eps)
    return centred * scale, scale


def norm_backward(gradient, gain, normal, scale):
    d_normal = gradient * gain
    mean_first = jnp.mean(d_normal, axis=-1, keepdims=True)
    mean_second = jnp.mean(d_normal * normal, axis=-1, keepdims=True)
    return scale * (d_normal - mean_first - normal * mean_second)


def column_sum(inputs):
    return jnp.sum(inputs, axis=0, keepdims=True)


def feed_kernel(pieces, run, scalars, rows, attended, cotangent, vectors, inner_bias, *refs):
    out_weights, inner_weights, outer_weights = (refs[i * pieces : (i + 1) * pieces] for i in range(3))
    refs = refs[3 * pieces :]
    out_content, out_query, d_mid_in, d_branch_out, d_att, small = refs[:6]
    outputs = 4 if pieces == 2 else 2
    grads = refs[6 : 6 + outputs]
    full_out, full_inner, full_outer, act_low, slope = refs[6 + outputs : 11 + outputs]
    if pieces == 2:
        held_outer, held_inner, sems, grad_sems = refs[11 + outputs :]
    else:
        (sems,) = refs[11 + outputs :]
    shard, place = scalars[0], scalars[1]
    copies = [
        weight_copies(out_weights, full_out, sems, 0, shard),
        weight_copies(inner_weights, full_inner, sems, pieces, shard),
        weight_copies(outer_weights, full_outer, sems, 2 * pieces, shard),
    ]
    for group in copies:
        for copy in group:
            copy.start()
    model = rows.shape[1]
    hidden = full_inner.shape[1]
    att_low = attended[...].astype(low)
    for copy in copies[0]:
        copy.wait()
    normal_first, scale_first = norm_forward(mm(att_low, full_out[...]) + rows[...].astype(f32))
    middle = normal_first * vectors[5:6, :] + vectors[6:7, :]
    middle_low = middle.astype(low)
    for copy in copies[1]:
        copy.wait()
    for copy in copies[2]:
        copy.wait()
    wide = model
    total = None
    for start in range(0, hidden, wide):
        at = slice(start, start + wide)
        pre = mm(middle_low, full_inner[:, at]) + inner_bias[:, at]
        squared = pre * pre
        bent = jnp.tanh(0.7978845608028654 * pre * (1.0 + 0.044715 * squared))
        half = 0.5 * (1.0 + bent)
        act = (pre * half).astype(low)
        act_low[:, at] = act
        slope[:, at] = half + (0.5 * 0.7978845608028654) * pre * (1.0 - bent * bent) * (
            1.0 + (3 * 0.044715) * squared
        )
        share = mm(act, full_outer[at, :])
        total = share if total is None else total + share
    normal_second, scale_second = norm_forward(total + vectors[4:5, :] + middle)
    final = (normal_second * vectors[7:8, :] + vectors[8:9, :]).astype(low)
    for micro in range(out_content.shape[0]):
        start = 2 * run * micro
        out_content[micro] = final[start : start + run]
        out_query[micro] = final[start + run : start + 2 * run]
    d_final = cotangent[...].astype(f32)
    small[7:8, :] = column_sum(d_final * normal_second)
    small[8:9, :] = column_sum(d_final)
    d_final_in = norm_backward(d_final, vectors[7:8, :], normal_second, scale_second)
    d_outer = d_final_in.astype(low)
    small[4:5, :] = column_sum(d_outer.astype(f32))
    block = model // 2

    def hold_outer(start, value):
        if pieces == 1:
            grads[0][start : start + block, :] = value.astype(low)
            return
        half = hidden // 2
        target = (start // half) ^ shard
        for down in range(2):
            for across in range(2):
                chunk = ((start % half) // (block // 2) + down) * 2 + across
                held_outer[target, chunk ^ place] = value[
                    down * (block // 2) : (down + 1) * (block // 2), across * block : (across + 1) * block
                ].astype(low)

    def hold_inner(start, value):
        if pieces == 1:
            grads[1][:, start : start + block] = value.astype(low)
            return
        for quarter in range(4):
            chunk = (quarter % 2) * 8 + start // block
            held_inner[(quarter // 2) ^ shard, chunk ^ place] = value[
                quarter * (block // 2) : (quarter + 1) * (block // 2), :
            ].astype(low)

    for start in range(0, hidden, block):
        hold_outer(start, mm_tn(act_low[:, start : start + block], d_outer))
    sent = []
    if pieces == 2:
        sent = [
            pltpu.make_async_copy(held_outer.at[0], grads[0], grad_sems.at[0]),
            pltpu.make_async_copy(held_outer.at[1], grads[1], grad_sems.at[1]),
        ]
        for copy in sent:
            copy.start()
    d_middle = d_final_in
    for start in range(0, hidden, block):
        at = slice(start, start + block)
        d_inner = (mm_nt(d_outer, full_outer[at, :]) * slope[:, at]).astype(low)
        summed = column_sum(d_inner.astype(f32))
        row, lane = start // model, start % model
        small[row : row + 1, lane : lane + block] = summed
        hold_inner(start, mm_tn(middle_low, d_inner))
        d_middle = d_middle + mm_nt(d_inner, full_inner[:, at])
    if pieces == 2:
        late = [
            pltpu.make_async_copy(held_inner.at[0], grads[2], grad_sems.at[2]),
            pltpu.make_async_copy(held_inner.at[1], grads[3], grad_sems.at[3]),
        ]
        for copy in late:
            copy.start()
        sent = sent + late
    small[5:6, :] = column_sum(d_middle * normal_first)
    small[6:7, :] = column_sum(d_middle)
    small[9:16, :] = jnp.zeros((7, model), f32)
    d_mid = norm_backward(d_middle, vectors[5:6, :], normal_first, scale_first)
    d_mid_in[...] = d_mid
    d_branch = d_mid.astype(low)
    d_branch_out[...] = d_branch
    d_att[...] = mm_nt(d_branch, full_out[...]).astype(low)
    for copy in sent:
        copy.wait()


def back_kernel(
    run,
    slots,
    scalars,
    query_low,
    query_segment,
    keys,
    values,
    probs,
    d_att,
    attended,
    vectors,
    d_query,
    d_keys,
    d_values,
    small,
    buckets,
):
    micro = pl.program_id(1)
    base, lo = scalar_at(scalars, slots, micro, 0), scalar_at(scalars, slots, micro, 1)
    span = slots * run
    first, mask_a, mask_b = head_masks()
    gradient = d_att[...]
    stacked = jnp.concatenate([gradient * mask_a, gradient * mask_b], axis=0)
    product = gradient.astype(f32) * attended[...]
    delta_a = jnp.sum(jnp.where(first, product, 0.0), axis=-1, keepdims=True)
    delta_b = jnp.sum(jnp.where(first, 0.0, product), axis=-1, keepdims=True)
    delta_row = jnp.concatenate([delta_a, delta_b], axis=0)
    probs_low = probs[0]
    d_probs = mm_nt(stacked, values[...])
    d_scores = (probs_low.astype(f32) * (d_probs - delta_row)).astype(low)
    left = stack_query(query_low[...], query_segment[...], mask_a, mask_b)
    right = stack_keys(keys[...], vectors[...], lo)
    d_left = mm(d_scores, right) * 0.125
    mine = jnp.concatenate([first, first], axis=1)
    d_left = jnp.where(mine, d_left[: 2 * run], d_left[2 * run :])
    d_content, d_segment = d_left[:, :128], d_left[:, 128:]
    d_query[...] = (d_content + d_segment).astype(low)
    d_right = mm_tn(d_scores, left) * 0.125
    d_keys[...] = d_right[:, :128].astype(low)
    d_values[...] = mm_tn(probs_low, stacked).astype(low)
    row = lax.broadcasted_iota(jnp.int32, (span, 1), 0)
    d_embed = d_right[:, 128:]
    shares = jnp.concatenate(
        [
            column_sum(d_content),
            column_sum(d_segment),
            column_sum(jnp.where(row >= lo, 0.0, d_embed)),
            column_sum(jnp.where(row >= lo, d_embed, 0.0)),
            jnp.zeros((4, 128), f32),
        ],
        axis=0,
    )
    delta, _ = offsets_of(base, run, span)
    exact = d_scores.astype(f32)
    tallies = []
    for head in range(2):
        at = 2 * run * head
        both = exact[at : at + run] + exact[at + run : at + 2 * run]
        rows = [None] * 16
        rows[0] = column_sum(jnp.where(delta == 0, both, 0.0))
        for step, threshold in enumerate(thresholds):
            if threshold < span:
                later = thresholds[step + 1] if step + 1 < len(thresholds) else span
                above = (delta >= threshold) & (delta < later)
                below = (delta <= -threshold) & (delta > -later)
                rows[1 + step] = column_sum(jnp.where(above, both, 0.0))
                rows[9 + step] = column_sum(jnp.where(below, both, 0.0))
        blank = jnp.zeros((1, span), f32)
        tallies.append(jnp.concatenate([blank if entry is None else entry for entry in rows], axis=0))

    @pl.when(micro == 0)
    def _():
        small[...] = shares
        for head in range(2):
            buckets[head] = tallies[head]

    @pl.when(micro != 0)
    def _():
        small[...] += shares
        for head in range(2):
            buckets[head] += tallies[head]


def weights_kernel(pieces, columns, run, slots, scalars, rows, path, attended, d_branch, d_query, d_keys, d_values, d_mid_in, *refs):
    weights = [refs[i * pieces : (i + 1) * pieces] for i in range(3)]
    refs = refs[3 * pieces :]
    d_content, d_state = refs[:2]
    parts = refs[2 : 2 + len(columns)]
    refs = refs[2 + len(columns) :]
    if pieces == 2:
        kept, sent, full, held, sems, grad_sems = refs
    else:
        natural, full, sems = refs[:4], refs[4], refs[5]
    shard, place = scalars[0], scalars[1]
    copies = [weight_copies(weights[i], full.at[i], sems, i * pieces, shard) for i in range(3)]
    for group in copies:
        for copy in group:
            copy.start()
    model = rows.shape[1]
    block = model // 2
    small_rows = block // 8

    def hold(which, value):
        if pieces == 1:
            natural[which][...] = value.astype(low)
            return
        for half in range(2):
            for down in range(8):
                for across in range(2):
                    start = half * block + down * small_rows
                    held[half ^ shard, (down * 2 + across) ^ place, which * small_rows : (which + 1) * small_rows, :] = value[
                        start : start + small_rows, across * block : (across + 1) * block
                    ].astype(low)

    hold(0, mm_tn(rows[...], d_query[...]))
    hold(1, mm_tn(path[...], d_keys[...]))
    hold(2, mm_tn(path[...], d_values[...]))
    hold(3, mm_tn(attended[...].astype(low), d_branch[...]))
    leaving = []
    if pieces == 2:
        leaving = [
            pltpu.make_async_copy(held.at[0], kept, grad_sems.at[0]),
            pltpu.make_async_copy(held.at[1], sent, grad_sems.at[1]),
        ]
        for copy in leaving:
            copy.start()
    for group in copies:
        for copy in group:
            copy.wait()
    for part in parts:
        part[...] = jnp.zeros(part.shape, part.dtype)
    span = slots * run
    for micro in range(rows.shape[0] // (2 * run)):
        at = slice(micro * span, (micro + 1) * span)
        shares = mm_nt(d_keys[at, :], full[1]) + mm_nt(d_values[at, :], full[2])
        for slot in range(slots):
            relative = scalar_at(scalars, slots, micro, 3 + slot)
            for part, (start, width) in enumerate(columns):
                piece = shares[slot * run : (slot + 1) * run, start : start + width]
                spot = (relative, slice(micro * run, (micro + 1) * run), slice(None))
                parts[part][spot] = (parts[part][spot].astype(f32) + piece).astype(low)
    d_both = d_mid_in[...] + mm_nt(d_query[...], full[0])
    for micro in range(rows.shape[0] // (2 * run)):
        start = 2 * run * micro
        d_content[micro] = d_both[start : start + run]
        d_state[micro] = d_both[start + run : start + 2 * run]
    for copy in leaving:
        copy.wait()


def spread_kernel(layout, scalars, *refs):
    source, targets = refs[0], refs[1:]
    for which, target in enumerate(targets):
        rows = target.shape[0]
        target[...] = source[0, which * rows : (which + 1) * rows, :].astype(f32)


def send(inputs, mask):
    return lax.ppermute(inputs, "dp", [(i, i ^ mask) for i in range(lax.axis_size("dp"))])


def bits_of(order):
    named = {"x": (0,), "y": (1,), "z": (2, 3)}
    total = lax.axis_size("dp").bit_length() - 1
    return [named[axis] for axis in order] + [(bit,) for bit in range(4, total)], total


def gather_blocks(block, order):
    stages, total = bits_of(order)
    held = block.reshape((1,) * total + block.shape)
    for bits in stages:
        if len(bits) == 2:
            near, far, both = send(held, 4), send(held, 8), send(held, 12)
            at = total - 1 - bits[0]
            held = jnp.concatenate(
                [jnp.concatenate([held, near], axis=at), jnp.concatenate([far, both], axis=at)], axis=at - 1
            )
        else:
            held = jnp.concatenate([held, send(held, 1 << bits[0])], axis=total - 1 - bits[0])
    return held.reshape((1 << total,) + block.shape)


def scatter_blocks(blocks, order):
    stages, total = bits_of(order[::-1])
    held = blocks.reshape((2,) * total + blocks.shape[1:])

    def part(inputs, bit, which):
        return lax.slice_in_dim(inputs, which, which + 1, axis=total - 1 - bit)

    for bits in stages[::-1]:
        if len(bits) == 2:
            lower, upper = part(held, 3, 0), part(held, 3, 1)
            near, far, both = send(part(lower, 2, 1), 4), send(part(upper, 2, 0), 8), send(part(upper, 2, 1), 12)
            held = (part(lower, 2, 0).astype(f32) + near + far + both).astype(low)
        else:
            held = part(held, bits[0], 0) + send(part(held, bits[0], 1), 1 << bits[0])
    return held.reshape(blocks.shape[1:])


def all_sum(blocks):
    rows = blocks.shape[1]
    cuts = (0, rows // 2, rows * 3 // 4, rows)
    orders = ("yxz", "zxy", "xzy")
    pieces = []
    for part, order in enumerate(orders):
        share = scatter_blocks(blocks[:, cuts[part] : cuts[part + 1]], order)
        pieces.append(gather_blocks(share, order[::-1]))
    return jnp.concatenate(pieces, axis=1)


def shards(
    content,
    query_state,
    token_seg,
    positions,
    parent,
    w_query,
    w_key,
    w_value,
    w_out,
    w_inner,
    w_outer,
    b_inner,
    b_outer,
    gain_attn,
    bias_attn,
    gain_ffn,
    bias_ffn,
    bias_content,
    bias_segment,
    seg_embed,
    rel_table,
    cot_content,
    cot_query,
):
    micro_count, run, model = content.shape
    shard_count, dp_count = lax.axis_size("shard"), lax.axis_size("dp")
    shard, place = lax.axis_index("shard"), lax.axis_index("dp")
    heads = rel_table.shape[1]
    bucket_total = rel_table.shape[0] * shard_count
    hidden = w_inner.shape[1]
    pairs = heads // 2
    per_run = dp_count // tree_runs
    slots = path_runs * per_run
    span = slots * run
    rows_total = 2 * run * micro_count
    pieces = 2 if shard_count == 2 and dp_count == tree_runs else 1
    part_width = model // shard_count

    def fetch(weight):
        if pieces == 2:
            return [weight, lax.ppermute(weight, "shard", [(0, 1), (1, 0)])]
        return [lax.all_gather(weight, "shard", axis=0, tiled=True)]

    own_seg = token_seg[:, 0]
    own_slot = positions[:, 0] // run
    facts = jnp.stack([own_seg, own_slot], axis=1).reshape(2 * micro_count).astype(low)
    columns = ((0, model // 2), (model // 2, model // 6), (model // 2 + model // 6, model // 3))
    orders = ("zxy", "xyz", "yzx")
    flat_content = content.reshape(micro_count * run, model)
    fact_rows = jnp.broadcast_to(
        jnp.pad(facts, (0, 16 - 2 * micro_count))[:, None], (16, columns[1][1])
    )
    tree_parts = []
    for part, (start, width) in enumerate(columns):
        block = flat_content[:, start : start + width]
        if part == 1:
            block = jnp.concatenate([block, fact_rows], axis=0)
        tree_parts.append(gather_blocks(block, orders[part]))

    small_parts = jnp.concatenate(
        [
            b_inner.reshape(-1, part_width),
            jnp.stack([b_outer, gain_attn, bias_attn, gain_ffn, bias_ffn, bias_content, bias_segment]),
            seg_embed,
            jnp.pad(rel_table.reshape(1, -1), ((0, 0), (0, part_width - rel_table.size))),
        ],
        axis=0,
    )
    inner_rows = b_inner.shape[0] // part_width
    fill = 16 - small_parts.shape[0]
    small_parts = jnp.pad(small_parts, ((0, fill), (0, 0)))
    if pieces == 2:
        other = lax.ppermute(small_parts, "shard", [(0, 1), (1, 0)])
        gathered = jnp.where(shard == 0, jnp.stack([small_parts, other]), jnp.stack([other, small_parts]))
    else:
        gathered = lax.all_gather(small_parts, "shard", axis=0, tiled=False)
    gathered = gathered.astype(f32)
    inner_bias = gathered[:, :inner_rows].reshape(1, hidden)
    vectors = jnp.transpose(gathered, (1, 0, 2)).reshape(16, model)
    table = gathered[:, 13, : rel_table.size].reshape(bucket_total, heads)

    query_weights, key_weights, value_weights = fetch(w_query), fetch(w_key), fetch(w_value)
    out_weights, inner_weights, outer_weights = fetch(w_out), fetch(w_inner), fetch(w_outer)

    every = jnp.transpose(
        tree_parts[1][:, micro_count * run : micro_count * run + 2 * micro_count, 0].astype(jnp.int32)
    ).reshape(micro_count, 2, dp_count)
    blocks = jnp.arange(dp_count, dtype=jnp.int32)
    entries = [shard, place]
    for micro in range(micro_count):
        segs, slots_of = every[micro, 0], every[micro, 1]
        mine = own_seg[micro]
        above = jnp.sum(jnp.where(jnp.arange(parent.shape[2]) == mine, parent[micro, 0], 0))
        trunk = mine == 0
        leaf = mine > 4
        branch = jnp.where(leaf, above, mine)
        base = own_slot[micro] * run
        first_branch, first_leaf = trunk_runs * per_run, (trunk_runs + 1) * per_run
        lo = jnp.where(trunk, 0, jnp.where(leaf, first_leaf, first_branch)) * run
        hi = jnp.where(trunk, first_branch, jnp.where(leaf, slots, first_leaf)) * run
        entries += [base, lo, hi]
        for slot in range(slots):
            wanted = 0 if slot < first_branch else branch if slot < first_leaf else mine
            shown = (segs == wanted) & (slots_of == slot)
            entries.append(jnp.sum(jnp.where(shown, blocks, 0)))
    scalars = jnp.stack([jnp.asarray(entry, jnp.int32) for entry in entries])
    early = jnp.stack([jnp.asarray(entry, jnp.int32) for entry in entries[:2]])

    rows = jnp.concatenate([content, query_state], axis=1).reshape(rows_total, model)
    cotangent = jnp.concatenate([cot_content, cot_query], axis=1).reshape(rows_total, model)
    grown = pltpu.CompilerParams(vmem_limit_bytes=vmem_bytes)

    def shape(dims, kind):
        return jax.ShapeDtypeStruct(dims, kind)

    dma = pltpu.SemaphoreType.DMA
    query_low, query_segment = pl.pallas_call(
        functools.partial(query_kernel, pieces),
        out_shape=(shape((rows_total, model), low),) * 2,
        in_specs=[smem_space, vmem_space, vmem_space] + [any_space] * pieces,
        out_specs=(vmem_space,) * 2,
        scratch_shapes=[pltpu.VMEM((model, model), low), dma((pieces,))],
        compiler_params=grown,
        name="query_projection",
    )(early, rows, vectors, *query_weights)

    path, keys, values = pl.pallas_call(
        functools.partial(keys_kernel, pieces, columns, run, slots),
        out_shape=(
            shape((micro_count, span, model), low),
            shape((micro_count * span, model), low),
            shape((micro_count * span, model), low),
        ),
        in_specs=[smem_space] + [any_space] * (len(columns) + 2 * pieces),
        out_specs=(vmem_space,) * 3,
        scratch_shapes=[
            pltpu.VMEM((model, model), low),
            pltpu.VMEM((model, model), low),
            dma((2 * pieces,)),
            dma((micro_count * slots * len(columns),)),
        ],
        compiler_params=grown,
        name="path_keys",
    )(scalars, *tree_parts, *key_weights, *value_weights)
    path = path.reshape(micro_count * span, model)

    row_block = pl.BlockSpec((2 * run, 128), lambda pair, micro: (micro, pair))
    key_block = pl.BlockSpec((span, 128), lambda pair, micro: (micro, pair))
    vector_block = pl.BlockSpec((16, 128), lambda pair, micro: (0, pair))
    prob_block = pl.BlockSpec((1, 4 * run, span), lambda pair, micro: (pair * micro_count + micro, 0, 0))
    probs, attended = pl.pallas_call(
        functools.partial(attend_kernel, run, slots),
        grid=(pairs, micro_count),
        out_shape=(
            shape((pairs * micro_count, 4 * run, span), low),
            shape((rows_total, model), f32),
        ),
        in_specs=[smem_space, smem_space, row_block, row_block, key_block, key_block, vector_block],
        out_specs=(prob_block, row_block),
        compiler_params=grown,
        name="attend",
    )(scalars, table, query_low, query_segment, keys, values, vectors)

    chunk = (dp_count, hidden // (8 * shard_count), model // 2)
    if pieces == 2:
        grad_shapes = [shape(chunk, low)] * 4
        grad_specs = [any_space] * 4
        grad_scratch = [pltpu.VMEM((2,) + chunk, low)] * 2
    else:
        grad_shapes = [shape((hidden, model), low), shape((model, hidden), low)]
        grad_specs = [vmem_space] * 2
        grad_scratch = []
    results = pl.pallas_call(
        functools.partial(feed_kernel, pieces, run),
        out_shape=[
            shape((micro_count, run, model), low),
            shape((micro_count, run, model), low),
            shape((rows_total, model), f32),
            shape((rows_total, model), low),
            shape((rows_total, model), low),
            shape((16, model), f32),
        ]
        + grad_shapes,
        in_specs=[smem_space] + [vmem_space] * 5 + [any_space] * (3 * pieces),
        out_specs=[vmem_space] * 6 + grad_specs,
        scratch_shapes=[
            pltpu.VMEM((model, model), low),
            pltpu.VMEM((model, hidden), low),
            pltpu.VMEM((hidden, model), low),
            pltpu.VMEM((rows_total, hidden), low),
            pltpu.VMEM((rows_total, hidden), f32),
        ]
        + grad_scratch
        + [dma((3 * pieces,))]
        + ([dma((4,))] if pieces == 2 else []),
        compiler_params=grown,
        name="feed_forward",
    )(scalars, rows, attended, cotangent, vectors, inner_bias, *out_weights, *inner_weights, *outer_weights)
    out_content, out_query, d_mid_in, d_branch, d_att, small_first = results[:6]

    d_query, d_keys, d_values, small_second, tallies = pl.pallas_call(
        functools.partial(back_kernel, run, slots),
        grid=(pairs, micro_count),
        out_shape=(
            shape((rows_total, model), low),
            shape((micro_count * span, model), low),
            shape((micro_count * span, model), low),
            shape((8, model), f32),
            shape((heads, 16, span), f32),
        ),
        in_specs=[smem_space, row_block, row_block, key_block, key_block, prob_block, row_block, row_block, vector_block],
        out_specs=(
            row_block,
            key_block,
            key_block,
            pl.BlockSpec((8, 128), lambda pair, micro: (0, pair)),
            pl.BlockSpec((2, 16, span), lambda pair, micro: (pair, 0, 0)),
        ),
        compiler_params=grown,
        name="attend_back",
    )(scalars, query_low, query_segment, keys, values, probs, d_att, attended, vectors)

    if pieces == 2:
        grad_shapes = [shape(chunk, low)] * 2
        grad_specs = [any_space] * 2
    else:
        grad_shapes = [shape((model, model), low)] * 4
        grad_specs = [vmem_space] * 4
    later = pl.pallas_call(
        functools.partial(weights_kernel, pieces, columns, run, slots),
        out_shape=[shape((micro_count, run, model), f32)] * 2
        + [shape((dp_count, micro_count * run, width), low) for _, width in columns]
        + grad_shapes,
        in_specs=[smem_space] + [vmem_space] * 8 + [any_space] * (3 * pieces),
        out_specs=[vmem_space] * (2 + len(columns)) + grad_specs,
        scratch_shapes=[pltpu.VMEM((3, model, model), low)]
        + ([pltpu.VMEM((2,) + chunk, low)] if pieces == 2 else [])
        + [dma((3 * pieces,))]
        + ([dma((2,))] if pieces == 2 else []),
        compiler_params=grown,
        name="weight_gradients",
    )(scalars, rows, path, attended, d_branch, d_query, d_keys, d_values, d_mid_in, *query_weights, *key_weights, *value_weights)
    d_content, grad_query = later[:2]
    tree_grads = later[2 : 2 + len(columns)]
    later = later[2 + len(columns) :]

    arrived = [scatter_blocks(part, order[::-1]) for part, order in zip(tree_grads, orders)]
    grad_content = d_content + jnp.concatenate(arrived, axis=1).astype(f32).reshape(content.shape)

    def spread(blocks_in, shapes, dims, place_of):
        return pl.pallas_call(
            functools.partial(spread_kernel, None),
            grid_spec=pltpu.PrefetchScalarGridSpec(
                num_scalar_prefetch=1,
                grid=(dp_count,),
                in_specs=[pl.BlockSpec((1,) + blocks_in.shape[1:], lambda i, s: (i ^ s[1], 0, 0))],
                out_specs=[pl.BlockSpec(dims, place_of)] * len(shapes),
            ),
            out_shape=[shape(entry, f32) for entry in shapes],
            compiler_params=grown,
            name="spread",
        )(early, blocks_in)

    half = model // 2
    if pieces == 2:
        swap = [(0, 1), (1, 0)]
        outer_sum = all_sum(results[6] + lax.ppermute(results[7], "shard", swap))
        inner_sum = all_sum(results[8] + lax.ppermute(results[9], "shard", swap))
        later_sum = all_sum(later[0] + lax.ppermute(later[1], "shard", swap))
        (grad_w_outer,) = spread(outer_sum, [w_outer.shape], (chunk[1], half), lambda i, s: (i // 2, i % 2))
        (grad_w_inner,) = spread(inner_sum, [w_inner.shape], (chunk[1], half), lambda i, s: (i // 8, i % 8))
        grad_w_query, grad_w_key, grad_w_value, grad_w_out = spread(
            later_sum, [w_query.shape] * 4, (half // 8, half), lambda i, s: (i // 2, i % 2)
        )
    else:
        totals = []
        for entry in (*results[6:8], *later):
            share = lax.psum_scatter(entry, "shard", scatter_dimension=0, tiled=True)
            totals.append(lax.psum(share, "dp").astype(f32))
        grad_w_outer, grad_w_inner, grad_w_query, grad_w_key, grad_w_value, grad_w_out = totals

    bucket_grads = jnp.transpose(jnp.sum(tallies, axis=-1)).reshape(1, -1)
    small = jnp.concatenate(
        [
            small_first[:9],
            small_second[:4],
            jnp.pad(bucket_grads, ((0, 0), (0, model - bucket_grads.shape[1]))),
        ],
        axis=0,
    )
    small = lax.psum(small, ("shard", "dp"))
    grad_b_inner = lax.dynamic_slice_in_dim(small[:4].reshape(-1), shard * b_inner.shape[0], b_inner.shape[0])
    narrow = lax.dynamic_slice_in_dim(small[4:13], shard * part_width, part_width, axis=1)
    grad_rel_table = lax.dynamic_slice_in_dim(
        small[13, : bucket_total * heads].reshape(bucket_total, heads),
        shard * rel_table.shape[0],
        rel_table.shape[0],
        axis=0,
    )
    return (
        out_content,
        out_query,
        grad_content,
        grad_query,
        grad_w_query,
        grad_w_key,
        grad_w_value,
        grad_w_out,
        grad_w_inner,
        grad_w_outer,
        grad_b_inner,
        narrow[0],
        narrow[1],
        narrow[2],
        narrow[3],
        narrow[4],
        narrow[5],
        narrow[6],
        narrow[7:9],
        grad_rel_table,
    )


def solution(mesh):
    rows = P(None, ("shard", "dp"), None)
    tokens = P(None, ("shard", "dp"))
    matrix = P("shard", None)
    vector = P("shard")
    return jax.shard_map(
        shards,
        mesh=mesh,
        in_specs=(rows, rows, tokens, tokens, P(None, "shard", None))
        + (matrix,) * 6
        + (vector,) * 8
        + (P(None, "shard"), matrix, rows, rows),
        out_specs=(rows,) * 4 + (matrix,) * 6 + (vector,) * 8 + (P(None, "shard"), matrix),
        check_vma=False,
    )
```

time: 1140 us -> 547 us (0.48)
  waiting for transfers between devices: 477 us -> 157 us
  matrix products: 165 us -> 0 us
  starting transfers between devices: 2.01 us -> 150 us
  local copies, waits for them, and re-layouts: 178 us -> 37.2 us
  blocking collectives: 180 us -> 45.9 us
  Pallas kernels: 0 us -> 103 us
  other arithmetic: 109 us -> 36.7 us
    reduce_scatter x10 -> x0, waiting for transfers between devices: 257 us -> none  [the longest x2 185 us: shards(): lax.psum_scatter(key_grads.reshape(tree_tokens, 2 * model_width).astype(j...]
    dot_general x86 -> x0, matrix products: 165 us -> none  [the longest x12 33.7 us: scores_of(): jnp.einsum('nar,nf->far', indicator_rows, reduced_table, preferred_elemen...]
    ppermute x0 -> x130, waiting for transfers between devices: none -> 157 us  [the longest x120 157 us: send(): lax.ppermute(inputs, 'dp', [(i, i ^ mask) for i in range(lax.axis_size('d...]
    ppermute x0 -> x130, starting transfers between devices: none -> 150 us  [the longest x120 149 us: send(): lax.ppermute(inputs, 'dp', [(i, i ^ mask) for i in range(lax.axis_size('d...]
    psum x1 -> x0, waiting for transfers between devices: 149 us -> none  [shards(): lax.psum(owned_shares[1].astype(jnp.bfloat16), 'dp').astype(jnp.float32)]
    pallas_call x0 -> x9, Pallas kernels: none -> 103 us  [the longest x3 31.8 us: spread(): pl.pallas_call(functools.partial(spread_kernel, None), grid_spec=pltpu.Pr...]
    unnamed x2 -> x0, blocking collectives: 81.4 us -> none
    unnamed x31 -> x0, waiting for transfers between devices: 49.6 us -> none
  transfers between devices with their start and end apart: 25 -> 130, of which waited for: 16 -> 55; matrix products, arithmetic and copies ran while one was open for 23% -> 11% of each run, Pallas kernels for 0% -> 8%
where the time goes in v1:
time: 547 us; the launch traced here: 539 us
  waiting for transfers between devices  157 us (29%)
  starting transfers between devices  150 us (27%)
  Pallas kernels  103 us (19%)
  blocking collectives  45.9 us (8%)
  local copies, waits for them, and re-layouts  37.2 us (7%)
  other arithmetic  36.7 us (7%)
  between operations  9.09 us (2%)
    ppermute x120, waiting for transfers between devices, send(): lax.ppermute(inputs, 'dp', [(i, i ^ mask) for i in range(lax.axis_size('d...  157 us
    ppermute x120, starting transfers between devices, send(): lax.ppermute(inputs, 'dp', [(i, i ^ mask) for i in range(lax.axis_size('d...  149 us
    psum x1, blocking collectives, shards(): small = lax.psum(small, ('shard', 'dp'))  45.9 us
    pallas_call x3, Pallas kernels, spread(): pl.pallas_call(functools.partial(spread_kernel, None), grid_spec=pltpu.Pr...  31.8 us
    pallas_call x1, Pallas kernels, shards(): pl.pallas_call(functools.partial(feed_kernel, pieces, run), out_shape=[sh...  21.1 us
    pallas_call x1, Pallas kernels, shards(): pl.pallas_call(functools.partial(back_kernel, run, slots), grid=(pairs, m...  14.4 us
    pallas_call x1, Pallas kernels, shards(): pl.pallas_call(functools.partial(weights_kernel, pieces, columns, run, sl...  13.7 us
    pallas_call x1, Pallas kernels, shards(): pl.pallas_call(functools.partial(attend_kernel, run, slots), grid=(pairs,...  11.7 us
  transfers between devices with their start and end apart: 130, of which 55 were waited for; matrix products, arithmetic and copies ran while one was open for 11% of the time, Pallas kernels for 8%

profile of v1, /device:TPU:0, one launch (start us, length us, event | category | flops | bytes accessed | tf_op | source)
XLA Modules:
  0.0 539.0 jit_solution(9333025430754020913)
XLA Ops:
  41.3 10.5 %collective-permute-done.14 = bf16[1,1,2,1,128,256]{5,4,3,2,1,0:T(8,128)(2,1)S(1)} collective-permute-done((bf16[1,1,2,1,128,256]{5,4,3,2,1,0:T(8,128)(2,1)S(1)}, bf16[1,1,2,1,128,256]{5,4,3,2,1,0:T(8,128)(2,1)S(1)}, u32[]{:S(2)}, u32[]{:S(2)}) %collective-permute-start.14) | collective-permute-done | bytes 131104 | tf_op jit(solution)/shard_map/ppermute | solution.py:453
  78.9 8.2 %stack.123.scalars = s32[20]{0:T(128)} concatenate(s32[1]{0:T(128)} %bitcast, s32[1]{0:T(128)} %bitcast.1, s32[1]{0:T(128)S(6)} %mul.29, s32[1]{0:T(128)} %bitcast.3, s32[1]{0:T(128)} %bitcast.4, s32[1]{0:T(128)} %bitcast.14, s32[1]{0:T(128)} %bitcast.16, s32[1]{0:T(128)} %bitcast.18, s32[1]{0:T(128)} %bitcast.20, s32[1]{0:T(128)} %bitcast.23, s32[1]{0:T(128)} %bitcast.25, ...), dimensions={0} | concatenate | bytes 160 | tf_op jit(solution)/shard_map/stack | solution.py:611
  96.7 6.2 %path_keys.1 = (bf16[2,384,768]{2,1,0:T(8,128)(2,1)}, bf16[768,768]{1,0:T(8,128)(2,1)}, bf16[768,768]{1,0:T(8,128)(2,1)}) custom-call(s32[20]{0:T(128)} %stack.123.scalars, bf16[16,128,384]{2,1,0:T(8,128)(2,1)} %bitcast.131, bf16[16,144,128]{2,1,0:T(8,128)(2,1)} %bitcast.143, bf16[16,128,256]{2,1,0:T(8,128)(2,1)} %bitcast.141, bf16[384,768]{1,0:T(8,128)(2,1)} %refs_2_.3, ...), custom_call_target="tpu_custom_call" | custom-call | tf_op jit(solution)/shard_map/path_keys/pallas_call | solution.py:632
  102.9 11.7 %attend.1 = (bf16[12,256,384]{2,1,0:T(8,128)(2,1)}, f32[256,768]{1,0:T(8,128)}) custom-call(s32[20]{0:T(128)} %stack.123.scalars, f32[16,12]{1,0:T(8,128)} %reshape_squeeze.6.table, bf16[256,768]{1,0:T(8,128)(2,1)} %get-tuple-element.53.query_low, bf16[256,768]{1,0:T(8,128)(2,1)} %get-tuple-element.54.query_segment, ...), custom_call_target="tpu_custom_call" | custom-call | tf_op jit(solution)/shard_map/attend/pallas_call | solution.py:656
  114.6 21.1 %feed_forward.1 = (bf16[2,64,768]{2,1,0:T(8,128)(2,1)}, bf16[2,64,768]{2,1,0:T(8,128)(2,1)}, f32[256,768]{1,0:T(8,128)}, bf16[256,768]{1,0:T(8,128)(2,1)}, bf16[...) custom-call(s32[20]{0:T(128)} %stack.123.scalars, ...), custom_call_target="tpu_custom_call" | custom-call | tf_op jit(solution)/shard_map/feed_forward/pallas_call | solution.py:678
  135.7 14.4 %attend_back.1 = (bf16[256,768]{1,0:T(8,128)(2,1)}, bf16[768,768]{1,0:T(8,128)(2,1)}, bf16[768,768]{1,0:T(8,128)(2,1)}, f32[8,768]{1,0:T(8,128)}, f32[12,16,384]{2,1,0:T(8,128)}) custom-call(s32[20]{0:T(128)} %stack.123.scalars, bf16[256,768]{1,0:T(8,128)(2,1)} %get-tuple-element.53.query_low, bf16[256,768]{1,0:T(8,128)(2,1)} %get-tuple-element.54.query_segment, ...), custom_call_target="tpu_custom_call" | custom-call | tf_op jit(solution)/shard_map/attend_back/pallas_call | solution.py:706
  152.1 13.7 %weight_gradients.1 = (f32[2,64,768]{2,1,0:T(8,128)}, f32[2,64,768]{2,1,0:T(8,128)}, bf16[16,128,384]{2,1,0:T(8,128)(2,1)}, bf16[16,128,128]{2,1,0:T(8,128)(2,1)...) custom-call(s32[20]{0:T(128)} %stack.123.scalars, ...), custom_call_target="tpu_custom_call" | custom-call | tf_op jit(solution)/shard_map/weight_gradients/pallas_call | solution.py:734
  175.0 45.9 %psum.7 = f32[14,768]{1,0:T(8,128)S(1)} all-reduce(f32[14,768]{1,0:T(8,128)S(1)} %select_maximum_fusion), channel_id=1, replica_groups=mesh['shard'=2,'dp'=16] {'shard','dp'}, use_global_device_ids=true, to_apply=%region_15.16 | all-reduce | flops 10752 | bytes 86016 | tf_op jit(solution)/shard_map/psum | solution.py:796
  230.5 11.0 %collective-permute-done.22 = bf16[2,2,1,2,128,384]{5,4,3,2,1,0:T(8,128)(2,1)} collective-permute-done((bf16[2,2,1,2,128,384]{5,4,3,2,1,0:T(8,128)(2,1)}, bf16[2,2,1,2,128,384]{5,4,3,2,1,0:T(8,128)(2,1)}, u32[]{:S(2)}, u32[]{:S(2)}) %collective-permute-start.22) | collective-permute-done | bytes 786464 | tf_op jit(solution)/shard_map/ppermute | solution.py:453
  254.4 4.2 collective-permute-done.23
  268.9 4.3 collective-permute-done.26
  285.8 8.4 %collective-permute-done.111 = bf16[1,1,2,2,48,384]{5,4,3,2,1,0:T(8,128)(2,1)S(1)} collective-permute-done((bf16[1,1,2,2,48,384]{5,4,3,2,1,0:T(8,128)(2,1)S(1)}, bf16[1,1,2,2,48,384]{5,4,3,2,1,0:T(8,128)(2,1)S(1)}, u32[]{:S(2)}, u32[]{:S(2)}) %collective-permute-start.111) | collective-permute-done | bytes 147488 | tf_op jit(solution)/shard_map/ppermute | solution.py:453
  296.1 6.5 %collective-permute-start.79 = (bf16[1,1,2,2,48,384]{5,4,3,2,1,0:T(8,128)(2,1)S(1)}, bf16[1,1,2,2,48,384]{5,4,3,2,1,0:T(8,128)(2,1)S(1)}, u32[]{:S(2)}, u32[]{:S(2)}) collective-permute-start(bf16[1,1,2,2,48,384]{5,4,3,2,1,0:T(8,128)(2,1)S(1)} %slice.731), channel_id=1, source_target_pairs={{0,4},{1,5},{2,6},{3,7},{4,0},{5,1},{6,2},{7,3},{8,12},{9,13},{10,... | collective-permute-start | bytes 442376 | tf_op jit(solution)/shard_map/ppermute | solution.py:453
  316.3 4.9 collective-permute-done.113
  348.4 4.7 collective-permute-done.91
  395.5 8.0 %collective-permute-done.87 = bf16[1,1,2,2,48,384]{5,4,3,2,1,0:T(8,128)(2,1)S(1)} collective-permute-done((bf16[1,1,2,2,48,384]{5,4,3,2,1,0:T(8,128)(2,1)S(1)}, bf16[1,1,2,2,48,384]{5,4,3,2,1,0:T(8,128)(2,1)S(1)}, u32[]{:S(2)}, u32[]{:S(2)}) %collective-permute-start.87) | collective-permute-done | bytes 147488 | tf_op jit(solution)/shard_map/ppermute | solution.py:453
  416.4 4.8 collective-permute-done.96
  424.1 4.5 collective-permute-done.65
  435.4 8.3 %collective-permute-done.101 = bf16[2,2,1,1,96,384]{5,4,3,2,1,0:T(8,128)(2,1)S(1)} collective-permute-done((bf16[2,2,1,1,96,384]{5,4,3,2,1,0:T(8,128)(2,1)S(1)}, bf16[2,2,1,1,96,384]{5,4,3,2,1,0:T(8,128)(2,1)S(1)}, u32[]{:S(2)}, u32[]{:S(2)}) %collective-permute-start.101) | collective-permute-done | bytes 294944 | tf_op jit(solution)/shard_map/ppermute | solution.py:453
  445.5 4.5 collective-permute-done.70
  451.2 5.1 collective-permute-done.39
  500.7 10.6 %spread.5 = f32[1536,768]{1,0:T(8,128)} custom-call(s32[2]{0:T(128)} %pad_add_fusion.scalars, bf16[16,192,384]{2,1,0:T(8,128)(2,1)} %pad_maximum_fusion.2.refs_0_), custom_call_target="tpu_custom_call" | custom-call | tf_op jit(solution)/shard_map/spread/pallas_call | solution.py:756
  514.3 10.6 %spread.4 = f32[384,3072]{1,0:T(8,128)} custom-call(s32[2]{0:T(128)} %pad_add_fusion.scalars, bf16[16,192,384]{2,1,0:T(8,128)(2,1)} %pad_maximum_fusion.1.refs_0_), custom_call_target="tpu_custom_call" | custom-call | tf_op jit(solution)/shard_map/spread/pallas_call | solution.py:756
  527.9 10.6 %spread.3 = (f32[384,768]{1,0:T(8,128)}, f32[384,768]{1,0:T(8,128)}, f32[384,768]{1,0:T(8,128)}, f32[384,768]{1,0:T(8,128)}) custom-call(s32[2]{0:T(128)} %pad_add_fusion.scalars, bf16[16,192,384]{2,1,0:T(8,128)(2,1)} %pad_maximum_fusion.refs_0_), custom_call_target="tpu_custom_call" | custom-call | tf_op jit(solution)/shard_map/spread/pallas_call | solution.py:756
  (499 shorter events, 287.1 us)
Async XLA Ops:
  7.3 107.3 %collective-permute-start.20 = (bf16[384,3072]{1,0:T(8,128)(2,1)}, bf16[384,3072]{1,0:T(8,128)(2,1)}, u32[]{:S(2)}, u32[]{:S(2)}) collective-permute-start(bf16[384,3072]{1,0:T(8,128)(2,1)} %refs_2_.2), channel_id=1, source_target_pairs={{0,16},{16,0},{1,17},{17,1},{2,18},{18,2},{3,19},{19,3},{4,20},{20... | collective-permute-start | bytes 7077896 | tf_op jit(solution)/shard_map/ppermute | solution.py:546
  7.3 107.4 %collective-permute-start.21 = (bf16[1536,768]{1,0:T(8,128)(2,1)}, bf16[1536,768]{1,0:T(8,128)(2,1)}, u32[]{:S(2)}, u32[]{:S(2)}) collective-permute-start(bf16[1536,768]{1,0:T(8,128)(2,1)} %refs_4_.2), channel_id=1, source_target_pairs={{0,16},{16,0},{1,17},{17,1},{2,18},{18,2},{3,19},{19,3},{4,20},{20... | collective-permute-start | bytes 7077896 | tf_op jit(solution)/shard_map/ppermute | solution.py:546
  73.3 22.3 %collective-permute-start.17 = (bf16[384,768]{1,0:T(8,128)(2,1)S(1)}, bf16[384,768]{1,0:T(8,128)(2,1)S(1)}, u32[]{:S(2)}, u32[]{:S(2)}) collective-permute-start(bf16[384,768]{1,0:T(8,128)(2,1)S(1)} %copy-done.6), channel_id=1, source_target_pairs={{0,16},{16,0},{1,17},{17,1},{2,18},{18,2},{3,19},{19,3},{4,20},{20... | collective-permute-start | bytes 1769480 | tf_op jit(solution)/shard_map/ppermute | solution.py:546
  74.7 39.9 %collective-permute-start.19 = (bf16[384,768]{1,0:T(8,128)(2,1)}, bf16[384,768]{1,0:T(8,128)(2,1)}, u32[]{:S(2)}, u32[]{:S(2)}) collective-permute-start(bf16[384,768]{1,0:T(8,128)(2,1)} %refs_0_.4), channel_id=1, source_target_pairs={{0,16},{16,0},{1,17},{17,1},{2,18},{18,2},{3,19},{19,3},{4,20},{20... | collective-permute-start | bytes 1769480 | tf_op jit(solution)/shard_map/ppermute | solution.py:546
  167.8 59.1 %collective-permute-start.28 = (bf16[1,1,2,2,128,128]{5,4,3,2,1,0:T(8,128)(2,1)}, bf16[1,1,2,2,128,128]{5,4,3,2,1,0:T(8,128)(2,1)}, u32[]{:S(2)}, u32[]{:S(2)}) collective-permute-start(bf16[1,1,2,2,128,128]{5,4,3,2,1,0:T(8,128)(2,1)} %get-tuple-element.145), channel_id=1, source_target_pairs={{0,8},{1,9},{2,10},{3,11},{4,12},{5,13},{6,14},{7,15},{8,0},{9,1},... | collective-permute-start | bytes 393224 | tf_op jit(solution)/shard_map/ppermute | solution.py:453
  169.9 57.0 %collective-permute-start.29 = (bf16[1,1,2,2,128,128]{5,4,3,2,1,0:T(8,128)(2,1)}, bf16[1,1,2,2,128,128]{5,4,3,2,1,0:T(8,128)(2,1)}, u32[]{:S(2)}, u32[]{:S(2)}) collective-permute-start(bf16[1,1,2,2,128,128]{5,4,3,2,1,0:T(8,128)(2,1)} %get-tuple-element.146), channel_id=1, source_target_pairs={{0,12},{1,13},{2,14},{3,15},{4,8},{5,9},{6,10},{7,11},{8,4},{9,5},... | collective-permute-start | bytes 393224 | tf_op jit(solution)/shard_map/ppermute | solution.py:453
  171.8 55.6 %collective-permute-start.27 = (bf16[1,1,2,2,128,128]{5,4,3,2,1,0:T(8,128)(2,1)}, bf16[1,1,2,2,128,128]{5,4,3,2,1,0:T(8,128)(2,1)}, u32[]{:S(2)}, u32[]{:S(2)}) collective-permute-start(bf16[1,1,2,2,128,128]{5,4,3,2,1,0:T(8,128)(2,1)} %slice.677), channel_id=1, source_target_pairs={{0,4},{1,5},{2,6},{3,7},{4,0},{5,1},{6,2},{7,3},{8,12},{9,13},{10,... | collective-permute-start | bytes 393224 | tf_op jit(solution)/shard_map/ppermute | solution.py:453
  173.8 54.8 %collective-permute-start.32 = (bf16[2,2,2,1,128,256]{5,4,3,2,1,0:T(8,128)(2,1)}, bf16[2,2,2,1,128,256]{5,4,3,2,1,0:T(8,128)(2,1)S(1)}, u32[]{:S(2)}, u32[]{:S(2)}) collective-permute-start(bf16[2,2,2,1,128,256]{5,4,3,2,1,0:T(8,128)(2,1)} %slice.685), channel_id=1, source_target_pairs={{0,1},{1,0},{2,3},{3,2},{4,5},{5,4},{6,7},{7,6},{8,9},{9,8},{10,11... | collective-permute-start | bytes 1572872 | tf_op jit(solution)/shard_map/ppermute | solution.py:453
  226.9 47.2 %collective-permute-start.99 = (bf16[16,192,384]{2,1,0:T(8,128)(2,1)}, bf16[16,192,384]{2,1,0:T(8,128)(2,1)S(1)}, u32[]{:S(2)}, u32[]{:S(2)}) collective-permute-start(bf16[16,192,384]{2,1,0:T(8,128)(2,1)} %get-tuple-element.82), channel_id=1, source_target_pairs={{0,16},{16,0},{1,17},{17,1},{2,18},{18,2},{3,19},{19,3},{4,20},{20... | collective-permute-start | bytes 7077896 | tf_op jit(solution)/shard_map/ppermute | solution.py:772
  226.9 48.0 %collective-permute-start.68 = (bf16[16,192,384]{2,1,0:T(8,128)(2,1)}, bf16[16,192,384]{2,1,0:T(8,128)(2,1)S(1)}, u32[]{:S(2)}, u32[]{:S(2)}) collective-permute-start(bf16[16,192,384]{2,1,0:T(8,128)(2,1)} %get-tuple-element.80), channel_id=1, source_target_pairs={{0,16},{16,0},{1,17},{17,1},{2,18},{18,2},{3,19},{19,3},{4,20},{20... | collective-permute-start | bytes 7077896 | tf_op jit(solution)/shard_map/ppermute | solution.py:773
  244.6 32.8 %collective-permute-start.37 = (bf16[16,192,384]{2,1,0:T(8,128)(2,1)S(1)}, bf16[16,192,384]{2,1,0:T(8,128)(2,1)S(1)}, u32[]{:S(2)}, u32[]{:S(2)}) collective-permute-start(bf16[16,192,384]{2,1,0:T(8,128)(2,1)S(1)} %copy-done.35), channel_id=1, source_target_pairs={{0,16},{16,0},{1,17},{17,1},{2,18},{18,2},{3,19},{19,3},{4,20},{20... | collective-permute-start | bytes 7077896 | tf_op jit(solution)/shard_map/ppermute | solution.py:774
  283.6 50.9 %collective-permute-start.120 = (bf16[2,2,2,1,48,384]{5,4,3,2,1,0:T(8,128)(2,1)S(1)}, bf16[2,2,2,1,48,384]{5,4,3,2,1,0:T(8,128)(2,1)S(1)}, u32[]{:S(2)}, u32[]{:S(2)}) collective-permute-start(bf16[2,2,2,1,48,384]{5,4,3,2,1,0:T(8,128)(2,1)S(1)} %slice.769), channel_id=1, source_target_pairs={{0,1},{1,0},{2,3},{3,2},{4,5},{5,4},{6,7},{7,6},{8,9},{9,8},{10,11... | collective-permute-start | bytes 884744 | tf_op jit(solution)/shard_map/ppermute | solution.py:453
  302.6 33.0 %collective-permute-start.89 = (bf16[2,2,2,1,48,384]{5,4,3,2,1,0:T(8,128)(2,1)S(1)}, bf16[2,2,2,1,48,384]{5,4,3,2,1,0:T(8,128)(2,1)S(1)}, u32[]{:S(2)}, u32[]{:S(2)}) collective-permute-start(bf16[2,2,2,1,48,384]{5,4,3,2,1,0:T(8,128)(2,1)S(1)} %slice.741), channel_id=1, source_target_pairs={{0,1},{1,0},{2,3},{3,2},{4,5},{5,4},{6,7},{7,6},{8,9},{9,8},{10,11... | collective-permute-start | bytes 884744 | tf_op jit(solution)/shard_map/ppermute | solution.py:453
  313.6 22.2 %collective-permute-start.58 = (bf16[2,2,2,1,48,384]{5,4,3,2,1,0:T(8,128)(2,1)S(1)}, bf16[2,2,2,1,48,384]{5,4,3,2,1,0:T(8,128)(2,1)S(1)}, u32[]{:S(2)}, u32[]{:S(2)}) collective-permute-start(bf16[2,2,2,1,48,384]{5,4,3,2,1,0:T(8,128)(2,1)S(1)} %slice.713), channel_id=1, source_target_pairs={{0,1},{1,0},{2,3},{3,2},{4,5},{5,4},{6,7},{7,6},{8,9},{9,8},{10,11... | collective-permute-start | bytes 884744 | tf_op jit(solution)/shard_map/ppermute | solution.py:453
  340.4 23.5 %collective-permute-start.85 = (bf16[1,1,2,1,48,384]{5,4,3,2,1,0:T(8,128)(2,1)S(1)}, bf16[1,1,2,1,48,384]{5,4,3,2,1,0:T(8,128)(2,1)S(1)}, u32[]{:S(2)}, u32[]{:S(2)}) collective-permute-start(bf16[1,1,2,1,48,384]{5,4,3,2,1,0:T(8,128)(2,1)S(1)} %pad_maximum_fusion.25), channel_id=1, source_target_pairs={{0,1},{1,0},{2,3},{3,2},{4,5},{5,4},{6,7},{7,6},{8,9},{9,8},{10,11... | collective-permute-start | bytes 221192 | tf_op jit(solution)/shard_map/ppermute | solution.py:453
  357.6 31.5 %collective-permute-start.117 = (bf16[1,1,2,2,48,384]{5,4,3,2,1,0:T(8,128)(2,1)S(1)}, bf16[1,1,2,2,48,384]{5,4,3,2,1,0:T(8,128)(2,1)S(1)}, u32[]{:S(2)}, u32[]{:S(2)}) collective-permute-start(bf16[1,1,2,2,48,384]{5,4,3,2,1,0:T(8,128)(2,1)S(1)} %pad_maximum_fusion.20), channel_id=1, source_target_pairs={{0,4},{1,5},{2,6},{3,7},{4,0},{5,1},{6,2},{7,3},{8,12},{9,13},{10,... | collective-permute-start | bytes 442376 | tf_op jit(solution)/shard_map/ppermute | solution.py:453
  358.3 32.6 %collective-permute-start.118 = (bf16[1,1,2,2,48,384]{5,4,3,2,1,0:T(8,128)(2,1)S(1)}, bf16[1,1,2,2,48,384]{5,4,3,2,1,0:T(8,128)(2,1)S(1)}, u32[]{:S(2)}, u32[]{:S(2)}) collective-permute-start(bf16[1,1,2,2,48,384]{5,4,3,2,1,0:T(8,128)(2,1)S(1)} %pad_maximum_fusion.20), channel_id=1, source_target_pairs={{0,8},{1,9},{2,10},{3,11},{4,12},{5,13},{6,14},{7,15},{8,0},{9,1},... | collective-permute-start | bytes 442376 | tf_op jit(solution)/shard_map/ppermute | solution.py:453
  361.8 30.9 %collective-permute-start.119 = (bf16[1,1,2,2,48,384]{5,4,3,2,1,0:T(8,128)(2,1)S(1)}, bf16[1,1,2,2,48,384]{5,4,3,2,1,0:T(8,128)(2,1)S(1)}, u32[]{:S(2)}, u32[]{:S(2)}) collective-permute-start(bf16[1,1,2,2,48,384]{5,4,3,2,1,0:T(8,128)(2,1)S(1)} %pad_maximum_fusion.20), channel_id=1, source_target_pairs={{0,12},{1,13},{2,14},{3,15},{4,8},{5,9},{6,10},{7,11},{8,4},{9,5},... | collective-permute-start | bytes 442376 | tf_op jit(solution)/shard_map/ppermute | solution.py:453
  364.7 28.8 %collective-permute-start.86 = (bf16[1,1,2,2,48,384]{5,4,3,2,1,0:T(8,128)(2,1)S(1)}, bf16[1,1,2,2,48,384]{5,4,3,2,1,0:T(8,128)(2,1)S(1)}, u32[]{:S(2)}, u32[]{:S(2)}) collective-permute-start(bf16[1,1,2,2,48,384]{5,4,3,2,1,0:T(8,128)(2,1)S(1)} %pad_maximum_fusion.19), channel_id=1, source_target_pairs={{0,4},{1,5},{2,6},{3,7},{4,0},{5,1},{6,2},{7,3},{8,12},{9,13},{10,... | collective-permute-start | bytes 442376 | tf_op jit(solution)/shard_map/ppermute | solution.py:453
  403.4 27.3 %collective-permute-start.100 = (bf16[2,2,1,2,96,384]{5,4,3,2,1,0:T(8,128)(2,1)S(1)}, bf16[2,2,1,2,96,384]{5,4,3,2,1,0:T(8,128)(2,1)S(1)}, u32[]{:S(2)}, u32[]{:S(2)}) collective-permute-start(bf16[2,2,1,2,96,384]{5,4,3,2,1,0:T(8,128)(2,1)S(1)} %slice.750), channel_id=1, source_target_pairs={{0,2},{1,3},{2,0},{3,1},{4,6},{5,7},{6,4},{7,5},{8,10},{9,11},{10,... | collective-permute-start | bytes 1769480 | tf_op jit(solution)/shard_map/ppermute | solution.py:453
  404.4 27.6 %collective-permute-start.69 = (bf16[2,2,1,2,96,384]{5,4,3,2,1,0:T(8,128)(2,1)S(1)}, bf16[2,2,1,2,96,384]{5,4,3,2,1,0:T(8,128)(2,1)S(1)}, u32[]{:S(2)}, u32[]{:S(2)}) collective-permute-start(bf16[2,2,1,2,96,384]{5,4,3,2,1,0:T(8,128)(2,1)S(1)} %slice.722), channel_id=1, source_target_pairs={{0,2},{1,3},{2,0},{3,1},{4,6},{5,7},{6,4},{7,5},{8,10},{9,11},{10,... | collective-permute-start | bytes 1769480 | tf_op jit(solution)/shard_map/ppermute | solution.py:453
  429.5 63.0 %collective-permute-start.98 = (bf16[2,2,2,1,48,384]{5,4,3,2,1,0:T(8,128)(2,1)S(1)}, bf16[2,2,2,1,48,384]{5,4,3,2,1,0:T(8,128)(2,1)S(1)}, u32[]{:S(2)}, u32[]{:S(2)}) collective-permute-start(bf16[2,2,2,1,48,384]{5,4,3,2,1,0:T(8,128)(2,1)S(1)} %maximum_maximum_fusion.9), channel_id=1, source_target_pairs={{0,1},{1,0},{2,3},{3,2},{4,5},{5,4},{6,7},{7,6},{8,9},{9,8},{10,11... | collective-permute-start | bytes 884744 | tf_op jit(solution)/shard_map/ppermute | solution.py:453
  433.5 22.8 %collective-permute-start.39 = (bf16[2,2,1,1,96,384]{5,4,3,2,1,0:T(8,128)(2,1)S(1)}, bf16[2,2,1,1,96,384]{5,4,3,2,1,0:T(8,128)(2,1)S(1)}, u32[]{:S(2)}, u32[]{:S(2)}) collective-permute-start(bf16[2,2,1,1,96,384]{5,4,3,2,1,0:T(8,128)(2,1)S(1)} %slice.696), channel_id=1, source_target_pairs={{0,1},{1,0},{2,3},{3,2},{4,5},{5,4},{6,7},{7,6},{8,9},{9,8},{10,11... | collective-permute-start | bytes 884744 | tf_op jit(solution)/shard_map/ppermute | solution.py:453
  497.3 27.6 %collective-permute-start.47 = (bf16[2,2,1,2,96,384]{5,4,3,2,1,0:T(8,128)(2,1)}, bf16[2,2,1,2,96,384]{5,4,3,2,1,0:T(8,128)(2,1)}, u32[]{:S(2)}, u32[]{:S(2)}) collective-permute-start(bf16[2,2,1,2,96,384]{5,4,3,2,1,0:T(8,128)(2,1)} %pad_maximum_fusion.9), channel_id=1, source_target_pairs={{0,2},{1,3},{2,0},{3,1},{4,6},{5,7},{6,4},{7,5},{8,10},{9,11},{10,... | collective-permute-start | bytes 1769480 | tf_op jit(solution)/shard_map/ppermute | solution.py:453
  (142 other events, 1756.7 us)

commit v2 on v1

--- a/solution.py
+++ b/solution.py
@@ -16,6 +16,10 @@
 vmem_bytes = 60 * 1024 * 1024
 low = jnp.bfloat16
 f32 = jnp.float32
+def cost(microseconds):
+    return pl.CostEstimate(flops=int(microseconds * 1e9), bytes_accessed=0, transcendentals=0)
+
+
 any_space = pl.BlockSpec(memory_space=pl.ANY)
 smem_space = pl.BlockSpec(memory_space=pltpu.SMEM)
 vmem_space = pl.BlockSpec(memory_space=pltpu.VMEM)
@@ -45,8 +49,24 @@
     ]
 
 
-def scalar_at(scalars, slots, micro, entry):
-    return scalars[2 + (3 + slots) * micro + entry]
+def scalar_at(scalars, micro, entry):
+    return scalars[2 + 5 * micro + entry]
+
+
+def block_index(at, total):
+    return tuple((at >> (total - 1 - i)) & 1 for i in range(total))
+
+
+def half_index(bit, which, total):
+    everything = [slice(None)] * total
+    everything[total - 1 - bit] = pl.ds(which, 1)
+    return tuple(everything)
+
+
+def half_at(bit, which, total):
+    everything = [slice(None)] * total
+    everything[total - 1 - bit] = which
+    return tuple(everything)
 
 
 def query_kernel(pieces, scalars, rows, vectors, *refs):
@@ -62,31 +82,48 @@
     query_segment[...] = (raw + vectors[10:11, :]).astype(low)
 
 
-def keys_kernel(pieces, columns, run, slots, scalars, *refs):
-    parts = refs[: len(columns)]
-    refs = refs[len(columns) :]
+def keys_kernel(pieces, columns, lasts, run, slots, scalars, *refs):
+    parts = refs[: 2 * len(columns)]
+    refs = refs[2 * len(columns) :]
     key_weights, value_weights = refs[:pieces], refs[pieces : 2 * pieces]
-    path, keys, values, full_key, full_value, sems, path_sems = refs[2 * pieces :]
+    path, keys, values, found, full_key, full_value, tree, sems, tree_sems = refs[2 * pieces :]
     shard = scalars[0]
+    total = len(tree.shape) - 2
+    moves = []
+    for part, (start, width) in enumerate(columns):
+        for which in range(2):
+            source = parts[2 * part + which]
+            target = tree.at[
+                (*half_index(lasts[part], which, total), pl.ds(0, source.shape[-2]), pl.ds(start, width))
+            ]
+            moves.append(pltpu.make_async_copy(source, target, tree_sems.at[2 * part + which]))
     copies = weight_copies(key_weights, full_key, sems, 0, shard)
     copies = copies + weight_copies(value_weights, full_value, sems, pieces, shard)
-    moves = []
-    micro_count = path.shape[0]
-    for micro in range(micro_count):
-        for slot in range(slots):
-            relative = scalar_at(scalars, slots, micro, 3 + slot)
-            for part, (start, width) in enumerate(columns):
-                index = (micro * slots + slot) * len(columns) + part
-                moves.append(
-                    pltpu.make_async_copy(
-                        parts[part].at[relative, pl.ds(micro * run, run), :],
-                        path.at[micro, pl.ds(slot * run, run), pl.ds(start, width)],
-                        path_sems.at[index],
-                    )
-                )
     for copy in moves + copies:
         copy.start()
-    for copy in moves + copies:
+    for copy in moves:
+        copy.wait()
+    micro_count = path.shape[0]
+    content_rows = micro_count * run
+    facts = [
+        tree[(*block_index(block, total), slice(content_rows, content_rows + 16), slice(0, 128))].astype(f32)
+        for block in range(1 << total)
+    ]
+    numbers = lax.broadcasted_iota(jnp.int32, (1 << total, 128), 0)
+    for micro in range(micro_count):
+        segs = jnp.concatenate([entry[2 * micro : 2 * micro + 1] for entry in facts], axis=0).astype(jnp.int32)
+        places = jnp.concatenate([entry[2 * micro + 1 : 2 * micro + 2] for entry in facts], axis=0).astype(jnp.int32)
+        for slot in range(slots):
+            if slot < slots // path_runs * trunk_runs:
+                wanted = 0
+            else:
+                wanted = scalar_at(scalars, micro, 4 if slot < slots // path_runs * (trunk_runs + 1) else 3)
+            shown = (segs == wanted) & (places == slot)
+            relative = jnp.max(jnp.where(shown, numbers, 0))
+            found[micro * slots + slot] = relative
+            at = block_index(relative, total)
+            path[micro, slot * run : (slot + 1) * run, :] = tree[(*at, slice(micro * run, (micro + 1) * run), slice(None))]
+    for copy in copies:
         copy.wait()
     for micro in range(micro_count):
         rows = path[micro]
@@ -122,7 +159,7 @@
 
 def attend_kernel(run, slots, scalars, table, query_low, query_segment, keys, values, vectors, probs, attended):
     pair, micro = pl.program_id(0), pl.program_id(1)
-    base, lo, hi = (scalar_at(scalars, slots, micro, entry) for entry in range(3))
+    base, lo, hi = (scalar_at(scalars, micro, entry) for entry in range(3))
     span = slots * run
     first, mask_a, mask_b = head_masks()
     left = stack_query(query_low[...], query_segment[...], mask_a, mask_b)
@@ -168,15 +205,34 @@
     return jnp.sum(inputs, axis=0, keepdims=True)
 
 
+def feed_cuts(pieces, model):
+    if pieces == 1:
+        return ()
+    step = model // 6
+    return ((0, step), (step, step), (2 * step, step))
+
+
+def later_cuts(model):
+    whole = model // 4 + 16
+    step = whole // 48 * 16
+    return ((0, step), (step, step), (2 * step, whole - 2 * step))
+
+
+def tree_cuts(height):
+    step = height // 48 * 16 + 16
+    return ((0, step), (step, step), (2 * step, height - 2 * step))
+
+
 def feed_kernel(pieces, run, scalars, rows, attended, cotangent, vectors, inner_bias, *refs):
     out_weights, inner_weights, outer_weights = (refs[i * pieces : (i + 1) * pieces] for i in range(3))
     refs = refs[3 * pieces :]
     out_content, out_query, d_mid_in, d_branch_out, d_att, small = refs[:6]
+    routes = feed_cuts(pieces, rows.shape[1])
     outputs = 4 if pieces == 2 else 2
     grads = refs[6 : 6 + outputs]
     full_out, full_inner, full_outer, act_low, slope = refs[6 + outputs : 11 + outputs]
     if pieces == 2:
-        held_outer, held_inner, sems, grad_sems = refs[11 + outputs :]
+        held, sems, grad_sems = refs[11 + outputs :]
     else:
         (sems,) = refs[11 + outputs :]
     shard, place = scalars[0], scalars[1]
@@ -238,7 +294,7 @@
         for down in range(2):
             for across in range(2):
                 chunk = ((start % half) // (block // 2) + down) * 2 + across
-                held_outer[target, chunk ^ place] = value[
+                held[(target, *block_index(chunk ^ place, 4), slice(0, block // 2), slice(None))] = value[
                     down * (block // 2) : (down + 1) * (block // 2), across * block : (across + 1) * block
                 ].astype(low)
 
@@ -248,20 +304,14 @@
             return
         for quarter in range(4):
             chunk = (quarter % 2) * 8 + start // block
-            held_inner[(quarter // 2) ^ shard, chunk ^ place] = value[
+            held[
+                ((quarter // 2) ^ shard, *block_index(chunk ^ place, 4), slice(block // 2, block), slice(None))
+            ] = value[
                 quarter * (block // 2) : (quarter + 1) * (block // 2), :
             ].astype(low)
 
     for start in range(0, hidden, block):
         hold_outer(start, mm_tn(act_low[:, start : start + block], d_outer))
-    sent = []
-    if pieces == 2:
-        sent = [
-            pltpu.make_async_copy(held_outer.at[0], grads[0], grad_sems.at[0]),
-            pltpu.make_async_copy(held_outer.at[1], grads[1], grad_sems.at[1]),
-        ]
-        for copy in sent:
-            copy.start()
     d_middle = d_final_in
     for start in range(0, hidden, block):
         at = slice(start, start + block)
@@ -271,14 +321,16 @@
         small[row : row + 1, lane : lane + block] = summed
         hold_inner(start, mm_tn(middle_low, d_inner))
         d_middle = d_middle + mm_nt(d_inner, full_inner[:, at])
-    if pieces == 2:
-        late = [
-            pltpu.make_async_copy(held_inner.at[0], grads[2], grad_sems.at[2]),
-            pltpu.make_async_copy(held_inner.at[1], grads[3], grad_sems.at[3]),
-        ]
-        for copy in late:
-            copy.start()
-        sent = sent + late
+    sent = []
+    for part, (start, height) in enumerate(routes):
+        for side in range(2):
+            for which in range(2):
+                rows_at = (pl.ds(start, height), slice(None))
+                source = held.at[(side, *half_at(routes_out[part][0], which, 4), *rows_at)]
+                target = grads[2 * side + which].at[(*(slice(None),) * 3, *rows_at)]
+                sent.append(pltpu.make_async_copy(source, target, grad_sems.at[4 * part + 2 * side + which]))
+    for copy in sent:
+        copy.start()
     small[5:6, :] = column_sum(d_middle * normal_first)
     small[6:7, :] = column_sum(d_middle)
     small[9:16, :] = jnp.zeros((7, model), f32)
@@ -310,7 +362,7 @@
     buckets,
 ):
     micro = pl.program_id(1)
-    base, lo = scalar_at(scalars, slots, micro, 0), scalar_at(scalars, slots, micro, 1)
+    base, lo = scalar_at(scalars, micro, 0), scalar_at(scalars, micro, 1)
     span = slots * run
     first, mask_a, mask_b = head_masks()
     gradient = d_att[...]
@@ -375,23 +427,39 @@
             buckets[head] += tallies[head]
 
 
-def weights_kernel(pieces, columns, run, slots, scalars, rows, path, attended, d_branch, d_query, d_keys, d_values, d_mid_in, *refs):
+def weights_kernel(
+    pieces,
+    run,
+    slots,
+    scalars,
+    found,
+    rows,
+    path,
+    attended,
+    d_branch,
+    d_query,
+    d_keys,
+    d_values,
+    d_mid_in,
+    small_first,
+    small_second,
+    tallies,
+    *refs,
+):
     weights = [refs[i * pieces : (i + 1) * pieces] for i in range(3)]
     refs = refs[3 * pieces :]
     d_content, d_state = refs[:2]
-    parts = refs[2 : 2 + len(columns)]
-    refs = refs[2 + len(columns) :]
+    model = rows.shape[1]
+    block = model // 2
     if pieces == 2:
-        kept, sent, full, held, sems, grad_sems = refs
+        kept, sent, full, tree, held, sems, grad_sems = refs[2:4], refs[4:6], *refs[6:]
     else:
-        natural, full, sems = refs[:4], refs[4], refs[5]
+        natural, tree_out, small_out, full, tree, sems, grad_sems = refs[2:6], *refs[6:]
     shard, place = scalars[0], scalars[1]
     copies = [weight_copies(weights[i], full.at[i], sems, i * pieces, shard) for i in range(3)]
     for group in copies:
         for copy in group:
             copy.start()
-    model = rows.shape[1]
-    block = model // 2
     small_rows = block // 8
 
     def hold(which, value):
@@ -402,7 +470,8 @@
             for down in range(8):
                 for across in range(2):
                     start = half * block + down * small_rows
-                    held[half ^ shard, (down * 2 + across) ^ place, which * small_rows : (which + 1) * small_rows, :] = value[
+                    spot = slice(which * small_rows, (which + 1) * small_rows)
+                    held[(half ^ shard, *block_index((down * 2 + across) ^ place, 4), spot, slice(None))] = value[
                         start : start + small_rows, across * block : (across + 1) * block
                     ].astype(low)
 
@@ -410,96 +479,263 @@
     hold(1, mm_tn(path[...], d_keys[...]))
     hold(2, mm_tn(path[...], d_values[...]))
     hold(3, mm_tn(attended[...].astype(low), d_branch[...]))
+    ones = jnp.ones((8, tallies.shape[2]), f32)
+    sums = []
+    for head in range(tallies.shape[0]):
+        sums.append(
+            lax.dot_general(
+                ones,
+                tallies[head],
+                (((1,), (1,)), ((), ())),
+                precision=lax.Precision.HIGHEST,
+                preferred_element_type=f32,
+            )[:1]
+        )
+    buckets = jnp.concatenate(sums, axis=0)
+    if pieces == 1:
+        small_out[:9, :] = small_first[:9, :]
+        small_out[9:13, :] = small_second[:4, :]
+        small_out[13:, :] = jnp.zeros((small_out.shape[0] - 13, model), f32)
+        small_out[16 : 16 + buckets.shape[0], :16] = buckets
+    else:
+        last = model // 4
+        for half in range(2):
+            at = slice(half * block, (half + 1) * block)
+            lines = [
+                small_first[2 * half + i // 2 : 2 * half + i // 2 + 1, (i % 2) * block : (i % 2 + 1) * block]
+                for i in range(4)
+            ]
+            lines += [small_first[i : i + 1, at] for i in range(4, 9)]
+            lines += [small_second[i : i + 1, at] for i in range(4)]
+            for chunk in range(16):
+                line = lines[chunk].astype(low) if chunk < 13 else jnp.zeros((1, block), low)
+                spread_line = jnp.concatenate([line.astype(f32), jnp.zeros((15, block), f32)], axis=0)
+                held[(half ^ shard, *block_index(chunk ^ place, 4), slice(last, last + 16), slice(None))] = spread_line.astype(low)
+            wide = jnp.concatenate(
+                [buckets[:, 8 * half : 8 * half + 8], jnp.zeros((buckets.shape[0], block - 8), f32)], axis=1
+            )
+            wide = jnp.concatenate([wide, jnp.zeros((16 - buckets.shape[0], block), f32)], axis=0)
+            held[(half ^ shard, *block_index(13 ^ place, 4), slice(last, last + 16), slice(None))] = wide.astype(low)
     leaving = []
     if pieces == 2:
-        leaving = [
-            pltpu.make_async_copy(held.at[0], kept, grad_sems.at[0]),
-            pltpu.make_async_copy(held.at[1], sent, grad_sems.at[1]),
-        ]
+        for part, (start, height) in enumerate(later_cuts(model)):
+            for which in range(2):
+                at = 2 * part + which
+                rows_at = (pl.ds(start, height), slice(None))
+                for side in range(2):
+                    source = held.at[(side, *half_at(routes_out[part][0], which, 4), *rows_at)]
+                    target = (kept, sent)[side][which].at[(*(slice(None),) * 3, *rows_at)]
+                    leaving.append(pltpu.make_async_copy(source, target, grad_sems.at[6 * side + at]))
         for copy in leaving:
             copy.start()
     for group in copies:
         for copy in group:
             copy.wait()
-    for part in parts:
-        part[...] = jnp.zeros(part.shape, part.dtype)
+    tree[...] = jnp.zeros(tree.shape, tree.dtype)
     span = slots * run
-    for micro in range(rows.shape[0] // (2 * run)):
+    micro_count = rows.shape[0] // (2 * run)
+    for micro in range(micro_count):
         at = slice(micro * span, (micro + 1) * span)
         shares = mm_nt(d_keys[at, :], full[1]) + mm_nt(d_values[at, :], full[2])
         for slot in range(slots):
-            relative = scalar_at(scalars, slots, micro, 3 + slot)
-            for part, (start, width) in enumerate(columns):
-                piece = shares[slot * run : (slot + 1) * run, start : start + width]
-                spot = (relative, slice(micro * run, (micro + 1) * run), slice(None))
-                parts[part][spot] = (parts[part][spot].astype(f32) + piece).astype(low)
+            relative = found[micro * slots + slot]
+            for half in range(2):
+                piece = shares[slot * run : (slot + 1) * run, half * block : (half + 1) * block]
+                start = (half * micro_count + micro) * run
+                spot = (*block_index(relative, len(tree.shape) - 2), slice(start, start + run), slice(None))
+                tree[spot] = (tree[spot].astype(f32) + piece).astype(low)
+    if pieces == 2:
+        last_copies = []
+        skip = model // 4 + 16
+        for part, (start, height) in enumerate(tree_cuts(tree.shape[-2])):
+            for which in range(2):
+                source = tree.at[(*half_at(routes_out[part][0], which, 4), pl.ds(start, height), slice(None))]
+                target = kept[which].at[(*(slice(None),) * 3, pl.ds(skip + start, height), slice(None))]
+                last_copies.append(pltpu.make_async_copy(source, target, grad_sems.at[12 + 2 * part + which]))
+    else:
+        last_copies = [pltpu.make_async_copy(tree, tree_out, grad_sems.at[0])]
+    for copy in last_copies:
+        copy.start()
     d_both = d_mid_in[...] + mm_nt(d_query[...], full[0])
-    for micro in range(rows.shape[0] // (2 * run)):
+    for micro in range(micro_count):
         start = 2 * run * micro
         d_content[micro] = d_both[start : start + run]
         d_state[micro] = d_both[start + run : start + 2 * run]
-    for copy in leaving:
+    for copy in leaving + last_copies:
         copy.wait()
 
 
-def spread_kernel(layout, scalars, *refs):
-    source, targets = refs[0], refs[1:]
-    for which, target in enumerate(targets):
-        rows = target.shape[0]
-        target[...] = source[0, which * rows : (which + 1) * rows, :].astype(f32)
-
-
-def send(inputs, mask):
-    return lax.ppermute(inputs, "dp", [(i, i ^ mask) for i in range(lax.axis_size("dp"))])
-
-
-def bits_of(order):
-    named = {"x": (0,), "y": (1,), "z": (2, 3)}
-    total = lax.axis_size("dp").bit_length() - 1
-    return [named[axis] for axis in order] + [(bit,) for bit in range(4, total)], total
-
-
-def gather_blocks(block, order):
-    stages, total = bits_of(order)
-    held = block.reshape((1,) * total + block.shape)
-    for bits in stages:
-        if len(bits) == 2:
-            near, far, both = send(held, 4), send(held, 8), send(held, 12)
-            at = total - 1 - bits[0]
-            held = jnp.concatenate(
-                [jnp.concatenate([held, near], axis=at), jnp.concatenate([far, both], axis=at)], axis=at - 1
-            )
-        else:
-            held = jnp.concatenate([held, send(held, 1 << bits[0])], axis=total - 1 - bits[0])
-    return held.reshape((1 << total,) + block.shape)
-
-
-def scatter_blocks(blocks, order):
-    stages, total = bits_of(order[::-1])
-    held = blocks.reshape((2,) * total + blocks.shape[1:])
-
-    def part(inputs, bit, which):
-        return lax.slice_in_dim(inputs, which, which + 1, axis=total - 1 - bit)
-
-    for bits in stages[::-1]:
-        if len(bits) == 2:
-            lower, upper = part(held, 3, 0), part(held, 3, 1)
-            near, far, both = send(part(lower, 2, 1), 4), send(part(upper, 2, 0), 8), send(part(upper, 2, 1), 12)
-            held = (part(lower, 2, 0).astype(f32) + near + far + both).astype(low)
-        else:
-            held = part(held, bits[0], 0) + send(part(held, bits[0], 1), 1 << bits[0])
-    return held.reshape(blocks.shape[1:])
-
-
-def all_sum(blocks):
-    rows = blocks.shape[1]
-    cuts = (0, rows // 2, rows * 3 // 4, rows)
-    orders = ("yxz", "zxy", "xzy")
-    pieces = []
-    for part, order in enumerate(orders):
-        share = scatter_blocks(blocks[:, cuts[part] : cuts[part + 1]], order)
-        pieces.append(gather_blocks(share, order[::-1]))
-    return jnp.concatenate(pieces, axis=1)
+def collect_pieces(refs, held, sems):
+    copies = []
+    for part, route in enumerate(routes_out):
+        for which in range(2):
+            at = 2 * part + which
+            target = held[part].at[(*half_index(route[0], which, 4), slice(None), slice(None))]
+            copies.append(pltpu.make_async_copy(refs[at], target, sems.at[at]))
+    for copy in copies:
+        copy.start()
+    for copy in copies:
+        copy.wait()
+
+
+def feed_spread_kernel(scalars, *refs):
+    outer, inner, first, second, third, sems = refs[6:]
+    collect_pieces(refs[:6], (first, second, third), sems)
+    place = scalars[1]
+    height, side = first.shape[-2:]
+    total = 3 * height // 2
+    for chunk in range(16):
+        at = block_index(chunk ^ place, 4)
+        down, across = (chunk // 2) * total, (chunk % 2) * side
+        outer[down : down + height, across : across + side] = first[at].astype(f32)
+        middle = second[at].astype(f32)
+        outer[down + height : down + total, across : across + side] = middle[: total - height]
+        down, across = (chunk // 8) * total, (chunk % 8) * side
+        inner[down : down + total - height, across : across + side] = middle[total - height :]
+        inner[down + total - height : down + total, across : across + side] = third[at].astype(f32)
+
+
+def later_spread_kernel(scalars, *refs):
+    weights, small, sources, sems = refs[6:10], refs[10], refs[11:14], refs[14]
+    collect_pieces(refs[:6], sources, sems)
+    place = scalars[1]
+    side = sources[0].shape[-1]
+    rows = weights[0].shape[0] // 8
+    cuts = later_cuts(2 * side)
+    for chunk in range(16):
+        at = block_index(chunk ^ place, 4)
+        down, across = (chunk // 2) * rows, (chunk % 2) * side
+        for source, (start, height) in zip(sources, cuts):
+            value = source[at].astype(f32)
+            for which in range(4):
+                begin, end = max(start, which * rows), min(start + height, (which + 1) * rows)
+                if begin < end:
+                    top = down + begin - which * rows
+                    weights[which][top : top + end - begin, across : across + side] = value[begin - start : end - start]
+            begin = 4 * rows
+            if start <= begin < start + height:
+                small[chunk] = value[begin - start : begin - start + 16]
+
+
+routes_out = ((0, 1, 2), (1, 2, 0), (2, 0, 1))
+
+
+def send(inputs, bit):
+    count = lax.axis_size("dp")
+    return lax.ppermute(inputs, "dp", [(i, i ^ (1 << bit)) for i in range(count)])
+
+
+def half_dims(bit):
+    return tuple(1 if i == bit_total() - 1 - bit else 2 for i in range(bit_total()))
+
+
+def bit_total():
+    return lax.axis_size("dp").bit_length() - 1
+
+
+def extra_bits():
+    return tuple(range(3, bit_total()))
+
+
+def grow(held, bit):
+    return jnp.concatenate([held, send(held, bit)], axis=bit_total() - 1 - bit)
+
+
+def part_of(held, bit, which):
+    total = bit_total()
+    if held.ndim == 3:
+        held = held.reshape((2,) * total + held.shape[1:])
+    return lax.slice_in_dim(held, which, which + 1, axis=total - 1 - bit)
+
+
+def scatter_rest(held, route):
+    for bit in route + extra_bits()[::-1]:
+        held = part_of(held, bit, 0) + send(part_of(held, bit, 1), bit)
+    return held.reshape(held.shape[-2:])
+
+
+def scatter_blocks(blocks, route):
+    held = part_of(blocks, route[0], 0) + send(part_of(blocks, route[0], 1), route[0])
+    return scatter_rest(held, route[1:])
+
+
+def axis_of(bit):
+    return bit_total() - 1 - bit
+
+
+def sum_rounds(lower, upper, keep):
+    ready = yield list(upper)
+    held = [own + send(entry, route[0]) for own, entry, route in zip(lower, ready, routes_out)]
+    for step in (1, 2):
+        ready = yield [part_of(entry, route[step], 1) for entry, route in zip(held, routes_out)]
+        held = [
+            part_of(entry, route[step], 0) + send(other, route[step])
+            for entry, other, route in zip(held, ready, routes_out)
+        ]
+    for bit in extra_bits()[::-1]:
+        (ready,) = yield [jnp.concatenate([part_of(entry, bit, 1) for entry in held], axis=-2)]
+        arrived = send(ready, bit)
+        start, later = 0, []
+        for entry in held:
+            height = entry.shape[-2]
+            later.append(part_of(entry, bit, 0) + arrived[..., start : start + height, :])
+            start += height
+        held = later
+    shares = held
+    joined = jnp.concatenate([entry[..., :rows, :] for entry, rows in zip(held, keep)], axis=-2)
+    for bit in extra_bits():
+        (ready,) = yield [joined]
+        joined = jnp.concatenate([joined, send(ready, bit)], axis=axis_of(bit))
+    start, held = 0, []
+    for rows in keep:
+        held.append(joined[..., start : start + rows, :])
+        start += rows
+    for step in (2, 1):
+        ready = yield held
+        held = [
+            jnp.concatenate([entry, send(entry, route[step])], axis=axis_of(route[step]))
+            for entry, route in zip(ready, routes_out)
+        ]
+    ready = yield held
+    arrived = [send(entry, route[0]) for entry, route in zip(ready, routes_out)]
+    return [piece for pair in zip(ready, arrived) for piece in pair], shares
+
+
+class Rounds:
+    def __init__(self, steps):
+        self.steps = steps
+        self.pending = next(steps)
+        self.result = None
+
+    def advance(self, ready):
+        try:
+            self.pending = self.steps.send(ready)
+        except StopIteration as stop:
+            self.pending, self.result = [], stop.value
+
+
+def advance_after(group, other):
+    joined = lax.optimization_barrier(list(group.pending) + list(other.pending))
+    group.advance(joined[: len(group.pending)])
+
+
+def advance_free(pending, others):
+    joined = lax.optimization_barrier(list(pending) + list(others))
+    return joined[: len(pending)], joined[len(pending) :]
+
+
+def spread_dims(held, route):
+    return jnp.expand_dims(held, axis_of(route[0]))
+
+
+def advance_together(groups, others=()):
+    joined = [entry for group in groups for entry in group.pending] + list(others)
+    joined = lax.optimization_barrier(joined)
+    for group in groups:
+        count = len(group.pending)
+        ready, joined = joined[:count], joined[count:]
+        group.advance(ready)
+    return joined
 
 
 def shards(
@@ -548,19 +784,49 @@
 
     own_seg = token_seg[:, 0]
     own_slot = positions[:, 0] // run
-    facts = jnp.stack([own_seg, own_slot], axis=1).reshape(2 * micro_count).astype(low)
-    columns = ((0, model // 2), (model // 2, model // 6), (model // 2 + model // 6, model // 3))
-    orders = ("zxy", "xyz", "yzx")
-    flat_content = content.reshape(micro_count * run, model)
-    fact_rows = jnp.broadcast_to(
-        jnp.pad(facts, (0, 16 - 2 * micro_count))[:, None], (16, columns[1][1])
+    facts = jnp.stack([own_seg, own_slot], axis=1).reshape(2 * micro_count, 1).astype(low)
+    fact_rows = jnp.broadcast_to(jnp.pad(facts, ((0, 16 - 2 * micro_count), (0, 0))), (16, model))
+    third = model // 3
+    columns = ((0, third), (third, third), (2 * third, third))
+    content_rows = micro_count * run
+    block = jnp.concatenate([content.reshape(content_rows, model), fact_rows], axis=0)
+    total_bits = bit_total()
+    block, b_inner, b_outer, parent, w_query, w_key = lax.optimization_barrier(
+        (block, b_inner, b_outer, parent, w_query, w_key)
     )
-    tree_parts = []
+    held = block.reshape((1,) * total_bits + block.shape)
+    for bit in extra_bits():
+        held = grow(held, bit)
+    query_weights, key_weights = fetch(w_query), fetch(w_key)
+    parts = []
     for part, (start, width) in enumerate(columns):
-        block = flat_content[:, start : start + width]
-        if part == 1:
-            block = jnp.concatenate([block, fact_rows], axis=0)
-        tree_parts.append(gather_blocks(block, orders[part]))
+        height = block.shape[0] if part == 0 else content_rows
+        parts.append(held[..., :height, start : start + width])
+    parts, (query_weights[-1], key_weights[-1], w_value, w_out) = advance_free(
+        parts, [query_weights[-1], key_weights[-1], w_value, w_out]
+    )
+    value_weights, out_weights = fetch(w_value), fetch(w_out)
+    parts = [grow(piece, route[2]) for piece, route in zip(parts, routes_out)]
+    parts, (value_weights[-1], out_weights[-1], w_inner) = advance_free(
+        parts, [value_weights[-1], out_weights[-1], w_inner]
+    )
+    inner_weights = fetch(w_inner)
+    parts = [grow(piece, route[1]) for piece, route in zip(parts, routes_out)]
+    parts, (inner_weights[-1], w_outer) = advance_free(parts, [inner_weights[-1], w_outer])
+    outer_weights = fetch(w_outer)
+    tree_parts = [entry for piece, route in zip(parts, routes_out) for entry in (piece, send(piece, route[0]))]
+    tree_parts, (outer_weights[-1],) = advance_free(tree_parts, [outer_weights[-1]])
+
+    first_branch, first_leaf = trunk_runs * per_run, (trunk_runs + 1) * per_run
+    mine = own_seg
+    above = jnp.sum(jnp.where(jnp.arange(parent.shape[2]) == mine[:, None], parent[:, 0], 0), axis=1)
+    trunk, leaf = mine == 0, mine > trunk_runs
+    branch = jnp.where(leaf, above, mine)
+    lo = jnp.where(trunk, 0, jnp.where(leaf, first_leaf, first_branch)) * run
+    hi = jnp.where(trunk, first_branch, jnp.where(leaf, slots, first_leaf)) * run
+    early = jnp.stack([shard, place]).astype(jnp.int32)
+    facts_own = jnp.stack([own_slot * run, lo, hi, mine, branch], axis=1)
+    scalars = jnp.concatenate([early, facts_own.reshape(-1)]).astype(jnp.int32)
 
     small_parts = jnp.concatenate(
         [
@@ -584,33 +850,6 @@
     vectors = jnp.transpose(gathered, (1, 0, 2)).reshape(16, model)
     table = gathered[:, 13, : rel_table.size].reshape(bucket_total, heads)
 
-    query_weights, key_weights, value_weights = fetch(w_query), fetch(w_key), fetch(w_value)
-    out_weights, inner_weights, outer_weights = fetch(w_out), fetch(w_inner), fetch(w_outer)
-
-    every = jnp.transpose(
-        tree_parts[1][:, micro_count * run : micro_count * run + 2 * micro_count, 0].astype(jnp.int32)
-    ).reshape(micro_count, 2, dp_count)
-    blocks = jnp.arange(dp_count, dtype=jnp.int32)
-    entries = [shard, place]
-    for micro in range(micro_count):
-        segs, slots_of = every[micro, 0], every[micro, 1]
-        mine = own_seg[micro]
-        above = jnp.sum(jnp.where(jnp.arange(parent.shape[2]) == mine, parent[micro, 0], 0))
-        trunk = mine == 0
-        leaf = mine > 4
-        branch = jnp.where(leaf, above, mine)
-        base = own_slot[micro] * run
-        first_branch, first_leaf = trunk_runs * per_run, (trunk_runs + 1) * per_run
-        lo = jnp.where(trunk, 0, jnp.where(leaf, first_leaf, first_branch)) * run
-        hi = jnp.where(trunk, first_branch, jnp.where(leaf, slots, first_leaf)) * run
-        entries += [base, lo, hi]
-        for slot in range(slots):
-            wanted = 0 if slot < first_branch else branch if slot < first_leaf else mine
-            shown = (segs == wanted) & (slots_of == slot)
-            entries.append(jnp.sum(jnp.where(shown, blocks, 0)))
-    scalars = jnp.stack([jnp.asarray(entry, jnp.int32) for entry in entries])
-    early = jnp.stack([jnp.asarray(entry, jnp.int32) for entry in entries[:2]])
-
     rows = jnp.concatenate([content, query_state], axis=1).reshape(rows_total, model)
     cotangent = jnp.concatenate([cot_content, cot_query], axis=1).reshape(rows_total, model)
     grown = pltpu.CompilerParams(vmem_limit_bytes=vmem_bytes)
@@ -627,25 +866,29 @@
         scratch_shapes=[pltpu.VMEM((model, model), low), dma((pieces,))],
         compiler_params=grown,
         name="query_projection",
+        cost_estimate=cost(4),
     )(early, rows, vectors, *query_weights)
 
-    path, keys, values = pl.pallas_call(
-        functools.partial(keys_kernel, pieces, columns, run, slots),
+    path, keys, values, found = pl.pallas_call(
+        functools.partial(keys_kernel, pieces, columns, [route[0] for route in routes_out], run, slots),
         out_shape=(
             shape((micro_count, span, model), low),
             shape((micro_count * span, model), low),
             shape((micro_count * span, model), low),
+            shape((micro_count * slots,), jnp.int32),
         ),
-        in_specs=[smem_space] + [any_space] * (len(columns) + 2 * pieces),
-        out_specs=(vmem_space,) * 3,
+        in_specs=[smem_space] + [any_space] * (2 * len(columns) + 2 * pieces),
+        out_specs=(vmem_space,) * 3 + (smem_space,),
         scratch_shapes=[
             pltpu.VMEM((model, model), low),
             pltpu.VMEM((model, model), low),
+            pltpu.VMEM((2,) * total_bits + (content_rows + 16, model), low),
             dma((2 * pieces,)),
-            dma((micro_count * slots * len(columns),)),
+            dma((2 * len(columns),)),
         ],
         compiler_params=grown,
         name="path_keys",
+        cost_estimate=cost(6),
     )(scalars, *tree_parts, *key_weights, *value_weights)
     path = path.reshape(micro_count * span, model)
 
@@ -664,13 +907,14 @@
         out_specs=(prob_block, row_block),
         compiler_params=grown,
         name="attend",
+        cost_estimate=cost(11),
     )(scalars, table, query_low, query_segment, keys, values, vectors)
 
-    chunk = (dp_count, hidden // (8 * shard_count), model // 2)
+    half = model // 2
     if pieces == 2:
-        grad_shapes = [shape(chunk, low)] * 4
-        grad_specs = [any_space] * 4
-        grad_scratch = [pltpu.VMEM((2,) + chunk, low)] * 2
+        grad_shapes = [shape((2,) * (total_bits - 1) + (half, half), low)] * 4
+        grad_specs = [any_space] * len(grad_shapes)
+        grad_scratch = [pltpu.VMEM((2,) * (1 + total_bits) + (half, half), low)]
     else:
         grad_shapes = [shape((hidden, model), low), shape((model, hidden), low)]
         grad_specs = [vmem_space] * 2
@@ -697,11 +941,17 @@
         ]
         + grad_scratch
         + [dma((3 * pieces,))]
-        + ([dma((4,))] if pieces == 2 else []),
+        + ([dma((12,))] if pieces == 2 else []),
         compiler_params=grown,
         name="feed_forward",
+        cost_estimate=cost(21),
     )(scalars, rows, attended, cotangent, vectors, inner_bias, *out_weights, *inner_weights, *outer_weights)
     out_content, out_query, d_mid_in, d_branch, d_att, small_first = results[:6]
+
+    swap = [(0, 1), (1, 0)]
+    if pieces == 2:
+        feed_grads = results[6:]
+        feed_other = [lax.ppermute(entry, "shard", swap) for entry in (feed_grads[3], feed_grads[2])]
 
     d_query, d_keys, d_values, small_second, tallies = pl.pallas_call(
         functools.partial(back_kernel, run, slots),
@@ -723,85 +973,138 @@
         ),
         compiler_params=grown,
         name="attend_back",
+        cost_estimate=cost(14),
     )(scalars, query_low, query_segment, keys, values, probs, d_att, attended, vectors)
 
     if pieces == 2:
-        grad_shapes = [shape(chunk, low)] * 2
-        grad_specs = [any_space] * 2
+        sizes = [height for _, height in feed_cuts(pieces, model)]
+        upper = [
+            spread_dims(feed_grads[1][..., start : start + height, :] + feed_other[0][..., start : start + height, :], route)
+            for (start, height), route in zip(feed_cuts(pieces, model), routes_out)
+        ]
+        feed_lower = feed_other[1]
+        *upper, feed_lower, d_query = lax.optimization_barrier((*upper, feed_lower, d_query))
+        lower = [
+            spread_dims(feed_grads[0][..., start : start + height, :] + feed_lower[..., start : start + height, :], route)
+            for (start, height), route in zip(feed_cuts(pieces, model), routes_out)
+        ]
+        feed_rounds = Rounds(sum_rounds(lower, upper, sizes))
+        feed_rounds.advance(feed_rounds.pending)
+    tree_height = 2 * micro_count * run
+    if pieces == 2:
+        whole = later_cuts(model)[-1][0] + later_cuts(model)[-1][1]
+        heights = [entry[1] for entry in later_cuts(model)]
+        grad_shapes = [shape((2,) * (total_bits - 1) + (whole + tree_height, half), low)] * 2
+        grad_shapes += [shape((2,) * (total_bits - 1) + (whole, half), low)] * 2
+        grad_specs = [any_space] * 4
+        extra = [pltpu.VMEM((2,) * (1 + total_bits) + (whole, half), low)]
     else:
-        grad_shapes = [shape((model, model), low)] * 4
-        grad_specs = [vmem_space] * 4
+        grad_shapes = [shape((model, model), low)] * 4 + [
+            shape((2,) * total_bits + (tree_height, half), low),
+            shape((32, model), f32),
+        ]
+        grad_specs = [vmem_space] * 4 + [any_space, vmem_space]
+        extra = []
     later = pl.pallas_call(
-        functools.partial(weights_kernel, pieces, columns, run, slots),
-        out_shape=[shape((micro_count, run, model), f32)] * 2
-        + [shape((dp_count, micro_count * run, width), low) for _, width in columns]
-        + grad_shapes,
-        in_specs=[smem_space] + [vmem_space] * 8 + [any_space] * (3 * pieces),
-        out_specs=[vmem_space] * (2 + len(columns)) + grad_specs,
-        scratch_shapes=[pltpu.VMEM((3, model, model), low)]
-        + ([pltpu.VMEM((2,) + chunk, low)] if pieces == 2 else [])
-        + [dma((3 * pieces,))]
-        + ([dma((2,))] if pieces == 2 else []),
+        functools.partial(weights_kernel, pieces, run, slots),
+        out_shape=[shape((micro_count, run, model), f32)] * 2 + grad_shapes,
+        in_specs=[smem_space] * 2 + [vmem_space] * 11 + [any_space] * (3 * pieces),
+        out_specs=[vmem_space] * 2 + grad_specs,
+        scratch_shapes=[pltpu.VMEM((3, model, model), low), pltpu.VMEM((2,) * total_bits + (tree_height, half), low)]
+        + extra
+        + [dma((3 * pieces,)), dma((18,))],
         compiler_params=grown,
         name="weight_gradients",
-    )(scalars, rows, path, attended, d_branch, d_query, d_keys, d_values, d_mid_in, *query_weights, *key_weights, *value_weights)
+        cost_estimate=cost(15),
+    )(
+        scalars,
+        found,
+        rows,
+        path,
+        attended,
+        d_branch,
+        d_query,
+        d_keys,
+        d_values,
+        d_mid_in,
+        small_first,
+        small_second,
+        tallies,
+        *query_weights,
+        *key_weights,
+        *value_weights,
+    )
     d_content, grad_query = later[:2]
-    tree_grads = later[2 : 2 + len(columns)]
-    later = later[2 + len(columns) :]
-
-    arrived = [scatter_blocks(part, order[::-1]) for part, order in zip(tree_grads, orders)]
-    grad_content = d_content + jnp.concatenate(arrived, axis=1).astype(f32).reshape(content.shape)
-
-    def spread(blocks_in, shapes, dims, place_of):
-        return pl.pallas_call(
-            functools.partial(spread_kernel, None),
-            grid_spec=pltpu.PrefetchScalarGridSpec(
-                num_scalar_prefetch=1,
-                grid=(dp_count,),
-                in_specs=[pl.BlockSpec((1,) + blocks_in.shape[1:], lambda i, s: (i ^ s[1], 0, 0))],
-                out_specs=[pl.BlockSpec(dims, place_of)] * len(shapes),
-            ),
-            out_shape=[shape(entry, f32) for entry in shapes],
+
+    if pieces == 2:
+        feed_rounds.pending, others = advance_free(feed_rounds.pending, [later[5], later[4]])
+        others = [lax.ppermute(entry, "shard", swap) for entry in others]
+        feed_rounds.advance(feed_rounds.pending)
+        feed_rounds.pending, others = advance_free(feed_rounds.pending, others)
+        feed_rounds.advance(feed_rounds.pending)
+
+        def route_sum(mine, other, part):
+            start, height = later_cuts(model)[part]
+            more, tall = tree_cuts(tree_height)[part]
+            summed = mine[..., start : start + height, :] + other[..., start : start + height, :]
+            more_rows = mine[..., whole + more : whole + more + tall, :]
+            return spread_dims(jnp.concatenate([summed, more_rows], axis=-2), routes_out[part])
+
+        lower = [route_sum(later[2], others[1], part) for part in range(3)]
+        upper = [route_sum(later[3], others[0], part) for part in range(3)]
+        later_rounds = Rounds(sum_rounds(lower, upper, heights))
+        for _ in range(5):
+            advance_after(later_rounds, feed_rounds)
+            feed_rounds.advance(feed_rounds.pending)
+        advance_together([later_rounds])
+        feed_done = advance_together([later_rounds], feed_rounds.result[0])
+        advance_together([later_rounds])
+
+        def pieces_scratch(sizes):
+            return [pltpu.VMEM((2,) * total_bits + (height, half), low) for height in sizes] + [dma((6,))]
+
+        grad_w_outer, grad_w_inner = pl.pallas_call(
+            feed_spread_kernel,
+            out_shape=(shape(w_outer.shape, f32), shape(w_inner.shape, f32)),
+            in_specs=[smem_space] + [any_space] * 6,
+            out_specs=(vmem_space,) * 2,
+            scratch_shapes=pieces_scratch([height for _, height in feed_cuts(pieces, model)]),
             compiler_params=grown,
-            name="spread",
-        )(early, blocks_in)
-
-    half = model // 2
-    if pieces == 2:
-        swap = [(0, 1), (1, 0)]
-        outer_sum = all_sum(results[6] + lax.ppermute(results[7], "shard", swap))
-        inner_sum = all_sum(results[8] + lax.ppermute(results[9], "shard", swap))
-        later_sum = all_sum(later[0] + lax.ppermute(later[1], "shard", swap))
-        (grad_w_outer,) = spread(outer_sum, [w_outer.shape], (chunk[1], half), lambda i, s: (i // 2, i % 2))
-        (grad_w_inner,) = spread(inner_sum, [w_inner.shape], (chunk[1], half), lambda i, s: (i // 8, i % 8))
-        grad_w_query, grad_w_key, grad_w_value, grad_w_out = spread(
-            later_sum, [w_query.shape] * 4, (half // 8, half), lambda i, s: (i // 2, i % 2)
-        )
+            name="feed_spread",
+            cost_estimate=cost(7),
+        )(early, *feed_done)
+        later_done, shares = later_rounds.result
+        arrived = [share.reshape(share.shape[-2:])[rows:] for share, rows in zip(shares, heights)]
+        tree_grad = jnp.concatenate(arrived, axis=0)
+        *squares, small = pl.pallas_call(
+            later_spread_kernel,
+            out_shape=[shape(w_query.shape, f32)] * 4 + [shape((dp_count, 16, half), f32)],
+            in_specs=[smem_space] + [any_space] * 6,
+            out_specs=[vmem_space] * 5,
+            scratch_shapes=pieces_scratch(heights),
+            compiler_params=grown,
+            name="later_spread",
+            cost_estimate=cost(4),
+        )(early, *later_done)
+        grad_w_query, grad_w_key, grad_w_value, grad_w_out = squares
+        grad_b_inner = small[:4, 0].reshape(-1)
+        narrow = small[4:13, 0]
+        grad_rel_table = jnp.transpose(small[13, :heads, : rel_table.shape[0]])
     else:
         totals = []
-        for entry in (*results[6:8], *later):
+        for entry in (*results[6:8], *later[2:6]):
             share = lax.psum_scatter(entry, "shard", scatter_dimension=0, tiled=True)
             totals.append(lax.psum(share, "dp").astype(f32))
         grad_w_outer, grad_w_inner, grad_w_query, grad_w_key, grad_w_value, grad_w_out = totals
-
-    bucket_grads = jnp.transpose(jnp.sum(tallies, axis=-1)).reshape(1, -1)
-    small = jnp.concatenate(
-        [
-            small_first[:9],
-            small_second[:4],
-            jnp.pad(bucket_grads, ((0, 0), (0, model - bucket_grads.shape[1]))),
-        ],
-        axis=0,
-    )
-    small = lax.psum(small, ("shard", "dp"))
-    grad_b_inner = lax.dynamic_slice_in_dim(small[:4].reshape(-1), shard * b_inner.shape[0], b_inner.shape[0])
-    narrow = lax.dynamic_slice_in_dim(small[4:13], shard * part_width, part_width, axis=1)
-    grad_rel_table = lax.dynamic_slice_in_dim(
-        small[13, : bucket_total * heads].reshape(bucket_total, heads),
-        shard * rel_table.shape[0],
-        rel_table.shape[0],
-        axis=0,
-    )
+        tree_grad = scatter_blocks(later[6], routes_out[0])
+        small = lax.psum(later[7], ("shard", "dp"))
+        grad_b_inner = lax.dynamic_slice_in_dim(small[:4].reshape(-1), shard * b_inner.shape[0], b_inner.shape[0])
+        narrow = lax.dynamic_slice_in_dim(small[4:13], shard * part_width, part_width, axis=1)
+        grad_rel_table = lax.dynamic_slice_in_dim(
+            jnp.transpose(small[16 : 16 + heads, :bucket_total]), shard * rel_table.shape[0], rel_table.shape[0], axis=0
+        )
+    halves = tree_grad.astype(f32).reshape(2, micro_count, run, half)
+    grad_content = d_content + jnp.concatenate([halves[0], halves[1]], axis=-1)
     return (
         out_content,
         out_query,

time: 547 us -> 312 us (0.57); the launches traced: 539 us -> 311 us
  starting transfers between devices: 150 us -> 65.9 us
  blocking collectives: 45.9 us -> 0 us
  waiting for transfers between devices: 157 us -> 127 us
  local copies, waits for them, and re-layouts: 37.2 us -> 15.7 us
  other arithmetic: 36.7 us -> 15.8 us
  Pallas kernels: 103 us -> 84.5 us
  between operations: 9.09 us -> 1.98 us
    ppermute x123 -> x54, starting transfers between devices: 149 us -> 64.1 us  [the longest x50 63.1 us: send(): return lax.ppermute(inputs, 'dp', [(i, i ^ 1 << bit) for i in range(count)])]
    psum x1 -> x0, blocking collectives: 45.9 us -> none  [shards(): small = lax.psum(small, ('shard', 'dp'))]
    ppermute x123 -> x54, waiting for transfers between devices: 157 us -> 127 us  [the longest x50 127 us: send(): return lax.ppermute(inputs, 'dp', [(i, i ^ 1 << bit) for i in range(count)])]
    pallas_call x5 -> x4, Pallas kernels: 51.8 us -> 33.6 us  [the longest x1 14.9 us: shards(): pl.pallas_call(functools.partial(weights_kernel, pieces, run, slots), out...]
    concatenate x41 -> x28, other arithmetic: 18.3 us -> 2.9 us  [the longest x1 1.18 us: shards(): jnp.concatenate([content.reshape(content_rows, model), fact_rows], axis=0)]
    another operation x2 -> x3, local copies, waits for them, and re-layouts: 8.28 us -> 0.81 us  [the longest x1 0.61 us: shards(): grad_b_inner = small[:4, 0].reshape(-1)]
    slice x57 -> x30, local copies, waits for them, and re-layouts: 10.4 us -> 3.13 us  [the longest x2 1.37 us: shards(): grad_rel_table = jnp.transpose(small[13, :heads, :rel_table.shape[0]])]
  transfers between devices with their start and end apart: 130 -> 61, of which waited for: 55 -> 32; matrix products, arithmetic and copies ran while one was open for 11% -> 5% of each run, Pallas kernels for 8% -> 13%
where the time goes in v2:
time: 312 us; the launch traced here: 311 us
  waiting for transfers between devices  127 us (41%)
  Pallas kernels  84.5 us (27%)
  starting transfers between devices  65.9 us (21%)
  other arithmetic  15.8 us (5%)
  local copies, waits for them, and re-layouts  15.7 us (5%)
    ppermute x50, waiting for transfers between devices, send(): return lax.ppermute(inputs, 'dp', [(i, i ^ 1 << bit) for i in range(count)])  127 us
    ppermute x50, starting transfers between devices, send(): return lax.ppermute(inputs, 'dp', [(i, i ^ 1 << bit) for i in range(count)])  63.1 us
    pallas_call x1, Pallas kernels, shards(): pl.pallas_call(functools.partial(feed_kernel, pieces, run), out_shape=[sh...  21.4 us
    pallas_call x1, Pallas kernels, shards(): pl.pallas_call(functools.partial(weights_kernel, pieces, run, slots), out...  14.9 us
    pallas_call x1, Pallas kernels, shards(): pl.pallas_call(functools.partial(back_kernel, run, slots), grid=(pairs, m...  14.3 us
    pallas_call x1, Pallas kernels, shards(): pl.pallas_call(functools.partial(attend_kernel, run, slots), grid=(pairs,...  11.6 us
    pallas_call x1, Pallas kernels, shards(): pl.pallas_call(feed_spread_kernel, out_shape=(shape(w_outer.shape, f32),...  7.36 us
    unnamed x95, local copies, waits for them, and re-layouts  6.83 us
  transfers between devices with their start and end apart: 61, of which 32 were waited for; matrix products, arithmetic and copies ran while one was open for 5% of the time, Pallas kernels for 13%

profile of v2, /device:TPU:0, one launch (start us, length us, event | category | flops | bytes accessed | tf_op | source)
XLA Modules:
  0.0 310.5 jit_solution(6377584116225956842)
XLA Ops:
  4.2 4.0 %collective-permute-start.1 = (bf16[1,1,1,1,144,768]{5,4,3,2,1,0:T(8,128)(2,1)S(1)}, bf16[1,1,1,1,144,768]{5,4,3,2,1,0:T(8,128)(2,1)S(1)}, u32[]{:S(2)}, u32[]{:S(2)}) collective-permute-start(bf16[1,1,1,1,144,768]{5,4,3,2,1,0:T(8,128)(2,1)S(1)} %bitcast.79), channel_id=1, source_target_pairs={{0,8},{1,9},{2,10},{3,11},{4,12},{5,13},{6,14},{7,15},{8,0},{9,1},... | collective-permute-start | bytes 663560 | tf_op jit(solution)/shard_map/ppermute | solution.py:625
  8.2 10.4 %collective-permute-done.1 = bf16[1,1,1,1,144,768]{5,4,3,2,1,0:T(8,128)(2,1)S(1)} collective-permute-done((bf16[1,1,1,1,144,768]{5,4,3,2,1,0:T(8,128)(2,1)S(1)}, bf16[1,1,1,1,144,768]{5,4,3,2,1,0:T(8,128)(2,1)S(1)}, u32[]{:S(2)}, u32[]{:S(2)}) %collective-permute-start.1) | collective-permute-done | bytes 221216 | tf_op jit(solution)/shard_map/ppermute | solution.py:625
  30.3 6.9 %collective-permute-done.10 = bf16[2,1,1,2,128,256]{5,4,3,2,1,0:T(8,128)(2,1)S(1)} collective-permute-done((bf16[2,1,1,2,128,256]{5,4,3,2,1,0:T(8,128)(2,1)S(1)}, bf16[2,1,1,2,128,256]{5,4,3,2,1,0:T(8,128)(2,1)S(1)}, u32[]{:S(2)}, u32[]{:S(2)}) %collective-permute-start.10) | collective-permute-done | bytes 262176 | tf_op jit(solution)/shard_map/ppermute | solution.py:625
  49.9 3.6 %query_projection.1 = (bf16[256,768]{1,0:T(8,128)(2,1)}, bf16[256,768]{1,0:T(8,128)(2,1)}) custom-call(s32[2]{0:T(128)} %pad_add_fusion.1.scalars, bf16[256,768]{1,0:T(8,128)(2,1)} %bitcast.85, f32[16,768]{1,0:T(8,128)} %bitcast.90, bf16[384,768]{1,0:T(8,128)(2,1)} %refs_0_.2, bf16[384,768]{1,0:T(8,128)(2,1)} %copy-done.37), custom_call_target="tpu_custom_call" | custom-call | flops 4000000000 | tf_op jit(solution)/shard_map/query_projection/pallas_call | solution.py:861
  53.6 4.9 %collective-permute-done.14.refs_3_ = bf16[2,2,1,2,128,256]{5,4,3,2,1,0:T(8,128)(2,1)S(1)} collective-permute-done((bf16[2,2,1,2,128,256]{5,4,3,2,1,0:T(8,128)(2,1)S(1)}, bf16[2,2,1,2,128,256]{5,4,3,2,1,0:T(8,128)(2,1)S(1)}, u32[]{:S(2)}, u32[]{:S(2)}) %collective-permute-start.14) | collective-permute-done | bytes 524320 | tf_op jit(solution)/shard_map/ppermute | solution.py:625
  61.9 6.4 %path_keys.1 = (bf16[2,384,768]{2,1,0:T(8,128)(2,1)}, bf16[768,768]{1,0:T(8,128)(2,1)}, bf16[768,768]{1,0:T(8,128)(2,1)}, s32[12]{0:T(128)}) custom-call(s32[12]{0:T(128)} %pad_add_fusion.scalars, bf16[2,2,2,1,144,256]{5,4,3,2,1,0:T(8,128)(2,1)} %copy-done.8, bf16[2,2,2,1,144,256]{5,4,3,2,1,0:T(8,128)(2,1)} %copy-done.41, ...), custom_call_target="tpu_custom_call" | custom-call | flops 6000000000 | tf_op jit(solution)/shard_map/path_keys/pallas_call | solution.py:872
  68.4 11.6 %attend.1 = (bf16[12,256,384]{2,1,0:T(8,128)(2,1)}, f32[256,768]{1,0:T(8,128)}) custom-call(s32[12]{0:T(128)} %pad_add_fusion.scalars, f32[16,12]{1,0:T(8,128)} %reshape_squeeze.6.table, bf16[256,768]{1,0:T(8,128)(2,1)} %get-tuple-element.135.query_low, bf16[256,768]{1,0:T(8,128)(2,1)} %get-tuple-element.136.query_segment, ...), custom_call_target="tpu_custom_call" | custom-call | flops 11000000512 | tf_op jit(solution)/shard_map/attend/pallas_call | solution.py:899
  80.0 21.4 %feed_forward.1 = (bf16[2,64,768]{2,1,0:T(8,128)(2,1)}, bf16[2,64,768]{2,1,0:T(8,128)(2,1)}, f32[256,768]{1,0:T(8,128)}, bf16[256,768]{1,0:T(8,128)(2,1)}, bf16[...) custom-call(s32[12]{0:T(128)} %pad_add_fusion.scalars, ...), custom_call_target="tpu_custom_call" | custom-call | flops 20999999488 | tf_op jit(solution)/shard_map/feed_forward/pallas_call | solution.py:922
  102.0 14.3 %attend_back.1 = (bf16[256,768]{1,0:T(8,128)(2,1)}, bf16[768,768]{1,0:T(8,128)(2,1)}, bf16[768,768]{1,0:T(8,128)(2,1)}, f32[8,768]{1,0:T(8,128)}, f32[12,16,384]{2,1,0:T(8,128)}) custom-call(s32[12]{0:T(128)} %pad_add_fusion.scalars, bf16[256,768]{1,0:T(8,128)(2,1)} %get-tuple-element.135.query_low, bf16[256,768]{1,0:T(8,128)(2,1)} %get-tuple-element.136.query_segment, ...), custom_call_target="tpu_custom_call" | custom-call | flops 14000000000 | tf_op jit(solution)/shard_map/attend_back/pallas_call | solution.py:956
  122.8 14.9 %weight_gradients.1 = (f32[2,64,768]{2,1,0:T(8,128)}, f32[2,64,768]{2,1,0:T(8,128)}, bf16[2,2,2,464,384]{4,3,2,1,0:T(8,128)(2,1)}, bf16[2,2,2,464,384]{4,3,2,1,0...) custom-call(s32[12]{0:T(128)} %pad_add_fusion.scalars, ...), custom_call_target="tpu_custom_call" | custom-call | flops 15000000512 | tf_op jit(solution)/shard_map/weight_gradients/pallas_call | solution.py:1008
  148.7 5.5 %collective-permute-done.22 = bf16[2,2,1,1,128,384]{5,4,2,1,0,3:T(8,128)(2,1)S(1)} collective-permute-done((bf16[2,2,1,1,128,384]{5,4,2,1,0,3:T(8,128)(2,1)S(1)}, bf16[2,2,1,1,128,384]{5,4,2,1,0,3:T(8,128)(2,1)S(1)}, u32[]{:S(2)}, u32[]{:S(2)}) %collective-permute-start.22) | collective-permute-done | bytes 393248 | tf_op jit(solution)/shard_map/ppermute | solution.py:625
  161.7 3.5 %collective-permute-done.28 = bf16[2,1,1,1,128,384]{5,4,3,1,0,2:T(8,128)(2,1)S(1)} collective-permute-done((bf16[2,1,1,1,128,384]{5,4,3,1,0,2:T(8,128)(2,1)S(1)}, bf16[2,1,1,1,128,384]{5,4,3,1,0,2:T(8,128)(2,1)S(1)}, u32[]{:S(2)}, u32[]{:S(2)}) %collective-permute-start.28) | collective-permute-done | bytes 196640 | tf_op jit(solution)/shard_map/ppermute | solution.py:625
  172.3 8.3 %collective-permute-done.33 = bf16[1,1,1,1,384,384]{5,4,3,2,1,0:T(8,128)(2,1)S(1)} collective-permute-done((bf16[1,1,1,1,384,384]{5,4,3,2,1,0:T(8,128)(2,1)S(1)}, bf16[1,1,1,1,384,384]{5,4,3,2,1,0:T(8,128)(2,1)S(1)}, u32[]{:S(2)}, u32[]{:S(2)}) %collective-permute-start.33) | collective-permute-done | bytes 294944 | tf_op jit(solution)/shard_map/ppermute | solution.py:625
  180.9 17.7 %collective-permute-done.37 = bf16[1,1,1,1,384,384]{5,4,3,2,1,0:T(8,128)(2,1)S(1)} collective-permute-done((bf16[1,1,1,1,384,384]{5,4,3,2,1,0:T(8,128)(2,1)S(1)}, bf16[1,1,1,1,384,384]{5,4,3,2,1,0:T(8,128)(2,1)S(1)}, u32[]{:S(2)}, u32[]{:S(2)}) %collective-permute-start.37) | collective-permute-done | bytes 294944 | tf_op jit(solution)/shard_map/ppermute | solution.py:625
  206.2 3.5 %collective-permute-done.43 = bf16[2,1,1,1,128,384]{5,4,3,2,1,0:T(8,128)(2,1)S(1)} collective-permute-done((bf16[2,1,1,1,128,384]{5,4,3,2,1,0:T(8,128)(2,1)S(1)}, bf16[2,1,1,1,128,384]{5,4,3,2,1,0:T(8,128)(2,1)S(1)}, u32[]{:S(2)}, u32[]{:S(2)}) %collective-permute-start.43) | collective-permute-done | bytes 196640 | tf_op jit(solution)/shard_map/ppermute | solution.py:625
  216.1 10.6 %collective-permute-done.35 = bf16[2,1,1,2,160,384]{5,4,3,2,1,0:T(8,128)(2,1)S(1)} collective-permute-done((bf16[2,1,1,2,160,384]{5,4,3,2,1,0:T(8,128)(2,1)S(1)}, bf16[2,1,1,2,160,384]{5,4,3,2,1,0:T(8,128)(2,1)S(1)}, u32[]{:S(2)}, u32[]{:S(2)}) %collective-permute-start.35) | collective-permute-done | bytes 491552 | tf_op jit(solution)/shard_map/ppermute | solution.py:625
  233.4 10.9 %collective-permute-done.38 = bf16[2,1,1,1,160,384]{5,4,3,2,1,0:T(8,128)(2,1)S(1)} collective-permute-done((bf16[2,1,1,1,160,384]{5,4,3,2,1,0:T(8,128)(2,1)S(1)}, bf16[2,1,1,1,160,384]{5,4,3,2,1,0:T(8,128)(2,1)S(1)}, u32[]{:S(2)}, u32[]{:S(2)}) %collective-permute-start.38) | collective-permute-done | bytes 245792 | tf_op jit(solution)/shard_map/ppermute | solution.py:625
  244.5 4.1 %collective-permute-start.44 = (bf16[1,1,1,1,464,384]{5,4,3,2,1,0:T(8,128)(2,1)S(1)}, bf16[1,1,1,1,464,384]{5,4,3,2,1,0:T(8,128)(2,1)S(1)}, u32[]{:S(2)}, u32[]{:S(2)}) collective-permute-start(bf16[1,1,1,1,464,384]{5,4,3,2,1,0:T(8,128)(2,1)S(1)} %pad_maximum_fusion.15), channel_id=1, source_target_pairs={{0,8},{1,9},{2,10},{3,11},{4,12},{5,13},{6,14},{7,15},{8,0},{9,1},... | collective-permute-start | bytes 1069064 | tf_op jit(solution)/shard_map/ppermute | solution.py:625
  254.7 5.0 %collective-permute-done.44 = bf16[1,1,1,1,464,384]{5,4,3,2,1,0:T(8,128)(2,1)S(1)} collective-permute-done((bf16[1,1,1,1,464,384]{5,4,3,2,1,0:T(8,128)(2,1)S(1)}, bf16[1,1,1,1,464,384]{5,4,3,2,1,0:T(8,128)(2,1)S(1)}, u32[]{:S(2)}, u32[]{:S(2)}) %collective-permute-start.44) | collective-permute-done | bytes 356384 | tf_op jit(solution)/shard_map/ppermute | solution.py:625
  260.2 6.8 %collective-permute-done.48 = bf16[1,1,1,1,208,384]{5,4,3,2,1,0:T(8,128)(2,1)S(1)} collective-permute-done((bf16[1,1,1,1,208,384]{5,4,3,2,1,0:T(8,128)(2,1)S(1)}, bf16[1,1,1,1,208,384]{5,4,3,2,1,0:T(8,128)(2,1)S(1)}, u32[]{:S(2)}, u32[]{:S(2)}) %collective-permute-start.48) | collective-permute-done | bytes 159776 | tf_op jit(solution)/shard_map/ppermute | solution.py:625
  272.4 3.5 %collective-permute-start.51 = (bf16[2,1,1,1,80,384]{5,4,3,2,1,0:T(8,128)(2,1)S(1)}, bf16[2,1,1,1,80,384]{5,4,3,2,1,0:T(8,128)(2,1)S(1)}, u32[]{:S(2)}, u32[]{:S(2)}) collective-permute-start(bf16[2,1,1,1,80,384]{5,4,3,2,1,0:T(8,128)(2,1)S(1)} %pad_maximum_fusion.27), channel_id=1, source_target_pairs={{0,2},{1,3},{2,0},{3,1},{4,6},{5,7},{6,4},{7,5},{8,10},{9,11},{10,... | collective-permute-start | bytes 368648 | tf_op jit(solution)/shard_map/ppermute | solution.py:625
  275.9 4.2 %collective-permute-done.51 = bf16[2,1,1,1,80,384]{5,4,3,2,1,0:T(8,128)(2,1)S(1)} collective-permute-done((bf16[2,1,1,1,80,384]{5,4,3,2,1,0:T(8,128)(2,1)S(1)}, bf16[2,1,1,1,80,384]{5,4,3,2,1,0:T(8,128)(2,1)S(1)}, u32[]{:S(2)}, u32[]{:S(2)}) %collective-permute-start.51) | collective-permute-done | bytes 122912 | tf_op jit(solution)/shard_map/ppermute | solution.py:625
  291.1 7.4 %feed_spread.1 = (f32[1536,768]{1,0:T(8,128)}, f32[384,3072]{1,0:T(8,128)}) custom-call(s32[2]{0:T(128)} %pad_add_fusion.1.scalars, bf16[2,2,2,1,128,384]{5,4,3,2,1,0:T(8,128)(2,1)} %copy-done.4, bf16[2,2,2,1,128,384]{5,4,3,2,1,0:T(8,128)(2,1)} %copy-done.34, bf16[2,2,1,2,128,384]{5,4,3,2,1,0:T(8,128)(2,1)} %copy-done.5, ...), custom_call_target="tpu_custom_call" | custom-call | flops 7000000000 | tf_op jit(solution)/shard_map/feed_spread/pallas_call | solution.py:1066
  300.1 4.9 %later_spread.1 = (f32[384,768]{1,0:T(8,128)}, f32[384,768]{1,0:T(8,128)}, f32[384,768]{1,0:T(8,128)}, f32[384,768]{1,0:T(8,128)}, f32[16,16,384]{2,1,0:T(8,128)}) custom-call(s32[2]{0:T(128)} %pad_add_fusion.1.scalars, bf16[2,2,2,1,64,384]{5,4,3,2,1,0:T(8,128)(2,1)} %copy-done.12, bf16[2,2,2,1,64,384]{5,4,3,2,1,0:T(8,128)(2,1)} %copy-done.45, ...), custom_call_target="tpu_custom_call" | custom-call | flops 4000000000 | tf_op jit(solution)/shard_map/later_spread/pallas_call | solution.py:1079
  (332 shorter events, 114.2 us)
Async XLA Ops:
  3.6 15.1 %collective-permute-start.2 = (bf16[384,768]{1,0:T(8,128)(2,1)}, bf16[384,768]{1,0:T(8,128)(2,1)S(1)}, u32[]{:S(2)}, u32[]{:S(2)}) collective-permute-start(bf16[384,768]{1,0:T(8,128)(2,1)} %refs_0_.2), channel_id=1, source_target_pairs={{0,16},{16,0},{1,17},{17,1},{2,18},{18,2},{3,19},{19,3},{4,20},{20... | collective-permute-start | bytes 1769480 | tf_op jit(solution)/shard_map/ppermute | solution.py:782
  4.1 14.6 %collective-permute-start.3 = (bf16[384,768]{1,0:T(8,128)(2,1)}, bf16[384,768]{1,0:T(8,128)(2,1)S(1)}, u32[]{:S(2)}, u32[]{:S(2)}) collective-permute-start(bf16[384,768]{1,0:T(8,128)(2,1)} %refs_2_.1), channel_id=1, source_target_pairs={{0,16},{16,0},{1,17},{17,1},{2,18},{18,2},{3,19},{19,3},{4,20},{20... | collective-permute-start | bytes 1769480 | tf_op jit(solution)/shard_map/ppermute | solution.py:782
  4.2 14.4 %collective-permute-start.1 = (bf16[1,1,1,1,144,768]{5,4,3,2,1,0:T(8,128)(2,1)S(1)}, bf16[1,1,1,1,144,768]{5,4,3,2,1,0:T(8,128)(2,1)S(1)}, u32[]{:S(2)}, u32[]{:S(2)}) collective-permute-start(bf16[1,1,1,1,144,768]{5,4,3,2,1,0:T(8,128)(2,1)S(1)} %bitcast.79), channel_id=1, source_target_pairs={{0,8},{1,9},{2,10},{3,11},{4,12},{5,13},{6,14},{7,15},{8,0},{9,1},... | collective-permute-start | bytes 663560 | tf_op jit(solution)/shard_map/ppermute | solution.py:625
  40.1 21.0 %collective-permute-start.16 = (bf16[1536,768]{1,0:T(8,128)(2,1)}, bf16[1536,768]{1,0:T(8,128)(2,1)}, u32[]{:S(2)}, u32[]{:S(2)}) collective-permute-start(bf16[1536,768]{1,0:T(8,128)(2,1)} %refs_4_), channel_id=1, source_target_pairs={{0,16},{16,0},{1,17},{17,1},{2,18},{18,2},{3,19},{19,3},{4,20},{20... | collective-permute-start | bytes 7077896 | tf_op jit(solution)/shard_map/ppermute | solution.py:782
  46.4 14.7 %collective-permute-start.13 = (bf16[2,2,2,1,144,256]{5,4,3,2,1,0:T(8,128)(2,1)S(1)}, bf16[2,2,2,1,144,256]{5,4,3,2,1,0:T(8,128)(2,1)S(1)}, u32[]{:S(2)}, u32[]{:S(2)}) collective-permute-start(bf16[2,2,2,1,144,256]{5,4,3,2,1,0:T(8,128)(2,1)S(1)} %pad_maximum_fusion.3.refs_0_), channel_id=1, source_target_pairs={{0,1},{1,0},{2,3},{3,2},{4,5},{5,4},{6,7},{7,6},{8,9},{9,8},{10,11... | collective-permute-start | bytes 1769480 | tf_op jit(solution)/shard_map/ppermute | solution.py:625
  101.4 14.9 %collective-permute-start.17 = (bf16[2,2,2,384,384]{4,3,2,1,0:T(8,128)(2,1)}, bf16[2,2,2,384,384]{4,3,2,1,0:T(8,128)(2,1)}, u32[]{:S(2)}, u32[]{:S(2)}) collective-permute-start(bf16[2,2,2,384,384]{4,3,2,1,0:T(8,128)(2,1)} %get-tuple-element.170), channel_id=1, source_target_pairs={{0,16},{16,0},{1,17},{17,1},{2,18},{18,2},{3,19},{19,3},{4,20},{20... | collective-permute-start | bytes 7077896 | tf_op jit(solution)/shard_map/ppermute | solution.py:954
  101.5 17.6 %collective-permute-start.18 = (bf16[2,2,2,384,384]{4,3,2,1,0:T(8,128)(2,1)}, bf16[2,2,2,384,384]{4,3,2,1,0:T(8,128)(2,1)}, u32[]{:S(2)}, u32[]{:S(2)}) collective-permute-start(bf16[2,2,2,384,384]{4,3,2,1,0:T(8,128)(2,1)} %get-tuple-element.171), channel_id=1, source_target_pairs={{0,16},{16,0},{1,17},{17,1},{2,18},{18,2},{3,19},{19,3},{4,20},{20... | collective-permute-start | bytes 7077896 | tf_op jit(solution)/shard_map/ppermute | solution.py:954
  119.1 19.8 %collective-permute-start.19 = (bf16[2,2,2,1,128,384]{5,4,2,1,0,3:T(8,128)(2,1)}, bf16[2,2,2,1,128,384]{5,4,2,1,0,3:T(8,128)(2,1)}, u32[]{:S(2)}, u32[]{:S(2)}) collective-permute-start(bf16[2,2,2,1,128,384]{5,4,2,1,0,3:T(8,128)(2,1)} %get-tuple-element.186), channel_id=1, source_target_pairs={{0,1},{1,0},{2,3},{3,2},{4,5},{5,4},{6,7},{7,6},{8,9},{9,8},{10,11... | collective-permute-start | bytes 2359304 | tf_op jit(solution)/shard_map/ppermute | solution.py:625
  120.6 19.9 %collective-permute-start.20 = (bf16[2,2,1,2,128,384]{5,4,3,1,0,2:T(8,128)(2,1)S(1)}, bf16[2,2,1,2,128,384]{5,4,3,1,0,2:T(8,128)(2,1)}, u32[]{:S(2)}, u32[]{:S(2)}) collective-permute-start(bf16[2,2,1,2,128,384]{5,4,3,1,0,2:T(8,128)(2,1)S(1)} %get-tuple-element.187), channel_id=1, source_target_pairs={{0,2},{1,3},{2,0},{3,1},{4,6},{5,7},{6,4},{7,5},{8,10},{9,11},{10,... | collective-permute-start | bytes 2359304 | tf_op jit(solution)/shard_map/ppermute | solution.py:625
  122.1 20.0 %collective-permute-start.21 = (bf16[2,1,2,2,128,384]{5,4,3,2,1,0:T(8,128)(2,1)S(1)}, bf16[2,1,2,2,128,384]{5,4,3,2,1,0:T(8,128)(2,1)}, u32[]{:S(2)}, u32[]{:S(2)}) collective-permute-start(bf16[2,1,2,2,128,384]{5,4,3,2,1,0:T(8,128)(2,1)S(1)} %get-tuple-element.188), channel_id=1, source_target_pairs={{0,4},{1,5},{2,6},{3,7},{4,0},{5,1},{6,2},{7,3},{8,12},{9,13},{10,... | collective-permute-start | bytes 2359304 | tf_op jit(solution)/shard_map/ppermute | solution.py:625
  169.5 30.7 %collective-permute-start.32 = (bf16[2,1,2,2,144,384]{5,4,3,2,1,0:T(8,128)(2,1)S(1)}, bf16[2,1,2,2,144,384]{5,4,3,2,1,0:T(8,128)(2,1)S(1)}, u32[]{:S(2)}, u32[]{:S(2)}) collective-permute-start(bf16[2,1,2,2,144,384]{5,4,3,2,1,0:T(8,128)(2,1)S(1)} %maximum_bitcast_fusion.4), channel_id=1, source_target_pairs={{0,4},{1,5},{2,6},{3,7},{4,0},{5,1},{6,2},{7,3},{8,12},{9,13},{10,... | collective-permute-start | bytes 2654216 | tf_op jit(solution)/shard_map/ppermute | solution.py:625
  171.3 29.2 %collective-permute-start.30 = (bf16[2,2,2,1,160,384]{5,4,3,2,1,0:T(8,128)(2,1)S(1)}, bf16[2,2,2,1,160,384]{5,4,3,2,1,0:T(8,128)(2,1)S(1)}, u32[]{:S(2)}, u32[]{:S(2)}) collective-permute-start(bf16[2,2,2,1,160,384]{5,4,3,2,1,0:T(8,128)(2,1)S(1)} %maximum_bitcast_fusion.1), channel_id=1, source_target_pairs={{0,1},{1,0},{2,3},{3,2},{4,5},{5,4},{6,7},{7,6},{8,9},{9,8},{10,11... | collective-permute-start | bytes 2949128 | tf_op jit(solution)/shard_map/ppermute | solution.py:625
  171.8 29.0 %collective-permute-start.31 = (bf16[2,2,1,2,160,384]{5,4,3,2,1,0:T(8,128)(2,1)S(1)}, bf16[2,2,1,2,160,384]{5,4,3,2,1,0:T(8,128)(2,1)S(1)}, u32[]{:S(2)}, u32[]{:S(2)}) collective-permute-start(bf16[2,2,1,2,160,384]{5,4,3,2,1,0:T(8,128)(2,1)S(1)} %maximum_bitcast_fusion.2), channel_id=1, source_target_pairs={{0,2},{1,3},{2,0},{3,1},{4,6},{5,7},{6,4},{7,5},{8,10},{9,11},{10,... | collective-permute-start | bytes 2949128 | tf_op jit(solution)/shard_map/ppermute | solution.py:625
  180.7 17.9 %collective-permute-start.37 = (bf16[1,1,1,1,384,384]{5,4,3,2,1,0:T(8,128)(2,1)S(1)}, bf16[1,1,1,1,384,384]{5,4,3,2,1,0:T(8,128)(2,1)S(1)}, u32[]{:S(2)}, u32[]{:S(2)}) collective-permute-start(bf16[1,1,1,1,384,384]{5,4,3,2,1,0:T(8,128)(2,1)S(1)} %pad_maximum_fusion.18), channel_id=1, source_target_pairs={{0,8},{1,9},{2,10},{3,11},{4,12},{5,13},{6,14},{7,15},{8,0},{9,1},... | collective-permute-start | bytes 884744 | tf_op jit(solution)/shard_map/ppermute | solution.py:625
  203.9 23.0 %collective-permute-start.42 = (bf16[2,1,1,1,128,384]{5,4,3,2,1,0:T(8,128)(2,1)S(1)}, bf16[2,1,1,1,128,384]{5,4,3,2,1,0:T(8,128)(2,1)S(1)}, u32[]{:S(2)}, u32[]{:S(2)}) collective-permute-start(bf16[2,1,1,1,128,384]{5,4,3,2,1,0:T(8,128)(2,1)S(1)} %get-tuple-element.259), channel_id=1, source_target_pairs={{0,1},{1,0},{2,3},{3,2},{4,5},{5,4},{6,7},{7,6},{8,9},{9,8},{10,11... | collective-permute-start | bytes 589832 | tf_op jit(solution)/shard_map/ppermute | solution.py:625
  205.4 23.6 %collective-permute-start.41 = (bf16[2,1,1,1,128,384]{5,4,3,2,1,0:T(8,128)(2,1)S(1)}, bf16[2,1,1,1,128,384]{5,4,3,2,1,0:T(8,128)(2,1)S(1)}, u32[]{:S(2)}, u32[]{:S(2)}) collective-permute-start(bf16[2,1,1,1,128,384]{5,4,3,2,1,0:T(8,128)(2,1)S(1)} %get-tuple-element.260), channel_id=1, source_target_pairs={{0,4},{1,5},{2,6},{3,7},{4,0},{5,1},{6,2},{7,3},{8,12},{9,13},{10,... | collective-permute-start | bytes 589832 | tf_op jit(solution)/shard_map/ppermute | solution.py:625
  209.8 42.2 %collective-permute-start.47 = (bf16[2,1,2,1,128,384]{5,4,3,2,1,0:T(8,128)(2,1)S(1)}, bf16[2,1,2,1,128,384]{5,4,3,2,1,0:T(8,128)(2,1)S(1)}, u32[]{:S(2)}, u32[]{:S(2)}) collective-permute-start(bf16[2,1,2,1,128,384]{5,4,3,2,1,0:T(8,128)(2,1)S(1)} %pad_maximum_fusion.12), channel_id=1, source_target_pairs={{0,1},{1,0},{2,3},{3,2},{4,5},{5,4},{6,7},{7,6},{8,9},{9,8},{10,11... | collective-permute-start | bytes 1179656 | tf_op jit(solution)/shard_map/ppermute | solution.py:625
  227.0 21.9 %collective-permute-start.46 = (bf16[2,1,1,2,128,384]{5,4,3,2,1,0:T(8,128)(2,1)S(1)}, bf16[2,1,1,2,128,384]{5,4,3,2,1,0:T(8,128)(2,1)S(1)}, u32[]{:S(2)}, u32[]{:S(2)}) collective-permute-start(bf16[2,1,1,2,128,384]{5,4,3,2,1,0:T(8,128)(2,1)S(1)} %pad_maximum_fusion.11), channel_id=1, source_target_pairs={{0,4},{1,5},{2,6},{3,7},{4,0},{5,1},{6,2},{7,3},{8,12},{9,13},{10,... | collective-permute-start | bytes 1179656 | tf_op jit(solution)/shard_map/ppermute | solution.py:625
  228.2 16.1 %collective-permute-start.38 = (bf16[2,1,1,1,160,384]{5,4,3,2,1,0:T(8,128)(2,1)S(1)}, bf16[2,1,1,1,160,384]{5,4,3,2,1,0:T(8,128)(2,1)S(1)}, u32[]{:S(2)}, u32[]{:S(2)}) collective-permute-start(bf16[2,1,1,1,160,384]{5,4,3,2,1,0:T(8,128)(2,1)S(1)} %slice.481), channel_id=1, source_target_pairs={{0,4},{1,5},{2,6},{3,7},{4,0},{5,1},{6,2},{7,3},{8,12},{9,13},{10,... | collective-permute-start | bytes 737288 | tf_op jit(solution)/shard_map/ppermute | solution.py:625
  229.1 19.5 %collective-permute-start.45 = (bf16[2,2,1,1,128,384]{5,4,3,2,1,0:T(8,128)(2,1)S(1)}, bf16[2,2,1,1,128,384]{5,4,3,2,1,0:T(8,128)(2,1)S(1)}, u32[]{:S(2)}, u32[]{:S(2)}) collective-permute-start(bf16[2,2,1,1,128,384]{5,4,3,2,1,0:T(8,128)(2,1)S(1)} %pad_maximum_fusion.10), channel_id=1, source_target_pairs={{0,2},{1,3},{2,0},{3,1},{4,6},{5,7},{6,4},{7,5},{8,10},{9,11},{10,... | collective-permute-start | bytes 1179656 | tf_op jit(solution)/shard_map/ppermute | solution.py:625
  244.5 15.2 %collective-permute-start.44 = (bf16[1,1,1,1,464,384]{5,4,3,2,1,0:T(8,128)(2,1)S(1)}, bf16[1,1,1,1,464,384]{5,4,3,2,1,0:T(8,128)(2,1)S(1)}, u32[]{:S(2)}, u32[]{:S(2)}) collective-permute-start(bf16[1,1,1,1,464,384]{5,4,3,2,1,0:T(8,128)(2,1)S(1)} %pad_maximum_fusion.15), channel_id=1, source_target_pairs={{0,8},{1,9},{2,10},{3,11},{4,12},{5,13},{6,14},{7,15},{8,0},{9,1},... | collective-permute-start | bytes 1069064 | tf_op jit(solution)/shard_map/ppermute | solution.py:625
  248.7 31.4 %collective-permute-start.52 = (bf16[2,2,2,1,128,384]{5,4,3,2,1,0:T(8,128)(2,1)S(1)}, bf16[2,2,2,1,128,384]{5,4,3,2,1,0:T(8,128)(2,1)S(1)}, u32[]{:S(2)}, u32[]{:S(2)}) collective-permute-start(bf16[2,2,2,1,128,384]{5,4,3,2,1,0:T(8,128)(2,1)S(1)} %pad_maximum_fusion.refs_0_), channel_id=1, source_target_pairs={{0,1},{1,0},{2,3},{3,2},{4,5},{5,4},{6,7},{7,6},{8,9},{9,8},{10,11... | collective-permute-start | bytes 2359304 | tf_op jit(solution)/shard_map/ppermute | solution.py:625
  248.9 31.2 %collective-permute-start.53 = (bf16[2,2,1,2,128,384]{5,4,3,2,1,0:T(8,128)(2,1)S(1)}, bf16[2,2,1,2,128,384]{5,4,3,2,1,0:T(8,128)(2,1)S(1)}, u32[]{:S(2)}, u32[]{:S(2)}) collective-permute-start(bf16[2,2,1,2,128,384]{5,4,3,2,1,0:T(8,128)(2,1)S(1)} %pad_maximum_fusion.1.refs_2_), channel_id=1, source_target_pairs={{0,2},{1,3},{2,0},{3,1},{4,6},{5,7},{6,4},{7,5},{8,10},{9,11},{10,... | collective-permute-start | bytes 2359304 | tf_op jit(solution)/shard_map/ppermute | solution.py:625
  252.1 28.1 %collective-permute-start.54 = (bf16[2,1,2,2,128,384]{5,4,3,2,1,0:T(8,128)(2,1)S(1)}, bf16[2,1,2,2,128,384]{5,4,3,2,1,0:T(8,128)(2,1)S(1)}, u32[]{:S(2)}, u32[]{:S(2)}) collective-permute-start(bf16[2,1,2,2,128,384]{5,4,3,2,1,0:T(8,128)(2,1)S(1)} %pad_maximum_fusion.2.refs_4_), channel_id=1, source_target_pairs={{0,4},{1,5},{2,6},{3,7},{4,0},{5,1},{6,2},{7,3},{8,12},{9,13},{10,... | collective-permute-start | bytes 2359304 | tf_op jit(solution)/shard_map/ppermute | solution.py:625
  (83 other events, 850.2 us)

commit v3 on v2

--- a/solution.py
+++ b/solution.py
@@ -158,34 +158,37 @@
 
 
 def attend_kernel(run, slots, scalars, table, query_low, query_segment, keys, values, vectors, probs, attended):
-    pair, micro = pl.program_id(0), pl.program_id(1)
-    base, lo, hi = (scalar_at(scalars, micro, entry) for entry in range(3))
+    pair = pl.program_id(0)
     span = slots * run
     first, mask_a, mask_b = head_masks()
-    left = stack_query(query_low[...], query_segment[...], mask_a, mask_b)
-    right = stack_keys(keys[...], vectors[...], lo)
-    raw = mm_nt(left, right)
-    delta, column = offsets_of(base, run, span)
-    visible = column < hi
-    biases = []
-    for head in range(2):
-        at = 2 * pair + head
-        bias = jnp.full((run, span), table[0, at], f32)
-        for step, threshold in enumerate(thresholds):
-            if threshold < span:
-                bias = jnp.where(delta >= threshold, table[1 + step, at], bias)
-                bias = jnp.where(delta <= -threshold, table[9 + step, at], bias)
-        bias = jnp.where(visible, bias, masked_score)
-        biases.append(bias)
-        biases.append(jnp.where(delta == 0, masked_score, bias))
-    scores = raw * 0.125 + jnp.concatenate(biases, axis=0)
-    peak = jnp.max(scores, axis=-1, keepdims=True)
-    mass = jnp.exp(scores - peak)
-    total = jnp.sum(mass, axis=-1, keepdims=True)
-    probs_low = (mass * (1.0 / total)).astype(low)
-    probs[0] = probs_low
-    heads = mm(probs_low, values[...])
-    attended[...] = jnp.where(first, heads[: 2 * run], heads[2 * run :])
+    for micro in range(probs.shape[0]):
+        base, lo, hi = (scalar_at(scalars, micro, entry) for entry in range(3))
+        rows = slice(micro * 2 * run, (micro + 1) * 2 * run)
+        columns = slice(micro * span, (micro + 1) * span)
+        left = stack_query(query_low[rows, :], query_segment[rows, :], mask_a, mask_b)
+        right = stack_keys(keys[columns, :], vectors[...], lo)
+        raw = mm_nt(left, right)
+        delta, column = offsets_of(base, run, span)
+        visible = column < hi
+        biases = []
+        for head in range(2):
+            at = 2 * pair + head
+            bias = jnp.full((run, span), table[0, at], f32)
+            for step, threshold in enumerate(thresholds):
+                if threshold < span:
+                    bias = jnp.where(delta >= threshold, table[1 + step, at], bias)
+                    bias = jnp.where(delta <= -threshold, table[9 + step, at], bias)
+            bias = jnp.where(visible, bias, masked_score)
+            biases.append(bias)
+            biases.append(jnp.where(delta == 0, masked_score, bias))
+        scores = raw * 0.125 + jnp.concatenate(biases, axis=0)
+        peak = jnp.max(scores, axis=-1, keepdims=True)
+        mass = jnp.exp(scores - peak)
+        total = jnp.sum(mass, axis=-1, keepdims=True)
+        probs_low = (mass * (1.0 / total)).astype(low)
+        probs[micro] = probs_low
+        heads = mm(probs_low, values[columns, :])
+        attended[rows, :] = jnp.where(first, heads[: 2 * run], heads[2 * run :])
 
 
 def norm_forward(inputs):
@@ -214,7 +217,7 @@
 
 def later_cuts(model):
     whole = model // 4 + 16
-    step = whole // 48 * 16
+    step = whole // 40 * 16
     return ((0, step), (step, step), (2 * step, whole - 2 * step))
 
 
@@ -254,8 +257,6 @@
     middle_low = middle.astype(low)
     for copy in copies[1]:
         copy.wait()
-    for copy in copies[2]:
-        copy.wait()
     wide = model
     total = None
     for start in range(0, hidden, wide):
@@ -269,6 +270,9 @@
         slope[:, at] = half + (0.5 * 0.7978845608028654) * pre * (1.0 - bent * bent) * (
             1.0 + (3 * 0.044715) * squared
         )
+        if start == 0:
+            for copy in copies[2]:
+                copy.wait()
         share = mm(act, full_outer[at, :])
         total = share if total is None else total + share
     normal_second, scale_second = norm_forward(total + vectors[4:5, :] + middle)
@@ -312,6 +316,16 @@
 
     for start in range(0, hidden, block):
         hold_outer(start, mm_tn(act_low[:, start : start + block], d_outer))
+    sent = []
+    for part, (start, height) in enumerate(routes):
+        for side in range(2):
+            for which in range(2):
+                rows_at = (pl.ds(start, height), slice(None))
+                source = held.at[(side, *half_at(routes_out[part][0], which, 4), *rows_at)]
+                target = grads[2 * side + which].at[(*(slice(None),) * 3, *rows_at)]
+                sent.append(pltpu.make_async_copy(source, target, grad_sems.at[4 * part + 2 * side + which]))
+    for copy in sent[:4]:
+        copy.start()
     d_middle = d_final_in
     for start in range(0, hidden, block):
         at = slice(start, start + block)
@@ -321,15 +335,7 @@
         small[row : row + 1, lane : lane + block] = summed
         hold_inner(start, mm_tn(middle_low, d_inner))
         d_middle = d_middle + mm_nt(d_inner, full_inner[:, at])
-    sent = []
-    for part, (start, height) in enumerate(routes):
-        for side in range(2):
-            for which in range(2):
-                rows_at = (pl.ds(start, height), slice(None))
-                source = held.at[(side, *half_at(routes_out[part][0], which, 4), *rows_at)]
-                target = grads[2 * side + which].at[(*(slice(None),) * 3, *rows_at)]
-                sent.append(pltpu.make_async_copy(source, target, grad_sems.at[4 * part + 2 * side + which]))
-    for copy in sent:
+    for copy in sent[4:]:
         copy.start()
     small[5:6, :] = column_sum(d_middle * normal_first)
     small[6:7, :] = column_sum(d_middle)
@@ -361,142 +367,134 @@
     small,
     buckets,
 ):
-    micro = pl.program_id(1)
-    base, lo = scalar_at(scalars, micro, 0), scalar_at(scalars, micro, 1)
     span = slots * run
     first, mask_a, mask_b = head_masks()
-    gradient = d_att[...]
-    stacked = jnp.concatenate([gradient * mask_a, gradient * mask_b], axis=0)
-    product = gradient.astype(f32) * attended[...]
-    delta_a = jnp.sum(jnp.where(first, product, 0.0), axis=-1, keepdims=True)
-    delta_b = jnp.sum(jnp.where(first, 0.0, product), axis=-1, keepdims=True)
-    delta_row = jnp.concatenate([delta_a, delta_b], axis=0)
-    probs_low = probs[0]
-    d_probs = mm_nt(stacked, values[...])
-    d_scores = (probs_low.astype(f32) * (d_probs - delta_row)).astype(low)
-    left = stack_query(query_low[...], query_segment[...], mask_a, mask_b)
-    right = stack_keys(keys[...], vectors[...], lo)
-    d_left = mm(d_scores, right) * 0.125
-    mine = jnp.concatenate([first, first], axis=1)
-    d_left = jnp.where(mine, d_left[: 2 * run], d_left[2 * run :])
-    d_content, d_segment = d_left[:, :128], d_left[:, 128:]
-    d_query[...] = (d_content + d_segment).astype(low)
-    d_right = mm_tn(d_scores, left) * 0.125
-    d_keys[...] = d_right[:, :128].astype(low)
-    d_values[...] = mm_tn(probs_low, stacked).astype(low)
-    row = lax.broadcasted_iota(jnp.int32, (span, 1), 0)
-    d_embed = d_right[:, 128:]
-    shares = jnp.concatenate(
-        [
-            column_sum(d_content),
-            column_sum(d_segment),
-            column_sum(jnp.where(row >= lo, 0.0, d_embed)),
-            column_sum(jnp.where(row >= lo, d_embed, 0.0)),
-            jnp.zeros((4, 128), f32),
-        ],
-        axis=0,
-    )
-    delta, _ = offsets_of(base, run, span)
-    exact = d_scores.astype(f32)
-    tallies = []
+    shares = jnp.zeros((8, 128), f32)
+    tallies = [jnp.zeros((16, span), f32)] * 2
+    for micro in range(probs.shape[0]):
+        base, lo = scalar_at(scalars, micro, 0), scalar_at(scalars, micro, 1)
+        rows = slice(micro * 2 * run, (micro + 1) * 2 * run)
+        columns = slice(micro * span, (micro + 1) * span)
+        gradient = d_att[rows, :]
+        stacked = jnp.concatenate([gradient * mask_a, gradient * mask_b], axis=0)
+        product = gradient.astype(f32) * attended[rows, :]
+        delta_a = jnp.sum(jnp.where(first, product, 0.0), axis=-1, keepdims=True)
+        delta_b = jnp.sum(jnp.where(first, 0.0, product), axis=-1, keepdims=True)
+        delta_row = jnp.concatenate([delta_a, delta_b], axis=0)
+        probs_low = probs[micro]
+        d_probs = mm_nt(stacked, values[columns, :])
+        d_scores = (probs_low.astype(f32) * (d_probs - delta_row)).astype(low)
+        left = stack_query(query_low[rows, :], query_segment[rows, :], mask_a, mask_b)
+        right = stack_keys(keys[columns, :], vectors[...], lo)
+        d_left = mm(d_scores, right) * 0.125
+        mine = jnp.concatenate([first, first], axis=1)
+        d_left = jnp.where(mine, d_left[: 2 * run], d_left[2 * run :])
+        d_content, d_segment = d_left[:, :128], d_left[:, 128:]
+        d_query[rows, :] = (d_content + d_segment).astype(low)
+        d_right = mm_tn(d_scores, left) * 0.125
+        d_keys[columns, :] = d_right[:, :128].astype(low)
+        d_values[columns, :] = mm_tn(probs_low, stacked).astype(low)
+        row = lax.broadcasted_iota(jnp.int32, (span, 1), 0)
+        d_embed = d_right[:, 128:]
+        shares = shares + jnp.concatenate(
+            [
+                column_sum(d_content),
+                column_sum(d_segment),
+                column_sum(jnp.where(row >= lo, 0.0, d_embed)),
+                column_sum(jnp.where(row >= lo, d_embed, 0.0)),
+                jnp.zeros((4, 128), f32),
+            ],
+            axis=0,
+        )
+        delta, _ = offsets_of(base, run, span)
+        exact = d_scores.astype(f32)
+        for head in range(2):
+            at = 2 * run * head
+            both = exact[at : at + run] + exact[at + run : at + 2 * run]
+            lines = [None] * 16
+            lines[0] = column_sum(jnp.where(delta == 0, both, 0.0))
+            for step, threshold in enumerate(thresholds):
+                if threshold < span:
+                    later = thresholds[step + 1] if step + 1 < len(thresholds) else span
+                    above = (delta >= threshold) & (delta < later)
+                    below = (delta <= -threshold) & (delta > -later)
+                    lines[1 + step] = column_sum(jnp.where(above, both, 0.0))
+                    lines[9 + step] = column_sum(jnp.where(below, both, 0.0))
+            blank = jnp.zeros((1, span), f32)
+            tallies[head] = tallies[head] + jnp.concatenate(
+                [blank if entry is None else entry for entry in lines], axis=0
+            )
+    small[...] = shares
     for head in range(2):
-        at = 2 * run * head
-        both = exact[at : at + run] + exact[at + run : at + 2 * run]
-        rows = [None] * 16
-        rows[0] = column_sum(jnp.where(delta == 0, both, 0.0))
-        for step, threshold in enumerate(thresholds):
-            if threshold < span:
-                later = thresholds[step + 1] if step + 1 < len(thresholds) else span
-                above = (delta >= threshold) & (delta < later)
-                below = (delta <= -threshold) & (delta > -later)
-                rows[1 + step] = column_sum(jnp.where(above, both, 0.0))
-                rows[9 + step] = column_sum(jnp.where(below, both, 0.0))
-        blank = jnp.zeros((1, span), f32)
-        tallies.append(jnp.concatenate([blank if entry is None else entry for entry in rows], axis=0))
-
-    @pl.when(micro == 0)
-    def _():
-        small[...] = shares
-        for head in range(2):
-            buckets[head] = tallies[head]
-
-    @pl.when(micro != 0)
-    def _():
-        small[...] += shares
-        for head in range(2):
-            buckets[head] += tallies[head]
+        buckets[head] = tallies[head]
+
+
+def columns_of(parts, at):
+    pieces, start = [], 0
+    for part in parts:
+        low_end, high_end = max(at.start, start), min(at.stop, start + part.shape[1])
+        if low_end < high_end:
+            pieces.append(part[:, low_end - start : high_end - start])
+        start += part.shape[1]
+    return pieces[0] if len(pieces) == 1 else jnp.concatenate(pieces, axis=1)
 
 
 def weights_kernel(
     pieces,
-    run,
-    slots,
     scalars,
-    found,
     rows,
     path,
     attended,
     d_branch,
-    d_query,
-    d_keys,
-    d_values,
-    d_mid_in,
     small_first,
-    small_second,
-    tallies,
     *refs,
 ):
-    weights = [refs[i * pieces : (i + 1) * pieces] for i in range(3)]
-    refs = refs[3 * pieces :]
-    d_content, d_state = refs[:2]
+    d_query, d_keys, d_values, small_second, tallies = (refs[i : 10 : 5] for i in range(5))
+    refs = refs[10:]
     model = rows.shape[1]
     block = model // 2
     if pieces == 2:
-        kept, sent, full, tree, held, sems, grad_sems = refs[2:4], refs[4:6], *refs[6:]
+        kept, sent, held, grad_sems = refs[:2], refs[2:4], *refs[4:]
     else:
-        natural, tree_out, small_out, full, tree, sems, grad_sems = refs[2:6], *refs[6:]
+        natural, small_out = refs[:4], refs[4]
     shard, place = scalars[0], scalars[1]
-    copies = [weight_copies(weights[i], full.at[i], sems, i * pieces, shard) for i in range(3)]
-    for group in copies:
-        for copy in group:
-            copy.start()
     small_rows = block // 8
 
-    def hold(which, value):
+    def hold(which, across, value):
         if pieces == 1:
-            natural[which][...] = value.astype(low)
+            natural[which][:, across * block : (across + 1) * block] = value.astype(low)
             return
+        spot = (slice(which * small_rows, (which + 1) * small_rows), slice(None))
         for half in range(2):
             for down in range(8):
-                for across in range(2):
-                    start = half * block + down * small_rows
-                    spot = slice(which * small_rows, (which + 1) * small_rows)
-                    held[(half ^ shard, *block_index((down * 2 + across) ^ place, 4), spot, slice(None))] = value[
-                        start : start + small_rows, across * block : (across + 1) * block
-                    ].astype(low)
-
-    hold(0, mm_tn(rows[...], d_query[...]))
-    hold(1, mm_tn(path[...], d_keys[...]))
-    hold(2, mm_tn(path[...], d_values[...]))
-    hold(3, mm_tn(attended[...].astype(low), d_branch[...]))
-    ones = jnp.ones((8, tallies.shape[2]), f32)
-    sums = []
-    for head in range(tallies.shape[0]):
-        sums.append(
-            lax.dot_general(
-                ones,
-                tallies[head],
-                (((1,), (1,)), ((), ())),
-                precision=lax.Precision.HIGHEST,
-                preferred_element_type=f32,
-            )[:1]
+                start = half * block + down * small_rows
+                held[(half ^ shard, *block_index((down * 2 + across) ^ place, 4), *spot)] = value[
+                    start : start + small_rows, :
+                ].astype(low)
+
+    for across in range(2):
+        at = slice(across * block, (across + 1) * block)
+        hold(0, across, mm_tn(rows[...], columns_of(d_query, at)))
+        hold(1, across, mm_tn(path[...], columns_of(d_keys, at)))
+        hold(2, across, mm_tn(path[...], columns_of(d_values, at)))
+        hold(3, across, mm_tn(attended[...].astype(low), d_branch[:, at]))
+    buckets = jnp.zeros((16, 16), f32)
+    every_head = [part[head] for part in tallies for head in range(part.shape[0])]
+    line = lax.broadcasted_iota(jnp.int32, every_head[0].shape, 0)
+    for head, tally in enumerate(every_head):
+        buckets = buckets + lax.dot_general(
+            tally,
+            (line == head).astype(f32),
+            (((1,), (1,)), ((), ())),
+            precision=lax.Precision.HIGHEST,
+            preferred_element_type=f32,
         )
-    buckets = jnp.concatenate(sums, axis=0)
     if pieces == 1:
         small_out[:9, :] = small_first[:9, :]
-        small_out[9:13, :] = small_second[:4, :]
+        for across in range(2):
+            small_out[9:13, across * block : (across + 1) * block] = columns_of(small_second, slice(across * block, (across + 1) * block))[:4]
         small_out[13:, :] = jnp.zeros((small_out.shape[0] - 13, model), f32)
-        small_out[16 : 16 + buckets.shape[0], :16] = buckets
+        small_out[16:32, :16] = buckets
     else:
         last = model // 4
         for half in range(2):
@@ -506,15 +504,14 @@
                 for i in range(4)
             ]
             lines += [small_first[i : i + 1, at] for i in range(4, 9)]
-            lines += [small_second[i : i + 1, at] for i in range(4)]
+            late_lines = columns_of(small_second, at)
+            lines += [late_lines[i : i + 1, :] for i in range(4)]
             for chunk in range(16):
                 line = lines[chunk].astype(low) if chunk < 13 else jnp.zeros((1, block), low)
                 spread_line = jnp.concatenate([line.astype(f32), jnp.zeros((15, block), f32)], axis=0)
                 held[(half ^ shard, *block_index(chunk ^ place, 4), slice(last, last + 16), slice(None))] = spread_line.astype(low)
-            wide = jnp.concatenate(
-                [buckets[:, 8 * half : 8 * half + 8], jnp.zeros((buckets.shape[0], block - 8), f32)], axis=1
-            )
-            wide = jnp.concatenate([wide, jnp.zeros((16 - buckets.shape[0], block), f32)], axis=0)
+            wide = jnp.concatenate([buckets[8 * half : 8 * half + 8], jnp.zeros((8, 16), f32)], axis=0)
+            wide = jnp.concatenate([wide, jnp.zeros((16, block - 16), f32)], axis=1)
             held[(half ^ shard, *block_index(13 ^ place, 4), slice(last, last + 16), slice(None))] = wide.astype(low)
     leaving = []
     if pieces == 2:
@@ -528,15 +525,35 @@
                     leaving.append(pltpu.make_async_copy(source, target, grad_sems.at[6 * side + at]))
         for copy in leaving:
             copy.start()
+    for copy in leaving:
+        copy.wait()
+
+
+def tree_kernel(pieces, run, slots, scalars, found, d_mid_in, *refs):
+    d_query, d_keys, d_values = (refs[i : 6 : 3] for i in range(3))
+    refs = refs[6:]
+    weights = [refs[i * pieces : (i + 1) * pieces] for i in range(3)]
+    refs = refs[3 * pieces :]
+    d_content, d_state = refs[:2]
+    if pieces == 2:
+        kept, full, tree, sems, grad_sems = refs[2:4], *refs[4:]
+    else:
+        tree_out, full, tree, sems, grad_sems = refs[2:]
+    copies = [weight_copies(weights[i], full.at[i], sems, i * pieces, scalars[0]) for i in range(3)]
     for group in copies:
         for copy in group:
+            copy.start()
+    block = d_mid_in.shape[1] // 2
+    tree[...] = jnp.zeros(tree.shape, tree.dtype)
+    for group in copies[1:]:
+        for copy in group:
             copy.wait()
-    tree[...] = jnp.zeros(tree.shape, tree.dtype)
     span = slots * run
-    micro_count = rows.shape[0] // (2 * run)
+    micro_count = d_mid_in.shape[0] // (2 * run)
     for micro in range(micro_count):
         at = slice(micro * span, (micro + 1) * span)
-        shares = mm_nt(d_keys[at, :], full[1]) + mm_nt(d_values[at, :], full[2])
+        shares = mm_nt(jnp.concatenate([entry[at, :] for entry in d_keys], axis=1), full[1])
+        shares = shares + mm_nt(jnp.concatenate([entry[at, :] for entry in d_values], axis=1), full[2])
         for slot in range(slots):
             relative = found[micro * slots + slot]
             for half in range(2):
@@ -546,22 +563,23 @@
                 tree[spot] = (tree[spot].astype(f32) + piece).astype(low)
     if pieces == 2:
         last_copies = []
-        skip = model // 4 + 16
         for part, (start, height) in enumerate(tree_cuts(tree.shape[-2])):
             for which in range(2):
                 source = tree.at[(*half_at(routes_out[part][0], which, 4), pl.ds(start, height), slice(None))]
-                target = kept[which].at[(*(slice(None),) * 3, pl.ds(skip + start, height), slice(None))]
-                last_copies.append(pltpu.make_async_copy(source, target, grad_sems.at[12 + 2 * part + which]))
+                target = kept[which].at[(*(slice(None),) * 3, pl.ds(start, height), slice(None))]
+                last_copies.append(pltpu.make_async_copy(source, target, grad_sems.at[2 * part + which]))
     else:
         last_copies = [pltpu.make_async_copy(tree, tree_out, grad_sems.at[0])]
     for copy in last_copies:
         copy.start()
-    d_both = d_mid_in[...] + mm_nt(d_query[...], full[0])
+    for copy in copies[0]:
+        copy.wait()
+    d_both = d_mid_in[...] + mm_nt(jnp.concatenate([entry[...] for entry in d_query], axis=1), full[0])
     for micro in range(micro_count):
         start = 2 * run * micro
         d_content[micro] = d_both[start : start + run]
         d_state[micro] = d_both[start + run : start + 2 * run]
-    for copy in leaving + last_copies:
+    for copy in last_copies:
         copy.wait()
 
 
@@ -596,7 +614,7 @@
 
 
 def later_spread_kernel(scalars, *refs):
-    weights, small, sources, sems = refs[6:10], refs[10], refs[11:14], refs[14]
+    weights, inner_bias, vectors, embed, table, sources, sems = refs[6:10], refs[10], refs[11:18], *refs[18:20], refs[20:23], refs[23]
     collect_pieces(refs[:6], sources, sems)
     place = scalars[1]
     side = sources[0].shape[-1]
@@ -614,7 +632,15 @@
                     weights[which][top : top + end - begin, across : across + side] = value[begin - start : end - start]
             begin = 4 * rows
             if start <= begin < start + height:
-                small[chunk] = value[begin - start : begin - start + 16]
+                line = value[begin - start : begin - start + 1]
+                if chunk < 4:
+                    inner_bias[chunk * side : (chunk + 1) * side] = line.reshape(side)
+                elif chunk < 11:
+                    vectors[chunk - 4][...] = line.reshape(side)
+                elif chunk < 13:
+                    embed[chunk - 11 : chunk - 10, :] = line
+                elif chunk == 13:
+                    table[...] = value[begin - start : begin - start + table.shape[0], : table.shape[1]]
 
 
 routes_out = ((0, 1, 2), (1, 2, 0), (2, 0, 1))
@@ -791,32 +817,26 @@
     content_rows = micro_count * run
     block = jnp.concatenate([content.reshape(content_rows, model), fact_rows], axis=0)
     total_bits = bit_total()
-    block, b_inner, b_outer, parent, w_query, w_key = lax.optimization_barrier(
-        (block, b_inner, b_outer, parent, w_query, w_key)
+    block, b_inner, b_outer, parent, seg_embed, w_query, w_key, cot_content = lax.optimization_barrier(
+        (block, b_inner, b_outer, parent, seg_embed, w_query, w_key, cot_content)
     )
     held = block.reshape((1,) * total_bits + block.shape)
     for bit in extra_bits():
         held = grow(held, bit)
     query_weights, key_weights = fetch(w_query), fetch(w_key)
+    inner_rows = b_inner.shape[0] // part_width
+    flat = [b_inner, b_outer, gain_attn, bias_attn, gain_ffn, bias_ffn, bias_content, bias_segment]
+    flat += [seg_embed.reshape(-1), rel_table.reshape(-1)]
+    fill = 16 * part_width - sum(entry.size for entry in flat)
+    small_parts = jnp.concatenate(flat + [jnp.zeros((fill,), low)]).reshape(16, part_width)
     parts = []
     for part, (start, width) in enumerate(columns):
         height = block.shape[0] if part == 0 else content_rows
         parts.append(held[..., :height, start : start + width])
-    parts, (query_weights[-1], key_weights[-1], w_value, w_out) = advance_free(
-        parts, [query_weights[-1], key_weights[-1], w_value, w_out]
+    parts, (query_weights[-1], key_weights[-1], w_value, small_parts, parent, content, cot_query) = advance_free(
+        parts, [query_weights[-1], key_weights[-1], w_value, small_parts, parent, content, cot_query]
     )
-    value_weights, out_weights = fetch(w_value), fetch(w_out)
-    parts = [grow(piece, route[2]) for piece, route in zip(parts, routes_out)]
-    parts, (value_weights[-1], out_weights[-1], w_inner) = advance_free(
-        parts, [value_weights[-1], out_weights[-1], w_inner]
-    )
-    inner_weights = fetch(w_inner)
-    parts = [grow(piece, route[1]) for piece, route in zip(parts, routes_out)]
-    parts, (inner_weights[-1], w_outer) = advance_free(parts, [inner_weights[-1], w_outer])
-    outer_weights = fetch(w_outer)
-    tree_parts = [entry for piece, route in zip(parts, routes_out) for entry in (piece, send(piece, route[0]))]
-    tree_parts, (outer_weights[-1],) = advance_free(tree_parts, [outer_weights[-1]])
-
+    value_weights = fetch(w_value)
     first_branch, first_leaf = trunk_runs * per_run, (trunk_runs + 1) * per_run
     mine = own_seg
     above = jnp.sum(jnp.where(jnp.arange(parent.shape[2]) == mine[:, None], parent[:, 0], 0), axis=1)
@@ -828,30 +848,31 @@
     facts_own = jnp.stack([own_slot * run, lo, hi, mine, branch], axis=1)
     scalars = jnp.concatenate([early, facts_own.reshape(-1)]).astype(jnp.int32)
 
-    small_parts = jnp.concatenate(
-        [
-            b_inner.reshape(-1, part_width),
-            jnp.stack([b_outer, gain_attn, bias_attn, gain_ffn, bias_ffn, bias_content, bias_segment]),
-            seg_embed,
-            jnp.pad(rel_table.reshape(1, -1), ((0, 0), (0, part_width - rel_table.size))),
-        ],
-        axis=0,
-    )
-    inner_rows = b_inner.shape[0] // part_width
-    fill = 16 - small_parts.shape[0]
-    small_parts = jnp.pad(small_parts, ((0, fill), (0, 0)))
+    rows = jnp.concatenate([content, query_state], axis=1).reshape(rows_total, model)
+    cotangent = jnp.concatenate([cot_content, cot_query], axis=1).reshape(rows_total, model)
     if pieces == 2:
         other = lax.ppermute(small_parts, "shard", [(0, 1), (1, 0)])
         gathered = jnp.where(shard == 0, jnp.stack([small_parts, other]), jnp.stack([other, small_parts]))
     else:
         gathered = lax.all_gather(small_parts, "shard", axis=0, tiled=False)
     gathered = gathered.astype(f32)
+    parts = [grow(piece, route[2]) for piece, route in zip(parts, routes_out)]
+    parts, (value_weights[-1], w_out, w_inner, gathered, scalars, rows, cotangent) = advance_free(
+        parts, [value_weights[-1], w_out, w_inner, gathered, scalars, rows, cotangent]
+    )
+    inner_weights, out_weights = fetch(w_inner), fetch(w_out)
     inner_bias = gathered[:, :inner_rows].reshape(1, hidden)
     vectors = jnp.transpose(gathered, (1, 0, 2)).reshape(16, model)
     table = gathered[:, 13, : rel_table.size].reshape(bucket_total, heads)
 
-    rows = jnp.concatenate([content, query_state], axis=1).reshape(rows_total, model)
-    cotangent = jnp.concatenate([cot_content, cot_query], axis=1).reshape(rows_total, model)
+    parts = [grow(piece, route[1]) for piece, route in zip(parts, routes_out)]
+    parts, (out_weights[-1], inner_weights[-1], w_outer, vectors, inner_bias, table) = advance_free(
+        parts, [out_weights[-1], inner_weights[-1], w_outer, vectors, inner_bias, table]
+    )
+    outer_weights = fetch(w_outer)
+    tree_parts = [entry for piece, route in zip(parts, routes_out) for entry in (piece, send(piece, route[0]))]
+    tree_parts, (outer_weights[-1],) = advance_free(tree_parts, [outer_weights[-1]])
+
     grown = pltpu.CompilerParams(vmem_limit_bytes=vmem_bytes)
 
     def shape(dims, kind):
@@ -866,7 +887,7 @@
         scratch_shapes=[pltpu.VMEM((model, model), low), dma((pieces,))],
         compiler_params=grown,
         name="query_projection",
-        cost_estimate=cost(4),
+        cost_estimate=cost(1),
     )(early, rows, vectors, *query_weights)
 
     path, keys, values, found = pl.pallas_call(
@@ -892,13 +913,18 @@
     )(scalars, *tree_parts, *key_weights, *value_weights)
     path = path.reshape(micro_count * span, model)
 
-    row_block = pl.BlockSpec((2 * run, 128), lambda pair, micro: (micro, pair))
-    key_block = pl.BlockSpec((span, 128), lambda pair, micro: (micro, pair))
-    vector_block = pl.BlockSpec((16, 128), lambda pair, micro: (0, pair))
-    prob_block = pl.BlockSpec((1, 4 * run, span), lambda pair, micro: (pair * micro_count + micro, 0, 0))
+    def blocks_at(first):
+        return (
+            pl.BlockSpec((rows_total, 128), lambda pair: (0, pair + first)),
+            pl.BlockSpec((micro_count * span, 128), lambda pair: (0, pair + first)),
+            pl.BlockSpec((micro_count, 4 * run, span), lambda pair: (pair + first, 0, 0)),
+            pl.BlockSpec((16, 128), lambda pair: (0, pair + first)),
+        )
+
+    row_block, key_block, prob_block, vector_block = blocks_at(0)
     probs, attended = pl.pallas_call(
         functools.partial(attend_kernel, run, slots),
-        grid=(pairs, micro_count),
+        grid=(pairs,),
         out_shape=(
             shape((pairs * micro_count, 4 * run, span), low),
             shape((rows_total, model), f32),
@@ -953,29 +979,32 @@
         feed_grads = results[6:]
         feed_other = [lax.ppermute(entry, "shard", swap) for entry in (feed_grads[3], feed_grads[2])]
 
-    d_query, d_keys, d_values, small_second, tallies = pl.pallas_call(
-        functools.partial(back_kernel, run, slots),
-        grid=(pairs, micro_count),
-        out_shape=(
-            shape((rows_total, model), low),
-            shape((micro_count * span, model), low),
-            shape((micro_count * span, model), low),
-            shape((8, model), f32),
-            shape((heads, 16, span), f32),
-        ),
-        in_specs=[smem_space, row_block, row_block, key_block, key_block, prob_block, row_block, row_block, vector_block],
-        out_specs=(
-            row_block,
-            key_block,
-            key_block,
-            pl.BlockSpec((8, 128), lambda pair, micro: (0, pair)),
-            pl.BlockSpec((2, 16, span), lambda pair, micro: (pair, 0, 0)),
-        ),
-        compiler_params=grown,
-        name="attend_back",
-        cost_estimate=cost(14),
-    )(scalars, query_low, query_segment, keys, values, probs, d_att, attended, vectors)
-
+    def attend_back(first, pair_count, gradient):
+        rows_in, keys_in, probs_in, vector_in = blocks_at(first)
+        return pl.pallas_call(
+            functools.partial(back_kernel, run, slots),
+            grid=(pair_count,),
+            out_shape=(
+                shape((rows_total, 128 * pair_count), low),
+                shape((micro_count * span, 128 * pair_count), low),
+                shape((micro_count * span, 128 * pair_count), low),
+                shape((8, 128 * pair_count), f32),
+                shape((2 * pair_count, 16, span), f32),
+            ),
+            in_specs=[smem_space, rows_in, rows_in, keys_in, keys_in, probs_in, rows_in, rows_in, vector_in],
+            out_specs=(
+                row_block,
+                key_block,
+                key_block,
+                pl.BlockSpec((8, 128), lambda pair: (0, pair)),
+                pl.BlockSpec((2, 16, span), lambda pair: (pair, 0, 0)),
+            ),
+            compiler_params=grown,
+            name="attend_back",
+            cost_estimate=cost(3),
+        )(scalars, query_low, query_segment, keys, values, probs, gradient, attended, vectors)
+
+    back_first = attend_back(0, pairs // 3, d_att)
     if pieces == 2:
         sizes = [height for _, height in feed_cuts(pieces, model)]
         upper = [
@@ -983,75 +1012,73 @@
             for (start, height), route in zip(feed_cuts(pieces, model), routes_out)
         ]
         feed_lower = feed_other[1]
-        *upper, feed_lower, d_query = lax.optimization_barrier((*upper, feed_lower, d_query))
+        *upper, feed_lower, d_att, _ = lax.optimization_barrier((*upper, feed_lower, d_att, back_first[0]))
         lower = [
             spread_dims(feed_grads[0][..., start : start + height, :] + feed_lower[..., start : start + height, :], route)
             for (start, height), route in zip(feed_cuts(pieces, model), routes_out)
         ]
         feed_rounds = Rounds(sum_rounds(lower, upper, sizes))
         feed_rounds.advance(feed_rounds.pending)
+    back_second = attend_back(pairs // 3, pairs - pairs // 3, d_att)
     tree_height = 2 * micro_count * run
     if pieces == 2:
         whole = later_cuts(model)[-1][0] + later_cuts(model)[-1][1]
         heights = [entry[1] for entry in later_cuts(model)]
-        grad_shapes = [shape((2,) * (total_bits - 1) + (whole + tree_height, half), low)] * 2
-        grad_shapes += [shape((2,) * (total_bits - 1) + (whole, half), low)] * 2
+        cube = (2,) * (total_bits - 1)
+        grad_shapes = [shape(cube + (whole, half), low)] * 4
         grad_specs = [any_space] * 4
-        extra = [pltpu.VMEM((2,) * (1 + total_bits) + (whole, half), low)]
+        extra = [pltpu.VMEM((2,) * (1 + total_bits) + (whole, half), low), dma((12,))]
+        tree_shapes = [shape(cube + (tree_height, half), low)] * 2
     else:
-        grad_shapes = [shape((model, model), low)] * 4 + [
-            shape((2,) * total_bits + (tree_height, half), low),
-            shape((32, model), f32),
-        ]
-        grad_specs = [vmem_space] * 4 + [any_space, vmem_space]
+        grad_shapes = [shape((model, model), low)] * 4 + [shape((32, model), f32)]
+        grad_specs = [vmem_space] * 5
         extra = []
+        tree_shapes = [shape((2,) * total_bits + (tree_height, half), low)]
     later = pl.pallas_call(
-        functools.partial(weights_kernel, pieces, run, slots),
-        out_shape=[shape((micro_count, run, model), f32)] * 2 + grad_shapes,
-        in_specs=[smem_space] * 2 + [vmem_space] * 11 + [any_space] * (3 * pieces),
-        out_specs=[vmem_space] * 2 + grad_specs,
-        scratch_shapes=[pltpu.VMEM((3, model, model), low), pltpu.VMEM((2,) * total_bits + (tree_height, half), low)]
-        + extra
-        + [dma((3 * pieces,)), dma((18,))],
+        functools.partial(weights_kernel, pieces),
+        out_shape=grad_shapes,
+        in_specs=[smem_space] + [vmem_space] * 15,
+        out_specs=grad_specs,
+        scratch_shapes=extra,
         compiler_params=grown,
         name="weight_gradients",
-        cost_estimate=cost(15),
-    )(
-        scalars,
-        found,
-        rows,
-        path,
-        attended,
-        d_branch,
-        d_query,
-        d_keys,
-        d_values,
-        d_mid_in,
-        small_first,
-        small_second,
-        tallies,
-        *query_weights,
-        *key_weights,
-        *value_weights,
-    )
-    d_content, grad_query = later[:2]
-
+        cost_estimate=cost(3),
+    )(scalars, rows, path, attended, d_branch, small_first, *back_first, *back_second)
     if pieces == 2:
-        feed_rounds.pending, others = advance_free(feed_rounds.pending, [later[5], later[4]])
-        others = [lax.ppermute(entry, "shard", swap) for entry in others]
+        feed_rounds.pending, later = advance_free(feed_rounds.pending, later)
+        feed_rounds.pending, (d_mid_in,) = advance_free(feed_rounds.pending, [d_mid_in])
         feed_rounds.advance(feed_rounds.pending)
+    d_content, grad_query, *tree_grads = pl.pallas_call(
+        functools.partial(tree_kernel, pieces, run, slots),
+        out_shape=[shape((micro_count, run, model), f32)] * 2 + tree_shapes,
+        in_specs=[smem_space] * 2 + [vmem_space] * 7 + [any_space] * (3 * pieces),
+        out_specs=[vmem_space] * 2 + [any_space] * len(tree_shapes),
+        scratch_shapes=[
+            pltpu.VMEM((3, model, model), low),
+            pltpu.VMEM((2,) * total_bits + (tree_height, half), low),
+            dma((3 * pieces,)),
+            dma((6,)),
+        ],
+        compiler_params=grown,
+        name="tree_gradients",
+        cost_estimate=cost(3),
+    )(scalars, found, d_mid_in, *back_first[:3], *back_second[:3], *query_weights, *key_weights, *value_weights)
+
+    if pieces == 2:
+        others = [lax.ppermute(entry, "shard", swap) for entry in (later[3], later[2])]
         feed_rounds.pending, others = advance_free(feed_rounds.pending, others)
+        feed_rounds.pending, tree_grads = advance_free(feed_rounds.pending, tree_grads)
         feed_rounds.advance(feed_rounds.pending)
 
-        def route_sum(mine, other, part):
+        def route_sum(which, part):
             start, height = later_cuts(model)[part]
             more, tall = tree_cuts(tree_height)[part]
-            summed = mine[..., start : start + height, :] + other[..., start : start + height, :]
-            more_rows = mine[..., whole + more : whole + more + tall, :]
-            return spread_dims(jnp.concatenate([summed, more_rows], axis=-2), routes_out[part])
-
-        lower = [route_sum(later[2], others[1], part) for part in range(3)]
-        upper = [route_sum(later[3], others[0], part) for part in range(3)]
+            mine, other = later[which][..., start : start + height, :], others[1 - which][..., start : start + height, :]
+            more_rows = tree_grads[which][..., more : more + tall, :]
+            return spread_dims(jnp.concatenate([mine + other, more_rows], axis=-2), routes_out[part])
+
+        lower = [route_sum(0, part) for part in range(3)]
+        upper = [route_sum(1, part) for part in range(3)]
         later_rounds = Rounds(sum_rounds(lower, upper, heights))
         for _ in range(5):
             advance_after(later_rounds, feed_rounds)
@@ -1076,32 +1103,33 @@
         later_done, shares = later_rounds.result
         arrived = [share.reshape(share.shape[-2:])[rows:] for share, rows in zip(shares, heights)]
         tree_grad = jnp.concatenate(arrived, axis=0)
-        *squares, small = pl.pallas_call(
+        spread_out = pl.pallas_call(
             later_spread_kernel,
-            out_shape=[shape(w_query.shape, f32)] * 4 + [shape((dp_count, 16, half), f32)],
+            out_shape=[shape(w_query.shape, f32)] * 4
+            + [shape(b_inner.shape, f32)]
+            + [shape(b_outer.shape, f32)] * 7
+            + [shape(seg_embed.shape, f32), shape(rel_table.shape, f32)],
             in_specs=[smem_space] + [any_space] * 6,
-            out_specs=[vmem_space] * 5,
+            out_specs=[vmem_space] * 14,
             scratch_shapes=pieces_scratch(heights),
             compiler_params=grown,
             name="later_spread",
             cost_estimate=cost(4),
         )(early, *later_done)
-        grad_w_query, grad_w_key, grad_w_value, grad_w_out = squares
-        grad_b_inner = small[:4, 0].reshape(-1)
-        narrow = small[4:13, 0]
-        grad_rel_table = jnp.transpose(small[13, :heads, : rel_table.shape[0]])
+        grad_w_query, grad_w_key, grad_w_value, grad_w_out, grad_b_inner, *narrow, grad_rel_table = spread_out
     else:
         totals = []
-        for entry in (*results[6:8], *later[2:6]):
+        for entry in (*results[6:8], *later[:4]):
             share = lax.psum_scatter(entry, "shard", scatter_dimension=0, tiled=True)
             totals.append(lax.psum(share, "dp").astype(f32))
         grad_w_outer, grad_w_inner, grad_w_query, grad_w_key, grad_w_value, grad_w_out = totals
-        tree_grad = scatter_blocks(later[6], routes_out[0])
-        small = lax.psum(later[7], ("shard", "dp"))
+        tree_grad = scatter_blocks(tree_grads[0], routes_out[0])
+        small = lax.psum(later[4], ("shard", "dp"))
         grad_b_inner = lax.dynamic_slice_in_dim(small[:4].reshape(-1), shard * b_inner.shape[0], b_inner.shape[0])
         narrow = lax.dynamic_slice_in_dim(small[4:13], shard * part_width, part_width, axis=1)
+        narrow = [*narrow[:7], narrow[7:9]]
         grad_rel_table = lax.dynamic_slice_in_dim(
-            jnp.transpose(small[16 : 16 + heads, :bucket_total]), shard * rel_table.shape[0], rel_table.shape[0], axis=0
+            small[16 : 16 + bucket_total, :heads], shard * rel_table.shape[0], rel_table.shape[0], axis=0
         )
     halves = tree_grad.astype(f32).reshape(2, micro_count, run, half)
     grad_content = d_content + jnp.concatenate([halves[0], halves[1]], axis=-1)
@@ -1124,7 +1152,7 @@
         narrow[4],
         narrow[5],
         narrow[6],
-        narrow[7:9],
+        narrow[7],
         grad_rel_table,
     )
 

time: 312 us -> 287 us (0.920)
  waiting for transfers between devices: 127 us -> 91.4 us
  starting transfers between devices: 65.9 us -> 72.3 us
  other arithmetic: 15.8 us -> 20.2 us
    ppermute x50, waiting for transfers between devices: 127 us -> 91.4 us  [send(): return lax.ppermute(inputs, 'dp', [(i, i ^ 1 << bit) for i in range(count)])]
    ppermute x50, starting transfers between devices: 63.1 us -> 70.3 us  [send(): return lax.ppermute(inputs, 'dp', [(i, i ^ 1 << bit) for i in range(count)])]
    concatenate x1, local copies, waits for them, and re-layouts: 0.07 us -> 5.61 us  [shards(): jnp.concatenate(flat + [jnp.zeros((fill,), low)]).reshape(16, part_width)]
    slice x7 -> x4, local copies, waits for them, and re-layouts: 4.69 us -> 0.38 us  [route_sum(): more_rows = tree_grads[which][..., more:more + tall, :]]
    pallas_call x2 -> x4, Pallas kernels: 29.2 us -> 31.4 us  [the longest x2 13.7 us: attend_back(): pl.pallas_call(functools.partial(back_kernel, run, slots), grid=(pair_cou...]
    unnamed x95 -> x70, local copies, waits for them, and re-layouts: 6.83 us -> 4.8 us
  transfers between devices with their start and end apart: 61 -> 61, of which waited for: 32 -> 26; matrix products, arithmetic and copies ran while one was open for 5% -> 10% of each run, Pallas kernels for 13% -> 15%
where the time goes in v3:
time: 287 us; the launch traced here: 286 us
  waiting for transfers between devices  91.4 us (32%)
  Pallas kernels  82.6 us (29%)
  starting transfers between devices  72.3 us (25%)
  other arithmetic  20.2 us (7%)
  local copies, waits for them, and re-layouts  17.1 us (6%)
    ppermute x50, waiting for transfers between devices, send(): return lax.ppermute(inputs, 'dp', [(i, i ^ 1 << bit) for i in range(count)])  91.4 us
    ppermute x50, starting transfers between devices, send(): return lax.ppermute(inputs, 'dp', [(i, i ^ 1 << bit) for i in range(count)])  70.3 us
    pallas_call x1, Pallas kernels, shards(): pl.pallas_call(functools.partial(feed_kernel, pieces, run), out_shape=[sh...  20.2 us
    pallas_call x2, Pallas kernels, attend_back(): pl.pallas_call(functools.partial(back_kernel, run, slots), grid=(pair_cou...  13.7 us
    pallas_call x1, Pallas kernels, shards(): pl.pallas_call(functools.partial(weights_kernel, pieces), out_shape=grad_...  8.97 us
    pallas_call x1, Pallas kernels, shards(): pl.pallas_call(functools.partial(tree_kernel, pieces, run, slots), out_sh...  8.77 us
    pallas_call x1, Pallas kernels, shards(): pl.pallas_call(functools.partial(attend_kernel, run, slots), grid=(pairs,...  8.72 us
    pallas_call x1, Pallas kernels, shards(): pl.pallas_call(feed_spread_kernel, out_shape=(shape(w_outer.shape, f32),...  7.36 us
  transfers between devices with their start and end apart: 61, of which 26 were waited for; matrix products, arithmetic and copies ran while one was open for 10% of the time, Pallas kernels for 15%

profile of v3, /device:TPU:0, one launch (start us, length us, event | category | flops | bytes accessed | tf_op | source)
XLA Modules:
  0.0 285.7 jit_solution(9571409921532702135)
XLA Ops:
  4.2 4.0 %collective-permute-start = (bf16[1,1,1,1,144,768]{5,4,3,2,1,0:T(8,128)(2,1)S(1)}, bf16[1,1,1,1,144,768]{5,4,3,2,1,0:T(8,128)(2,1)S(1)}, u32[]{:S(2)}, u32[]{:S(2)}) collective-permute-start(bf16[1,1,1,1,144,768]{5,4,3,2,1,0:T(8,128)(2,1)S(1)} %bitcast.71), channel_id=1, source_target_pairs={{0,8},{1,9},{2,10},{3,11},{4,12},{5,13},{6,14},{7,15},{8,0},{9,1},... | collective-permute-start | bytes 663560 | tf_op jit(solution)/shard_map/ppermute | solution.py:651
  9.8 5.6 %concatenate.117 = bf16[6144]{0:T(1024)(128)(2,1)S(1)} concatenate(bf16[1536]{0:T(1024)(128)(2,1)} %param.34, bf16[384]{0:T(512)(128)(2,1)} %param.35, bf16[384]{0:T(512)(128)(2,1)} %param.36, bf16[384]{0:T(512)(128)(2,1)} %param.37, bf16[384]{0:T(512)(128)(2,1)} %param.38, bf16[384]{0:T(512)(128)(2,1)} %param.39, bf16[384]{0:T(512)(128)(2,1)} %param.40, bf16[384]{0:T(512)(128)(2,1)} %param.41, ...), dimensions={0} | concatenate | bytes 24576 | tf_op jit(solution)/shard_map/concatenate | solution.py:831
  32.4 4.8 %collective-permute-done.9 = bf16[2,1,1,2,128,256]{5,4,3,2,1,0:T(8,128)(2,1)S(1)} collective-permute-done((bf16[2,1,1,2,128,256]{5,4,3,2,1,0:T(8,128)(2,1)S(1)}, bf16[2,1,1,2,128,256]{5,4,3,2,1,0:T(8,128)(2,1)S(1)}, u32[]{:S(2)}, u32[]{:S(2)}) %collective-permute-start.9) | collective-permute-done | bytes 262176 | tf_op jit(solution)/shard_map/ppermute | solution.py:651
  43.0 3.6 %query_projection.1 = (bf16[256,768]{1,0:T(8,128)(2,1)}, bf16[256,768]{1,0:T(8,128)(2,1)}) custom-call(s32[2]{0:T(128)} %pad_add_fusion.1.scalars, bf16[256,768]{1,0:T(8,128)(2,1)} %bitcast.77, f32[16,768]{1,0:T(8,128)} %bitcast.84, bf16[384,768]{1,0:T(8,128)(2,1)} %refs_6_.1, bf16[384,768]{1,0:T(8,128)(2,1)} %copy-done.27), custom_call_target="tpu_custom_call" | custom-call | flops 1000000000 | tf_op jit(solution)/shard_map/query_projection/pallas_call | solution.py:882
  46.7 7.9 %collective-permute-done.14.refs_3_ = bf16[2,2,1,2,128,256]{5,4,3,2,1,0:T(8,128)(2,1)S(1)} collective-permute-done((bf16[2,2,1,2,128,256]{5,4,3,2,1,0:T(8,128)(2,1)S(1)}, bf16[2,2,1,2,128,256]{5,4,3,2,1,0:T(8,128)(2,1)S(1)}, u32[]{:S(2)}, u32[]{:S(2)}) %collective-permute-start.14) | collective-permute-done | bytes 524320 | tf_op jit(solution)/shard_map/ppermute | solution.py:651
  55.8 6.4 %path_keys.1 = (bf16[2,384,768]{2,1,0:T(8,128)(2,1)}, bf16[768,768]{1,0:T(8,128)(2,1)}, bf16[768,768]{1,0:T(8,128)(2,1)}, s32[12]{0:T(128)}) custom-call(s32[12]{0:T(128)} %pad_add_fusion.scalars, bf16[2,2,2,1,144,256]{5,4,3,2,1,0:T(8,128)(2,1)} %copy-done.10, bf16[2,2,2,1,144,256]{5,4,3,2,1,0:T(8,128)(2,1)} %copy-done.29, ...), custom_call_target="tpu_custom_call" | custom-call | flops 6000000000 | tf_op jit(solution)/shard_map/path_keys/pallas_call | solution.py:893
  62.2 8.7 %attend.1 = (bf16[12,256,384]{2,1,0:T(8,128)(2,1)}, f32[256,768]{1,0:T(8,128)}) custom-call(s32[12]{0:T(128)} %pad_add_fusion.scalars, f32[16,12]{1,0:T(8,128)} %reshape_squeeze.3.table, bf16[256,768]{1,0:T(8,128)(2,1)} %get-tuple-element.195.query_low, bf16[256,768]{1,0:T(8,128)(2,1)} %get-tuple-element.196.query_segment, ...), custom_call_target="tpu_custom_call" | custom-call | flops 11000000512 | tf_op jit(solution)/shard_map/attend/pallas_call | solution.py:925
  70.9 20.2 %feed_forward.1 = (bf16[2,64,768]{2,1,0:T(8,128)(2,1)}, bf16[2,64,768]{2,1,0:T(8,128)(2,1)}, f32[256,768]{1,0:T(8,128)}, bf16[256,768]{1,0:T(8,128)(2,1)}, bf16[...) custom-call(s32[12]{0:T(128)} %pad_add_fusion.scalars, ...), custom_call_target="tpu_custom_call" | custom-call | flops 20999999488 | tf_op jit(solution)/shard_map/feed_forward/pallas_call | solution.py:948
  91.7 5.3 %attend_back.2 = (bf16[256,256]{1,0:T(8,128)(2,1)}, bf16[768,256]{1,0:T(8,128)(2,1)}, bf16[768,256]{1,0:T(8,128)(2,1)}, f32[8,256]{1,0:T(8,128)}, f32[4,16,384]{2,1,0:T(8,128)}) custom-call(s32[12]{0:T(128)} %pad_add_fusion.scalars, bf16[256,768]{1,0:T(8,128)(2,1)} %get-tuple-element.195.query_low, bf16[256,768]{1,0:T(8,128)(2,1)} %get-tuple-element.196.query_segment, ...), custom_call_target="tpu_custom_call" | custom-call | flops 3000000000 | tf_op jit(solution)/shard_map/attend_back/pallas_call | solution.py:984
  103.2 8.4 %attend_back.3 = (bf16[256,512]{1,0:T(8,128)(2,1)}, bf16[768,512]{1,0:T(8,128)(2,1)}, bf16[768,512]{1,0:T(8,128)(2,1)}, f32[8,512]{1,0:T(8,128)}, f32[8,16,384]{2,1,0:T(8,128)}) custom-call(s32[12]{0:T(128)} %pad_add_fusion.scalars, bf16[256,768]{1,0:T(8,128)(2,1)} %get-tuple-element.195.query_low, bf16[256,768]{1,0:T(8,128)(2,1)} %get-tuple-element.196.query_segment, ...), custom_call_target="tpu_custom_call" | custom-call | flops 3000000000 | tf_op jit(solution)/shard_map/attend_back/pallas_call | solution.py:984
  111.6 9.0 %weight_gradients.1 = (bf16[2,2,2,208,384]{4,3,2,1,0:T(8,128)(2,1)}, bf16[2,2,2,208,384]{4,3,2,1,0:T(8,128)(2,1)}, bf16[2,2,2,208,384]{4,3,2,1,0:T(8,128)(2,1)}, bf16[2,2,2,208,384]{4,3,2,1,0:T(8,128)(2,1)}) custom-call(s32[12]{0:T(128)} %pad_add_fusion.scalars, bf16[256,768]{1,0:T(8,128)(2,1)} %bitcast.79, bf16[768,768]{1,0:T(8,128)(2,1)} %bitcast.95, ...), custom_call_target="tpu_custom_call" | custom-call | flops 3000000000 | tf_op jit(solution)/shard_map/weight_gradients/pallas_call | solution.py:1037
  130.0 8.8 %tree_gradients.1 = (f32[2,64,768]{2,1,0:T(8,128)}, f32[2,64,768]{2,1,0:T(8,128)}, bf16[2,2,2,256,384]{4,3,2,1,0:T(8,128)(2,1)}, bf16[2,2,2,256,384]{4,3,2,1,0:T(8,128)(2,1)}) custom-call(s32[12]{0:T(128)} %pad_add_fusion.scalars, s32[12]{0:T(128)} %get-tuple-element.219.found, f32[256,768]{1,0:T(8,128)} %get-tuple-element.252.d_mid_in, ...), custom_call_target="tpu_custom_call" | custom-call | flops 3000000000 | tf_op jit(solution)/shard_map/tree_gradients/pallas_call | solution.py:1051
  157.5 7.5 %collective-permute-done.33 = bf16[1,1,1,1,384,384]{5,4,3,2,1,0:T(8,128)(2,1)S(1)} collective-permute-done((bf16[1,1,1,1,384,384]{5,4,3,2,1,0:T(8,128)(2,1)S(1)}, bf16[1,1,1,1,384,384]{5,4,3,2,1,0:T(8,128)(2,1)S(1)}, u32[]{:S(2)}, u32[]{:S(2)}) %collective-permute-start.33) | collective-permute-done | bytes 294944 | tf_op jit(solution)/shard_map/ppermute | solution.py:651
  165.5 13.6 %collective-permute-done.37 = bf16[1,1,1,1,384,384]{5,4,3,2,1,0:T(8,128)(2,1)S(1)} collective-permute-done((bf16[1,1,1,1,384,384]{5,4,3,2,1,0:T(8,128)(2,1)S(1)}, bf16[1,1,1,1,384,384]{5,4,3,2,1,0:T(8,128)(2,1)S(1)}, u32[]{:S(2)}, u32[]{:S(2)}) %collective-permute-start.37) | collective-permute-done | bytes 294944 | tf_op jit(solution)/shard_map/ppermute | solution.py:651
  193.0 4.3 %collective-permute-done.34 = bf16[2,2,1,1,176,384]{5,4,3,2,1,0:T(8,128)(2,1)S(1)} collective-permute-done((bf16[2,2,1,1,176,384]{5,4,3,2,1,0:T(8,128)(2,1)S(1)}, bf16[2,2,1,1,176,384]{5,4,3,2,1,0:T(8,128)(2,1)S(1)}, u32[]{:S(2)}, u32[]{:S(2)}) %collective-permute-start.34) | collective-permute-done | bytes 540704 | tf_op jit(solution)/shard_map/ppermute | solution.py:651
  197.3 4.6 %collective-permute-done.35 = bf16[2,1,1,2,176,384]{5,4,3,2,1,0:T(8,128)(2,1)S(1)} collective-permute-done((bf16[2,1,1,2,176,384]{5,4,3,2,1,0:T(8,128)(2,1)S(1)}, bf16[2,1,1,2,176,384]{5,4,3,2,1,0:T(8,128)(2,1)S(1)}, u32[]{:S(2)}, u32[]{:S(2)}) %collective-permute-start.35) | collective-permute-done | bytes 540704 | tf_op jit(solution)/shard_map/ppermute | solution.py:651
  209.9 6.2 %collective-permute-done.38 = bf16[2,1,1,1,176,384]{5,4,3,2,1,0:T(8,128)(2,1)S(1)} collective-permute-done((bf16[2,1,1,1,176,384]{5,4,3,2,1,0:T(8,128)(2,1)S(1)}, bf16[2,1,1,1,176,384]{5,4,3,2,1,0:T(8,128)(2,1)S(1)}, u32[]{:S(2)}, u32[]{:S(2)}) %collective-permute-start.38) | collective-permute-done | bytes 270368 | tf_op jit(solution)/shard_map/ppermute | solution.py:651
  216.2 5.7 %collective-permute-start.44 = (bf16[1,1,1,1,464,384]{5,4,3,2,1,0:T(8,128)(2,1)S(1)}, bf16[1,1,1,1,464,384]{5,4,3,2,1,0:T(8,128)(2,1)S(1)}, u32[]{:S(2)}, u32[]{:S(2)}) collective-permute-start(bf16[1,1,1,1,464,384]{5,4,3,2,1,0:T(8,128)(2,1)S(1)} %pad_maximum_fusion.14), channel_id=1, source_target_pairs={{0,8},{1,9},{2,10},{3,11},{4,12},{5,13},{6,14},{7,15},{8,0},{9,1},... | collective-permute-start | bytes 1069064 | tf_op jit(solution)/shard_map/ppermute | solution.py:651
  225.1 7.6 %collective-permute-done.44 = bf16[1,1,1,1,464,384]{5,4,3,2,1,0:T(8,128)(2,1)S(1)} collective-permute-done((bf16[1,1,1,1,464,384]{5,4,3,2,1,0:T(8,128)(2,1)S(1)}, bf16[1,1,1,1,464,384]{5,4,3,2,1,0:T(8,128)(2,1)S(1)}, u32[]{:S(2)}, u32[]{:S(2)}) %collective-permute-start.44) | collective-permute-done | bytes 356384 | tf_op jit(solution)/shard_map/ppermute | solution.py:651
  234.6 9.9 %collective-permute-done.48 = bf16[1,1,1,1,208,384]{5,4,3,2,1,0:T(8,128)(2,1)S(1)} collective-permute-done((bf16[1,1,1,1,208,384]{5,4,3,2,1,0:T(8,128)(2,1)S(1)}, bf16[1,1,1,1,208,384]{5,4,3,2,1,0:T(8,128)(2,1)S(1)}, u32[]{:S(2)}, u32[]{:S(2)}) %collective-permute-start.48) | collective-permute-done | bytes 159776 | tf_op jit(solution)/shard_map/ppermute | solution.py:651
  246.2 4.8 %collective-permute-start.49 = (bf16[2,1,1,1,80,384]{5,4,3,2,1,0:T(8,128)(2,1)S(1)}, bf16[2,1,1,1,80,384]{5,4,3,2,1,0:T(8,128)(2,1)S(1)}, u32[]{:S(2)}, u32[]{:S(2)}) collective-permute-start(bf16[2,1,1,1,80,384]{5,4,3,2,1,0:T(8,128)(2,1)S(1)} %get-tuple-element.285), channel_id=1, source_target_pairs={{0,4},{1,5},{2,6},{3,7},{4,0},{5,1},{6,2},{7,3},{8,12},{9,13},{10,... | collective-permute-start | bytes 368648 | tf_op jit(solution)/shard_map/ppermute | solution.py:651
  265.8 3.6 %collective-permute-start.60 = (bf16[2,1,2,2,48,384]{5,4,3,2,1,0:T(8,128)(2,1)S(1)}, bf16[2,1,2,2,48,384]{5,4,3,2,1,0:T(8,128)(2,1)S(1)}, u32[]{:S(2)}, u32[]{:S(2)}) collective-permute-start(bf16[2,1,2,2,48,384]{5,4,3,2,1,0:T(8,128)(2,1)S(1)} %pad_maximum_fusion.19.refs_4_), channel_id=1, source_target_pairs={{0,4},{1,5},{2,6},{3,7},{4,0},{5,1},{6,2},{7,3},{8,12},{9,13},{10,... | collective-permute-start | bytes 884744 | tf_op jit(solution)/shard_map/ppermute | solution.py:651
  271.6 7.4 %feed_spread.1 = (f32[1536,768]{1,0:T(8,128)}, f32[384,3072]{1,0:T(8,128)}) custom-call(s32[2]{0:T(128)} %pad_add_fusion.1.scalars, bf16[2,2,2,1,128,384]{5,4,3,2,1,0:T(8,128)(2,1)} %copy-done.7, bf16[2,2,2,1,128,384]{5,4,3,2,1,0:T(8,128)(2,1)} %copy-done.22, bf16[2,2,1,2,128,384]{5,4,3,2,1,0:T(8,128)(2,1)} %copy-done.8, ...), custom_call_target="tpu_custom_call" | custom-call | flops 7000000000 | tf_op jit(solution)/shard_map/feed_spread/pallas_call | solution.py:1093
  280.7 4.8 %later_spread.1 = (f32[384,768]{1,0:T(8,128)}, f32[384,768]{1,0:T(8,128)}, f32[384,768]{1,0:T(8,128)}, f32[384,768]{1,0:T(8,128)}, f32[1536]{0:T(1024)}, /*index...) custom-call(s32[2]{0:T(128)} %pad_add_fusion.1.scalars, ...), custom_call_target="tpu_custom_call" | custom-call | flops 4000000000 | tf_op jit(solution)/shard_map/later_spread/pallas_call | solution.py:1106
  (299 shorter events, 111.2 us)
Async XLA Ops:
  3.6 15.1 %collective-permute-start.1 = (bf16[384,768]{1,0:T(8,128)(2,1)}, bf16[384,768]{1,0:T(8,128)(2,1)S(1)}, u32[]{:S(2)}, u32[]{:S(2)}) collective-permute-start(bf16[384,768]{1,0:T(8,128)(2,1)} %refs_6_.1), channel_id=1, source_target_pairs={{0,16},{16,0},{1,17},{17,1},{2,18},{18,2},{3,19},{19,3},{4,20},{20... | collective-permute-start | bytes 1769480 | tf_op jit(solution)/shard_map/ppermute | solution.py:808
  4.2 14.6 %collective-permute-start.2 = (bf16[384,768]{1,0:T(8,128)(2,1)}, bf16[384,768]{1,0:T(8,128)(2,1)}, u32[]{:S(2)}, u32[]{:S(2)}) collective-permute-start(bf16[384,768]{1,0:T(8,128)(2,1)} %refs_8_.1), channel_id=1, source_target_pairs={{0,16},{16,0},{1,17},{17,1},{2,18},{18,2},{3,19},{19,3},{4,20},{20... | collective-permute-start | bytes 1769480 | tf_op jit(solution)/shard_map/ppermute | solution.py:808
  4.2 14.4 %collective-permute-start = (bf16[1,1,1,1,144,768]{5,4,3,2,1,0:T(8,128)(2,1)S(1)}, bf16[1,1,1,1,144,768]{5,4,3,2,1,0:T(8,128)(2,1)S(1)}, u32[]{:S(2)}, u32[]{:S(2)}) collective-permute-start(bf16[1,1,1,1,144,768]{5,4,3,2,1,0:T(8,128)(2,1)S(1)} %bitcast.71), channel_id=1, source_target_pairs={{0,8},{1,9},{2,10},{3,11},{4,12},{5,13},{6,14},{7,15},{8,0},{9,1},... | collective-permute-start | bytes 663560 | tf_op jit(solution)/shard_map/ppermute | solution.py:651
  39.0 16.0 %collective-permute-start.16 = (bf16[1536,768]{1,0:T(8,128)(2,1)}, bf16[1536,768]{1,0:T(8,128)(2,1)}, u32[]{:S(2)}, u32[]{:S(2)}) collective-permute-start(bf16[1536,768]{1,0:T(8,128)(2,1)} %refs_4_), channel_id=1, source_target_pairs={{0,16},{16,0},{1,17},{17,1},{2,18},{18,2},{3,19},{19,3},{4,20},{20... | collective-permute-start | bytes 7077896 | tf_op jit(solution)/shard_map/ppermute | solution.py:808
  39.1 15.9 %collective-permute-start.13 = (bf16[2,2,2,1,144,256]{5,4,3,2,1,0:T(8,128)(2,1)S(1)}, bf16[2,2,2,1,144,256]{5,4,3,2,1,0:T(8,128)(2,1)S(1)}, u32[]{:S(2)}, u32[]{:S(2)}) collective-permute-start(bf16[2,2,2,1,144,256]{5,4,3,2,1,0:T(8,128)(2,1)S(1)} %pad_maximum_fusion.3.refs_0_), channel_id=1, source_target_pairs={{0,1},{1,0},{2,3},{3,2},{4,5},{5,4},{6,7},{7,6},{8,9},{9,8},{10,11... | collective-permute-start | bytes 1769480 | tf_op jit(solution)/shard_map/ppermute | solution.py:651
  40.6 14.0 %collective-permute-start.14 = (bf16[2,2,1,2,128,256]{5,4,3,2,1,0:T(8,128)(2,1)S(1)}, bf16[2,2,1,2,128,256]{5,4,3,2,1,0:T(8,128)(2,1)S(1)}, u32[]{:S(2)}, u32[]{:S(2)}) collective-permute-start(bf16[2,2,1,2,128,256]{5,4,3,2,1,0:T(8,128)(2,1)S(1)} %pad_maximum_fusion.5.refs_2_), channel_id=1, source_target_pairs={{0,2},{1,3},{2,0},{3,1},{4,6},{5,7},{6,4},{7,5},{8,10},{9,11},{10,... | collective-permute-start | bytes 1572872 | tf_op jit(solution)/shard_map/ppermute | solution.py:651
  99.8 20.8 %collective-permute-start.19 = (bf16[2,2,2,1,128,384]{5,4,2,1,0,3:T(8,128)(2,1)}, bf16[2,2,2,1,128,384]{5,4,2,1,0,3:T(8,128)(2,1)S(1)}, u32[]{:S(2)}, u32[]{:S(2)}) collective-permute-start(bf16[2,2,2,1,128,384]{5,4,2,1,0,3:T(8,128)(2,1)} %get-tuple-element.228), channel_id=1, source_target_pairs={{0,1},{1,0},{2,3},{3,2},{4,5},{5,4},{6,7},{7,6},{8,9},{9,8},{10,11... | collective-permute-start | bytes 2359304 | tf_op jit(solution)/shard_map/ppermute | solution.py:651
  101.2 21.9 %collective-permute-start.20 = (bf16[2,2,1,2,128,384]{5,4,3,1,0,2:T(8,128)(2,1)S(1)}, bf16[2,2,1,2,128,384]{5,4,3,1,0,2:T(8,128)(2,1)S(1)}, u32[]{:S(2)}, u32[]{:S(2)}) collective-permute-start(bf16[2,2,1,2,128,384]{5,4,3,1,0,2:T(8,128)(2,1)S(1)} %get-tuple-element.229), channel_id=1, source_target_pairs={{0,2},{1,3},{2,0},{3,1},{4,6},{5,7},{6,4},{7,5},{8,10},{9,11},{10,... | collective-permute-start | bytes 2359304 | tf_op jit(solution)/shard_map/ppermute | solution.py:651
  101.9 22.6 %collective-permute-start.21 = (bf16[2,1,2,2,128,384]{5,4,3,2,1,0:T(8,128)(2,1)S(1)}, bf16[2,1,2,2,128,384]{5,4,3,2,1,0:T(8,128)(2,1)}, u32[]{:S(2)}, u32[]{:S(2)}) collective-permute-start(bf16[2,1,2,2,128,384]{5,4,3,2,1,0:T(8,128)(2,1)S(1)} %get-tuple-element.230), channel_id=1, source_target_pairs={{0,4},{1,5},{2,6},{3,7},{4,0},{5,1},{6,2},{7,3},{8,12},{9,13},{10,... | collective-permute-start | bytes 2359304 | tf_op jit(solution)/shard_map/ppermute | solution.py:651
  126.8 15.3 %collective-permute-start.25 = (bf16[2,2,2,208,384]{4,3,2,1,0:T(8,128)(2,1)}, bf16[2,2,2,208,384]{4,3,2,1,0:T(8,128)(2,1)}, u32[]{:S(2)}, u32[]{:S(2)}) collective-permute-start(bf16[2,2,2,208,384]{4,3,2,1,0:T(8,128)(2,1)} %get-tuple-element.258), channel_id=1, source_target_pairs={{0,16},{16,0},{1,17},{17,1},{2,18},{18,2},{3,19},{19,3},{4,20},{20... | collective-permute-start | bytes 3833864 | tf_op jit(solution)/shard_map/ppermute | solution.py:1068
  126.8 15.3 %collective-permute-start.26 = (bf16[2,2,2,208,384]{4,3,2,1,0:T(8,128)(2,1)}, bf16[2,2,2,208,384]{4,3,2,1,0:T(8,128)(2,1)S(1)}, u32[]{:S(2)}, u32[]{:S(2)}) collective-permute-start(bf16[2,2,2,208,384]{4,3,2,1,0:T(8,128)(2,1)} %get-tuple-element.259), channel_id=1, source_target_pairs={{0,16},{16,0},{1,17},{17,1},{2,18},{18,2},{3,19},{19,3},{4,20},{20... | collective-permute-start | bytes 3833864 | tf_op jit(solution)/shard_map/ppermute | solution.py:1068
  150.9 14.1 %collective-permute-start.33 = (bf16[1,1,1,1,384,384]{5,4,3,2,1,0:T(8,128)(2,1)S(1)}, bf16[1,1,1,1,384,384]{5,4,3,2,1,0:T(8,128)(2,1)S(1)}, u32[]{:S(2)}, u32[]{:S(2)}) collective-permute-start(bf16[1,1,1,1,384,384]{5,4,3,2,1,0:T(8,128)(2,1)S(1)} %pad_maximum_fusion.17), channel_id=1, source_target_pairs={{0,8},{1,9},{2,10},{3,11},{4,12},{5,13},{6,14},{7,15},{8,0},{9,1},... | collective-permute-start | bytes 884744 | tf_op jit(solution)/shard_map/ppermute | solution.py:651
  154.0 26.6 %collective-permute-start.32 = (bf16[2,1,2,2,112,384]{5,4,3,2,1,0:T(8,128)(2,1)S(1)}, bf16[2,1,2,2,112,384]{5,4,3,2,1,0:T(8,128)(2,1)S(1)}, u32[]{:S(2)}, u32[]{:S(2)}) collective-permute-start(bf16[2,1,2,2,112,384]{5,4,3,2,1,0:T(8,128)(2,1)S(1)} %maximum_bitcast_fusion.4), channel_id=1, source_target_pairs={{0,4},{1,5},{2,6},{3,7},{4,0},{5,1},{6,2},{7,3},{8,12},{9,13},{10,... | collective-permute-start | bytes 2064392 | tf_op jit(solution)/shard_map/ppermute | solution.py:651
  155.3 25.5 %collective-permute-start.30 = (bf16[2,2,2,1,176,384]{5,4,3,2,1,0:T(8,128)(2,1)S(1)}, bf16[2,2,2,1,176,384]{5,4,3,2,1,0:T(8,128)(2,1)S(1)}, u32[]{:S(2)}, u32[]{:S(2)}) collective-permute-start(bf16[2,2,2,1,176,384]{5,4,3,2,1,0:T(8,128)(2,1)S(1)} %maximum_bitcast_fusion.1), channel_id=1, source_target_pairs={{0,1},{1,0},{2,3},{3,2},{4,5},{5,4},{6,7},{7,6},{8,9},{9,8},{10,11... | collective-permute-start | bytes 3244040 | tf_op jit(solution)/shard_map/ppermute | solution.py:651
  156.0 25.2 %collective-permute-start.31 = (bf16[2,2,1,2,176,384]{5,4,3,2,1,0:T(8,128)(2,1)S(1)}, bf16[2,2,1,2,176,384]{5,4,3,2,1,0:T(8,128)(2,1)S(1)}, u32[]{:S(2)}, u32[]{:S(2)}) collective-permute-start(bf16[2,2,1,2,176,384]{5,4,3,2,1,0:T(8,128)(2,1)S(1)} %maximum_bitcast_fusion.2), channel_id=1, source_target_pairs={{0,2},{1,3},{2,0},{3,1},{4,6},{5,7},{6,4},{7,5},{8,10},{9,11},{10,... | collective-permute-start | bytes 3244040 | tf_op jit(solution)/shard_map/ppermute | solution.py:651
  184.2 18.2 %collective-permute-start.42 = (bf16[2,1,1,1,128,384]{5,4,3,2,1,0:T(8,128)(2,1)S(1)}, bf16[2,1,1,1,128,384]{5,4,3,2,1,0:T(8,128)(2,1)S(1)}, u32[]{:S(2)}, u32[]{:S(2)}) collective-permute-start(bf16[2,1,1,1,128,384]{5,4,3,2,1,0:T(8,128)(2,1)S(1)} %get-tuple-element.330), channel_id=1, source_target_pairs={{0,1},{1,0},{2,3},{3,2},{4,5},{5,4},{6,7},{7,6},{8,9},{9,8},{10,11... | collective-permute-start | bytes 589832 | tf_op jit(solution)/shard_map/ppermute | solution.py:651
  185.8 18.8 %collective-permute-start.41 = (bf16[2,1,1,1,128,384]{5,4,3,2,1,0:T(8,128)(2,1)S(1)}, bf16[2,1,1,1,128,384]{5,4,3,2,1,0:T(8,128)(2,1)S(1)}, u32[]{:S(2)}, u32[]{:S(2)}) collective-permute-start(bf16[2,1,1,1,128,384]{5,4,3,2,1,0:T(8,128)(2,1)S(1)} %get-tuple-element.331), channel_id=1, source_target_pairs={{0,4},{1,5},{2,6},{3,7},{4,0},{5,1},{6,2},{7,3},{8,12},{9,13},{10,... | collective-permute-start | bytes 589832 | tf_op jit(solution)/shard_map/ppermute | solution.py:651
  191.6 33.1 %collective-permute-start.47 = (bf16[2,1,2,1,128,384]{5,4,3,2,1,0:T(8,128)(2,1)S(1)}, bf16[2,1,2,1,128,384]{5,4,3,2,1,0:T(8,128)(2,1)S(1)}, u32[]{:S(2)}, u32[]{:S(2)}) collective-permute-start(bf16[2,1,2,1,128,384]{5,4,3,2,1,0:T(8,128)(2,1)S(1)} %pad_maximum_fusion.13), channel_id=1, source_target_pairs={{0,1},{1,0},{2,3},{3,2},{4,5},{5,4},{6,7},{7,6},{8,9},{9,8},{10,11... | collective-permute-start | bytes 1179656 | tf_op jit(solution)/shard_map/ppermute | solution.py:651
  202.5 20.9 %collective-permute-start.46 = (bf16[2,1,1,2,128,384]{5,4,3,2,1,0:T(8,128)(2,1)S(1)}, bf16[2,1,1,2,128,384]{5,4,3,2,1,0:T(8,128)(2,1)S(1)}, u32[]{:S(2)}, u32[]{:S(2)}) collective-permute-start(bf16[2,1,1,2,128,384]{5,4,3,2,1,0:T(8,128)(2,1)S(1)} %pad_maximum_fusion.12), channel_id=1, source_target_pairs={{0,4},{1,5},{2,6},{3,7},{4,0},{5,1},{6,2},{7,3},{8,12},{9,13},{10,... | collective-permute-start | bytes 1179656 | tf_op jit(solution)/shard_map/ppermute | solution.py:651
  204.6 17.3 %collective-permute-start.45 = (bf16[2,2,1,1,128,384]{5,4,3,2,1,0:T(8,128)(2,1)S(1)}, bf16[2,2,1,1,128,384]{5,4,3,2,1,0:T(8,128)(2,1)S(1)}, u32[]{:S(2)}, u32[]{:S(2)}) collective-permute-start(bf16[2,2,1,1,128,384]{5,4,3,2,1,0:T(8,128)(2,1)S(1)} %pad_maximum_fusion.11), channel_id=1, source_target_pairs={{0,2},{1,3},{2,0},{3,1},{4,6},{5,7},{6,4},{7,5},{8,10},{9,11},{10,... | collective-permute-start | bytes 1179656 | tf_op jit(solution)/shard_map/ppermute | solution.py:651
  216.2 16.4 %collective-permute-start.44 = (bf16[1,1,1,1,464,384]{5,4,3,2,1,0:T(8,128)(2,1)S(1)}, bf16[1,1,1,1,464,384]{5,4,3,2,1,0:T(8,128)(2,1)S(1)}, u32[]{:S(2)}, u32[]{:S(2)}) collective-permute-start(bf16[1,1,1,1,464,384]{5,4,3,2,1,0:T(8,128)(2,1)S(1)} %pad_maximum_fusion.14), channel_id=1, source_target_pairs={{0,8},{1,9},{2,10},{3,11},{4,12},{5,13},{6,14},{7,15},{8,0},{9,1},... | collective-permute-start | bytes 1069064 | tf_op jit(solution)/shard_map/ppermute | solution.py:651
  222.0 34.0 %collective-permute-start.52 = (bf16[2,2,2,1,128,384]{5,4,3,2,1,0:T(8,128)(2,1)S(1)}, bf16[2,2,2,1,128,384]{5,4,3,2,1,0:T(8,128)(2,1)S(1)}, u32[]{:S(2)}, u32[]{:S(2)}) collective-permute-start(bf16[2,2,2,1,128,384]{5,4,3,2,1,0:T(8,128)(2,1)S(1)} %pad_maximum_fusion.refs_0_), channel_id=1, source_target_pairs={{0,1},{1,0},{2,3},{3,2},{4,5},{5,4},{6,7},{7,6},{8,9},{9,8},{10,11... | collective-permute-start | bytes 2359304 | tf_op jit(solution)/shard_map/ppermute | solution.py:651
  223.5 32.5 %collective-permute-start.53 = (bf16[2,2,1,2,128,384]{5,4,3,2,1,0:T(8,128)(2,1)S(1)}, bf16[2,2,1,2,128,384]{5,4,3,2,1,0:T(8,128)(2,1)S(1)}, u32[]{:S(2)}, u32[]{:S(2)}) collective-permute-start(bf16[2,2,1,2,128,384]{5,4,3,2,1,0:T(8,128)(2,1)S(1)} %pad_maximum_fusion.1.refs_2_), channel_id=1, source_target_pairs={{0,2},{1,3},{2,0},{3,1},{4,6},{5,7},{6,4},{7,5},{8,10},{9,11},{10,... | collective-permute-start | bytes 2359304 | tf_op jit(solution)/shard_map/ppermute | solution.py:651
  224.8 31.3 %collective-permute-start.54 = (bf16[2,1,2,2,128,384]{5,4,3,2,1,0:T(8,128)(2,1)S(1)}, bf16[2,1,2,2,128,384]{5,4,3,2,1,0:T(8,128)(2,1)S(1)}, u32[]{:S(2)}, u32[]{:S(2)}) collective-permute-start(bf16[2,1,2,2,128,384]{5,4,3,2,1,0:T(8,128)(2,1)S(1)} %pad_maximum_fusion.2.refs_4_), channel_id=1, source_target_pairs={{0,4},{1,5},{2,6},{3,7},{4,0},{5,1},{6,2},{7,3},{8,12},{9,13},{10,... | collective-permute-start | bytes 2359304 | tf_op jit(solution)/shard_map/ppermute | solution.py:651
  (71 other events, 658.5 us)

commit v4 on v3

--- a/solution.py
+++ b/solution.py
@@ -698,24 +698,26 @@
             part_of(entry, route[step], 0) + send(other, route[step])
             for entry, other, route in zip(held, ready, routes_out)
         ]
-    for bit in extra_bits()[::-1]:
-        (ready,) = yield [jnp.concatenate([part_of(entry, bit, 1) for entry in held], axis=-2)]
-        arrived = send(ready, bit)
-        start, later = 0, []
-        for entry in held:
-            height = entry.shape[-2]
-            later.append(part_of(entry, bit, 0) + arrived[..., start : start + height, :])
-            start += height
-        held = later
-    shares = held
-    joined = jnp.concatenate([entry[..., :rows, :] for entry, rows in zip(held, keep)], axis=-2)
-    for bit in extra_bits():
-        (ready,) = yield [joined]
-        joined = jnp.concatenate([joined, send(ready, bit)], axis=axis_of(bit))
-    start, held = 0, []
-    for rows in keep:
-        held.append(joined[..., start : start + rows, :])
-        start += rows
+    (far,) = extra_bits()
+    both = [[part_of(entry, far, which) for entry in held] for which in range(2)]
+    leaving = [entry[..., :rows, :] for which in range(2) for entry, rows in zip(both[which], keep)]
+    leaving += [entry[..., rows:, :] for entry, rows in zip(both[1], keep) if rows < entry.shape[-2]]
+    (ready,) = yield [jnp.concatenate(leaving, axis=-2)]
+    arrived, start, received = send(ready, far), 0, []
+    for entry in leaving:
+        received.append(arrived[..., start : start + entry.shape[-2], :])
+        start += entry.shape[-2]
+    count = len(keep)
+    shares = [
+        entry[..., rows:, :] + other for entry, rows, other in zip(both[0], keep, received[2 * count :])
+    ]
+    held = [
+        jnp.concatenate(
+            [both[0][i][..., :rows, :] + received[count + i], both[1][i][..., :rows, :] + received[i]],
+            axis=axis_of(far),
+        )
+        for i, rows in enumerate(keep)
+    ]
     for step in (2, 1):
         ready = yield held
         held = [
@@ -1080,9 +1082,8 @@
         lower = [route_sum(0, part) for part in range(3)]
         upper = [route_sum(1, part) for part in range(3)]
         later_rounds = Rounds(sum_rounds(lower, upper, heights))
-        for _ in range(5):
-            advance_after(later_rounds, feed_rounds)
-            feed_rounds.advance(feed_rounds.pending)
+        for _ in range(4):
+            advance_together([feed_rounds, later_rounds])
         advance_together([later_rounds])
         feed_done = advance_together([later_rounds], feed_rounds.result[0])
         advance_together([later_rounds])
@@ -1101,7 +1102,7 @@
             cost_estimate=cost(7),
         )(early, *feed_done)
         later_done, shares = later_rounds.result
-        arrived = [share.reshape(share.shape[-2:])[rows:] for share, rows in zip(shares, heights)]
+        arrived = [share.reshape(share.shape[-2:]) for share in shares]
         tree_grad = jnp.concatenate(arrived, axis=0)
         spread_out = pl.pallas_call(
             later_spread_kernel,

time: 287 us -> 277 us (0.965)
  starting transfers between devices: 72.3 us -> 55.5 us
  waiting for transfers between devices: 91.4 us -> 99.2 us
    ppermute x50 -> x48, starting transfers between devices: 70.3 us -> 53.5 us  [send(): return lax.ppermute(inputs, 'dp', [(i, i ^ 1 << bit) for i in range(count)])]
    ppermute x50 -> x48, waiting for transfers between devices: 91.4 us -> 99.2 us  [send(): return lax.ppermute(inputs, 'dp', [(i, i ^ 1 << bit) for i in range(count)])]
  transfers between devices with their start and end apart: 61 -> 59, of which waited for: 26 -> 33; matrix products, arithmetic and copies ran while one was open for 10% -> 9% of each run, Pallas kernels for 15% -> 15%
where the time goes in v4:
time: 277 us; the launch traced here: 276 us
  waiting for transfers between devices  99.2 us (36%)
  Pallas kernels  82.6 us (30%)
  starting transfers between devices  55.5 us (20%)
  other arithmetic  20 us (7%)
  local copies, waits for them, and re-layouts  16.9 us (6%)
    ppermute x48, waiting for transfers between devices, send(): return lax.ppermute(inputs, 'dp', [(i, i ^ 1 << bit) for i in range(count)])  99.2 us
    ppermute x48, starting transfers between devices, send(): return lax.ppermute(inputs, 'dp', [(i, i ^ 1 << bit) for i in range(count)])  53.5 us
    pallas_call x1, Pallas kernels, shards(): pl.pallas_call(functools.partial(feed_kernel, pieces, run), out_shape=[sh...  20.2 us
    pallas_call x2, Pallas kernels, attend_back(): pl.pallas_call(functools.partial(back_kernel, run, slots), grid=(pair_cou...  13.7 us
    pallas_call x1, Pallas kernels, shards(): pl.pallas_call(functools.partial(weights_kernel, pieces), out_shape=grad_...  8.97 us
    pallas_call x1, Pallas kernels, shards(): pl.pallas_call(functools.partial(tree_kernel, pieces, run, slots), out_sh...  8.77 us
    pallas_call x1, Pallas kernels, shards(): pl.pallas_call(functools.partial(attend_kernel, run, slots), grid=(pairs,...  8.72 us
    pallas_call x1, Pallas kernels, shards(): pl.pallas_call(feed_spread_kernel, out_shape=(shape(w_outer.shape, f32),...  7.36 us
  transfers between devices with their start and end apart: 59, of which 33 were waited for; matrix products, arithmetic and copies ran while one was open for 9% of the time, Pallas kernels for 15%

profile of v4, /device:TPU:0, one launch (start us, length us, event | category | flops | bytes accessed | tf_op | source)
XLA Modules:
  0.0 276.1 jit_solution(16220547991347845943)
XLA Ops:
  4.2 4.0 %collective-permute-start = (bf16[1,1,1,1,144,768]{5,4,3,2,1,0:T(8,128)(2,1)S(1)}, bf16[1,1,1,1,144,768]{5,4,3,2,1,0:T(8,128)(2,1)S(1)}, u32[]{:S(2)}, u32[]{:S(2)}) collective-permute-start(bf16[1,1,1,1,144,768]{5,4,3,2,1,0:T(8,128)(2,1)S(1)} %bitcast.74), channel_id=1, source_target_pairs={{0,8},{1,9},{2,10},{3,11},{4,12},{5,13},{6,14},{7,15},{8,0},{9,1},... | collective-permute-start | bytes 663560 | tf_op jit(solution)/shard_map/ppermute | solution.py:651
  9.8 5.6 %concatenate.123 = bf16[6144]{0:T(1024)(128)(2,1)S(1)} concatenate(bf16[1536]{0:T(1024)(128)(2,1)} %param.34, bf16[384]{0:T(512)(128)(2,1)} %param.35, bf16[384]{0:T(512)(128)(2,1)} %param.36, bf16[384]{0:T(512)(128)(2,1)} %param.37, bf16[384]{0:T(512)(128)(2,1)} %param.38, bf16[384]{0:T(512)(128)(2,1)} %param.39, bf16[384]{0:T(512)(128)(2,1)} %param.40, bf16[384]{0:T(512)(128)(2,1)} %param.41, ...), dimensions={0} | concatenate | bytes 24576 | tf_op jit(solution)/shard_map/concatenate | solution.py:833
  15.5 3.2 %collective-permute-done = bf16[1,1,1,1,144,768]{5,4,3,2,1,0:T(8,128)(2,1)S(1)} collective-permute-done((bf16[1,1,1,1,144,768]{5,4,3,2,1,0:T(8,128)(2,1)S(1)}, bf16[1,1,1,1,144,768]{5,4,3,2,1,0:T(8,128)(2,1)S(1)}, u32[]{:S(2)}, u32[]{:S(2)}) %collective-permute-start) | collective-permute-done | bytes 221216 | tf_op jit(solution)/shard_map/ppermute | solution.py:651
  32.4 4.8 %collective-permute-done.9 = bf16[2,1,1,2,128,256]{5,4,3,2,1,0:T(8,128)(2,1)S(1)} collective-permute-done((bf16[2,1,1,2,128,256]{5,4,3,2,1,0:T(8,128)(2,1)S(1)}, bf16[2,1,1,2,128,256]{5,4,3,2,1,0:T(8,128)(2,1)S(1)}, u32[]{:S(2)}, u32[]{:S(2)}) %collective-permute-start.9) | collective-permute-done | bytes 262176 | tf_op jit(solution)/shard_map/ppermute | solution.py:651
  43.0 3.6 %query_projection.1 = (bf16[256,768]{1,0:T(8,128)(2,1)}, bf16[256,768]{1,0:T(8,128)(2,1)}) custom-call(s32[2]{0:T(128)} %pad_add_fusion.1.scalars, bf16[256,768]{1,0:T(8,128)(2,1)} %bitcast.84, f32[16,768]{1,0:T(8,128)} %bitcast.90, bf16[384,768]{1,0:T(8,128)(2,1)} %refs_6_.1, bf16[384,768]{1,0:T(8,128)(2,1)} %copy-done.27), custom_call_target="tpu_custom_call" | custom-call | flops 1000000000 | tf_op jit(solution)/shard_map/query_projection/pallas_call | solution.py:884
  46.7 7.9 %collective-permute-done.14.refs_3_ = bf16[2,2,1,2,128,256]{5,4,3,2,1,0:T(8,128)(2,1)S(1)} collective-permute-done((bf16[2,2,1,2,128,256]{5,4,3,2,1,0:T(8,128)(2,1)S(1)}, bf16[2,2,1,2,128,256]{5,4,3,2,1,0:T(8,128)(2,1)S(1)}, u32[]{:S(2)}, u32[]{:S(2)}) %collective-permute-start.14) | collective-permute-done | bytes 524320 | tf_op jit(solution)/shard_map/ppermute | solution.py:651
  55.8 6.4 %path_keys.1 = (bf16[2,384,768]{2,1,0:T(8,128)(2,1)}, bf16[768,768]{1,0:T(8,128)(2,1)}, bf16[768,768]{1,0:T(8,128)(2,1)}, s32[12]{0:T(128)}) custom-call(s32[12]{0:T(128)} %pad_add_fusion.scalars, bf16[2,2,2,1,144,256]{5,4,3,2,1,0:T(8,128)(2,1)} %copy-done.10, bf16[2,2,2,1,144,256]{5,4,3,2,1,0:T(8,128)(2,1)} %copy-done.29, ...), custom_call_target="tpu_custom_call" | custom-call | flops 6000000000 | tf_op jit(solution)/shard_map/path_keys/pallas_call | solution.py:895
  62.2 8.7 %attend.1 = (bf16[12,256,384]{2,1,0:T(8,128)(2,1)}, f32[256,768]{1,0:T(8,128)}) custom-call(s32[12]{0:T(128)} %pad_add_fusion.scalars, f32[16,12]{1,0:T(8,128)} %reshape_squeeze.3.table, bf16[256,768]{1,0:T(8,128)(2,1)} %get-tuple-element.204.query_low, bf16[256,768]{1,0:T(8,128)(2,1)} %get-tuple-element.205.query_segment, ...), custom_call_target="tpu_custom_call" | custom-call | flops 11000000512 | tf_op jit(solution)/shard_map/attend/pallas_call | solution.py:927
  70.9 20.2 %feed_forward.1 = (bf16[2,64,768]{2,1,0:T(8,128)(2,1)}, bf16[2,64,768]{2,1,0:T(8,128)(2,1)}, f32[256,768]{1,0:T(8,128)}, bf16[256,768]{1,0:T(8,128)(2,1)}, bf16[...) custom-call(s32[12]{0:T(128)} %pad_add_fusion.scalars, ...), custom_call_target="tpu_custom_call" | custom-call | flops 20999999488 | tf_op jit(solution)/shard_map/feed_forward/pallas_call | solution.py:950
  91.7 5.3 %attend_back.2 = (bf16[256,256]{1,0:T(8,128)(2,1)}, bf16[768,256]{1,0:T(8,128)(2,1)}, bf16[768,256]{1,0:T(8,128)(2,1)}, f32[8,256]{1,0:T(8,128)}, f32[4,16,384]{2,1,0:T(8,128)}) custom-call(s32[12]{0:T(128)} %pad_add_fusion.scalars, bf16[256,768]{1,0:T(8,128)(2,1)} %get-tuple-element.204.query_low, bf16[256,768]{1,0:T(8,128)(2,1)} %get-tuple-element.205.query_segment, ...), custom_call_target="tpu_custom_call" | custom-call | flops 3000000000 | tf_op jit(solution)/shard_map/attend_back/pallas_call | solution.py:986
  103.2 8.4 %attend_back.3 = (bf16[256,512]{1,0:T(8,128)(2,1)}, bf16[768,512]{1,0:T(8,128)(2,1)}, bf16[768,512]{1,0:T(8,128)(2,1)}, f32[8,512]{1,0:T(8,128)}, f32[8,16,384]{2,1,0:T(8,128)}) custom-call(s32[12]{0:T(128)} %pad_add_fusion.scalars, bf16[256,768]{1,0:T(8,128)(2,1)} %get-tuple-element.204.query_low, bf16[256,768]{1,0:T(8,128)(2,1)} %get-tuple-element.205.query_segment, ...), custom_call_target="tpu_custom_call" | custom-call | flops 3000000000 | tf_op jit(solution)/shard_map/attend_back/pallas_call | solution.py:986
  111.6 9.0 %weight_gradients.1 = (bf16[2,2,2,208,384]{4,3,2,1,0:T(8,128)(2,1)}, bf16[2,2,2,208,384]{4,3,2,1,0:T(8,128)(2,1)}, bf16[2,2,2,208,384]{4,3,2,1,0:T(8,128)(2,1)}, bf16[2,2,2,208,384]{4,3,2,1,0:T(8,128)(2,1)}) custom-call(s32[12]{0:T(128)} %pad_add_fusion.scalars, bf16[256,768]{1,0:T(8,128)(2,1)} %bitcast.86, bf16[768,768]{1,0:T(8,128)(2,1)} %bitcast.103, ...), custom_call_target="tpu_custom_call" | custom-call | flops 3000000000 | tf_op jit(solution)/shard_map/weight_gradients/pallas_call | solution.py:1039
  130.0 8.8 %tree_gradients.1 = (f32[2,64,768]{2,1,0:T(8,128)}, f32[2,64,768]{2,1,0:T(8,128)}, bf16[2,2,2,256,384]{4,3,2,1,0:T(8,128)(2,1)}, bf16[2,2,2,256,384]{4,3,2,1,0:T(8,128)(2,1)}) custom-call(s32[12]{0:T(128)} %pad_add_fusion.scalars, s32[12]{0:T(128)} %get-tuple-element.228.found, f32[256,768]{1,0:T(8,128)} %get-tuple-element.261.d_mid_in, ...), custom_call_target="tpu_custom_call" | custom-call | flops 3000000000 | tf_op jit(solution)/shard_map/tree_gradients/pallas_call | solution.py:1053
  160.5 20.0 %collective-permute-done.31 = bf16[1,1,1,1,768,384]{5,4,3,2,1,0:T(8,128)(2,1)S(1)} collective-permute-done((bf16[1,1,1,1,768,384]{5,4,3,2,1,0:T(8,128)(2,1)S(1)}, bf16[1,1,1,1,768,384]{5,4,3,2,1,0:T(8,128)(2,1)S(1)}, u32[]{:S(2)}, u32[]{:S(2)}) %collective-permute-start.31) | collective-permute-done | bytes 589856 | tf_op jit(solution)/shard_map/ppermute | solution.py:651
  180.6 3.0 %collective-permute-done.33 = bf16[2,1,2,2,112,384]{5,4,3,2,1,0:T(8,128)(2,1)S(1)} collective-permute-done((bf16[2,1,2,2,112,384]{5,4,3,2,1,0:T(8,128)(2,1)S(1)}, bf16[2,1,2,2,112,384]{5,4,3,2,1,0:T(8,128)(2,1)S(1)}, u32[]{:S(2)}, u32[]{:S(2)}) %collective-permute-start.33) | collective-permute-done | bytes 688160 | tf_op jit(solution)/shard_map/ppermute | solution.py:651
  189.3 3.1 %collective-permute-done.35 = bf16[2,1,1,1,128,384]{5,4,2,1,0,3:T(8,128)(2,1)S(1)} collective-permute-done((bf16[2,1,1,1,128,384]{5,4,2,1,0,3:T(8,128)(2,1)S(1)}, bf16[2,1,1,1,128,384]{5,4,2,1,0,3:T(8,128)(2,1)S(1)}, u32[]{:S(2)}, u32[]{:S(2)}) %collective-permute-start.35) | collective-permute-done | bytes 196640 | tf_op jit(solution)/shard_map/ppermute | solution.py:651
  196.1 6.0 %collective-permute-done.34 = bf16[2,2,1,1,176,384]{5,4,3,2,1,0:T(8,128)(2,1)S(1)} collective-permute-done((bf16[2,2,1,1,176,384]{5,4,3,2,1,0:T(8,128)(2,1)S(1)}, bf16[2,2,1,1,176,384]{5,4,3,2,1,0:T(8,128)(2,1)S(1)}, u32[]{:S(2)}, u32[]{:S(2)}) %collective-permute-start.34) | collective-permute-done | bytes 540704 | tf_op jit(solution)/shard_map/ppermute | solution.py:651
  216.7 4.7 %collective-permute-start.46 = (bf16[1,1,1,1,672,384]{5,4,3,2,1,0:T(8,128)(2,1)S(1)}, bf16[1,1,1,1,672,384]{5,4,3,2,1,0:T(8,128)(2,1)S(1)}, u32[]{:S(2)}, u32[]{:S(2)}) collective-permute-start(bf16[1,1,1,1,672,384]{5,4,3,2,1,0:T(8,128)(2,1)S(1)} %slice_dynamic-update-slice_fusion.8), channel_id=1, source_target_pairs={{0,8},{1,9},{2,10},{3,11},{4,12},{5,13},{6,14},{7,15},{8,0},{9,1},... | collective-permute-start | bytes 1548296 | tf_op jit(solution)/shard_map/ppermute | solution.py:651
  224.8 13.9 %collective-permute-done.46 = bf16[1,1,1,1,672,384]{5,4,3,2,1,0:T(8,128)(2,1)S(1)} collective-permute-done((bf16[1,1,1,1,672,384]{5,4,3,2,1,0:T(8,128)(2,1)S(1)}, bf16[1,1,1,1,672,384]{5,4,3,2,1,0:T(8,128)(2,1)S(1)}, u32[]{:S(2)}, u32[]{:S(2)}) %collective-permute-start.46) | collective-permute-done | bytes 516128 | tf_op jit(solution)/shard_map/ppermute | solution.py:651
  239.8 3.5 %collective-permute-done.49 = bf16[2,1,1,1,48,384]{5,4,3,2,1,0:T(8,128)(2,1)S(1)} collective-permute-done((bf16[2,1,1,1,48,384]{5,4,3,2,1,0:T(8,128)(2,1)S(1)}, bf16[2,1,1,1,48,384]{5,4,3,2,1,0:T(8,128)(2,1)S(1)}, u32[]{:S(2)}, u32[]{:S(2)}) %collective-permute-start.49) | collective-permute-done | bytes 73760 | tf_op jit(solution)/shard_map/ppermute | solution.py:651
  243.8 4.7 %collective-permute-done.47 = bf16[2,1,1,1,80,384]{5,4,3,2,1,0:T(8,128)(2,1)S(1)} collective-permute-done((bf16[2,1,1,1,80,384]{5,4,3,2,1,0:T(8,128)(2,1)S(1)}, bf16[2,1,1,1,80,384]{5,4,3,2,1,0:T(8,128)(2,1)S(1)}, u32[]{:S(2)}, u32[]{:S(2)}) %collective-permute-start.47) | collective-permute-done | bytes 122912 | tf_op jit(solution)/shard_map/ppermute | solution.py:651
  252.1 3.2 %collective-permute-done.55 = bf16[2,1,2,1,48,384]{5,4,3,2,1,0:T(8,128)(2,1)S(1)} collective-permute-done((bf16[2,1,2,1,48,384]{5,4,3,2,1,0:T(8,128)(2,1)S(1)}, bf16[2,1,2,1,48,384]{5,4,3,2,1,0:T(8,128)(2,1)S(1)}, u32[]{:S(2)}, u32[]{:S(2)}) %collective-permute-start.55) | collective-permute-done | bytes 147488 | tf_op jit(solution)/shard_map/ppermute | solution.py:651
  262.0 7.4 %feed_spread.1 = (f32[1536,768]{1,0:T(8,128)}, f32[384,3072]{1,0:T(8,128)}) custom-call(s32[2]{0:T(128)} %pad_add_fusion.1.scalars, bf16[2,2,2,1,128,384]{5,4,3,2,1,0:T(8,128)(2,1)} %bitcast.78, bf16[2,2,2,1,128,384]{5,4,3,2,1,0:T(8,128)(2,1)} %bitcast.100, bf16[2,2,1,2,128,384]{5,4,3,2,1,0:T(8,128)(2,1)} %bitcast.79, ...), custom_call_target="tpu_custom_call" | custom-call | flops 7000000000 | tf_op jit(solution)/shard_map/feed_spread/pallas_call | solution.py:1094
  271.1 4.8 %later_spread.1 = (f32[384,768]{1,0:T(8,128)}, f32[384,768]{1,0:T(8,128)}, f32[384,768]{1,0:T(8,128)}, f32[384,768]{1,0:T(8,128)}, f32[1536]{0:T(1024)}, /*index...) custom-call(s32[2]{0:T(128)} %pad_add_fusion.1.scalars, ...), custom_call_target="tpu_custom_call" | custom-call | flops 4000000000 | tf_op jit(solution)/shard_map/later_spread/pallas_call | solution.py:1107
  (298 shorter events, 103.9 us)
Async XLA Ops:
  3.6 15.1 %collective-permute-start.1 = (bf16[384,768]{1,0:T(8,128)(2,1)}, bf16[384,768]{1,0:T(8,128)(2,1)S(1)}, u32[]{:S(2)}, u32[]{:S(2)}) collective-permute-start(bf16[384,768]{1,0:T(8,128)(2,1)} %refs_6_.1), channel_id=1, source_target_pairs={{0,16},{16,0},{1,17},{17,1},{2,18},{18,2},{3,19},{19,3},{4,20},{20... | collective-permute-start | bytes 1769480 | tf_op jit(solution)/shard_map/ppermute | solution.py:810
  4.2 14.6 %collective-permute-start.2 = (bf16[384,768]{1,0:T(8,128)(2,1)}, bf16[384,768]{1,0:T(8,128)(2,1)}, u32[]{:S(2)}, u32[]{:S(2)}) collective-permute-start(bf16[384,768]{1,0:T(8,128)(2,1)} %refs_8_.1), channel_id=1, source_target_pairs={{0,16},{16,0},{1,17},{17,1},{2,18},{18,2},{3,19},{19,3},{4,20},{20... | collective-permute-start | bytes 1769480 | tf_op jit(solution)/shard_map/ppermute | solution.py:810
  4.2 14.4 %collective-permute-start = (bf16[1,1,1,1,144,768]{5,4,3,2,1,0:T(8,128)(2,1)S(1)}, bf16[1,1,1,1,144,768]{5,4,3,2,1,0:T(8,128)(2,1)S(1)}, u32[]{:S(2)}, u32[]{:S(2)}) collective-permute-start(bf16[1,1,1,1,144,768]{5,4,3,2,1,0:T(8,128)(2,1)S(1)} %bitcast.74), channel_id=1, source_target_pairs={{0,8},{1,9},{2,10},{3,11},{4,12},{5,13},{6,14},{7,15},{8,0},{9,1},... | collective-permute-start | bytes 663560 | tf_op jit(solution)/shard_map/ppermute | solution.py:651
  39.0 16.0 %collective-permute-start.16 = (bf16[1536,768]{1,0:T(8,128)(2,1)}, bf16[1536,768]{1,0:T(8,128)(2,1)}, u32[]{:S(2)}, u32[]{:S(2)}) collective-permute-start(bf16[1536,768]{1,0:T(8,128)(2,1)} %refs_4_), channel_id=1, source_target_pairs={{0,16},{16,0},{1,17},{17,1},{2,18},{18,2},{3,19},{19,3},{4,20},{20... | collective-permute-start | bytes 7077896 | tf_op jit(solution)/shard_map/ppermute | solution.py:810
  39.1 15.9 %collective-permute-start.13 = (bf16[2,2,2,1,144,256]{5,4,3,2,1,0:T(8,128)(2,1)S(1)}, bf16[2,2,2,1,144,256]{5,4,3,2,1,0:T(8,128)(2,1)S(1)}, u32[]{:S(2)}, u32[]{:S(2)}) collective-permute-start(bf16[2,2,2,1,144,256]{5,4,3,2,1,0:T(8,128)(2,1)S(1)} %pad_maximum_fusion.3.refs_0_), channel_id=1, source_target_pairs={{0,1},{1,0},{2,3},{3,2},{4,5},{5,4},{6,7},{7,6},{8,9},{9,8},{10,11... | collective-permute-start | bytes 1769480 | tf_op jit(solution)/shard_map/ppermute | solution.py:651
  40.6 14.0 %collective-permute-start.14 = (bf16[2,2,1,2,128,256]{5,4,3,2,1,0:T(8,128)(2,1)S(1)}, bf16[2,2,1,2,128,256]{5,4,3,2,1,0:T(8,128)(2,1)S(1)}, u32[]{:S(2)}, u32[]{:S(2)}) collective-permute-start(bf16[2,2,1,2,128,256]{5,4,3,2,1,0:T(8,128)(2,1)S(1)} %pad_maximum_fusion.4.refs_2_), channel_id=1, source_target_pairs={{0,2},{1,3},{2,0},{3,1},{4,6},{5,7},{6,4},{7,5},{8,10},{9,11},{10,... | collective-permute-start | bytes 1572872 | tf_op jit(solution)/shard_map/ppermute | solution.py:651
  41.1 13.8 %collective-permute-start.15 = (bf16[2,1,2,2,128,256]{5,4,3,2,1,0:T(8,128)(2,1)S(1)}, bf16[2,1,2,2,128,256]{5,4,3,2,1,0:T(8,128)(2,1)}, u32[]{:S(2)}, u32[]{:S(2)}) collective-permute-start(bf16[2,1,2,2,128,256]{5,4,3,2,1,0:T(8,128)(2,1)S(1)} %pad_maximum_fusion.5.refs_4_), channel_id=1, source_target_pairs={{0,4},{1,5},{2,6},{3,7},{4,0},{5,1},{6,2},{7,3},{8,12},{9,13},{10,... | collective-permute-start | bytes 1572872 | tf_op jit(solution)/shard_map/ppermute | solution.py:651
  99.8 20.8 %collective-permute-start.19 = (bf16[2,2,2,1,128,384]{5,4,2,1,0,3:T(8,128)(2,1)}, bf16[2,2,2,1,128,384]{5,4,2,1,0,3:T(8,128)(2,1)S(1)}, u32[]{:S(2)}, u32[]{:S(2)}) collective-permute-start(bf16[2,2,2,1,128,384]{5,4,2,1,0,3:T(8,128)(2,1)} %get-tuple-element.237), channel_id=1, source_target_pairs={{0,1},{1,0},{2,3},{3,2},{4,5},{5,4},{6,7},{7,6},{8,9},{9,8},{10,11... | collective-permute-start | bytes 2359304 | tf_op jit(solution)/shard_map/ppermute | solution.py:651
  101.2 21.9 %collective-permute-start.20 = (bf16[2,2,1,2,128,384]{5,4,3,1,0,2:T(8,128)(2,1)S(1)}, bf16[2,2,1,2,128,384]{5,4,3,1,0,2:T(8,128)(2,1)S(1)}, u32[]{:S(2)}, u32[]{:S(2)}) collective-permute-start(bf16[2,2,1,2,128,384]{5,4,3,1,0,2:T(8,128)(2,1)S(1)} %get-tuple-element.238), channel_id=1, source_target_pairs={{0,2},{1,3},{2,0},{3,1},{4,6},{5,7},{6,4},{7,5},{8,10},{9,11},{10,... | collective-permute-start | bytes 2359304 | tf_op jit(solution)/shard_map/ppermute | solution.py:651
  101.9 22.6 %collective-permute-start.21 = (bf16[2,1,2,2,128,384]{5,4,3,2,1,0:T(8,128)(2,1)S(1)}, bf16[2,1,2,2,128,384]{5,4,3,2,1,0:T(8,128)(2,1)}, u32[]{:S(2)}, u32[]{:S(2)}) collective-permute-start(bf16[2,1,2,2,128,384]{5,4,3,2,1,0:T(8,128)(2,1)S(1)} %get-tuple-element.239), channel_id=1, source_target_pairs={{0,4},{1,5},{2,6},{3,7},{4,0},{5,1},{6,2},{7,3},{8,12},{9,13},{10,... | collective-permute-start | bytes 2359304 | tf_op jit(solution)/shard_map/ppermute | solution.py:651
  126.8 15.3 %collective-permute-start.25 = (bf16[2,2,2,208,384]{4,3,2,1,0:T(8,128)(2,1)}, bf16[2,2,2,208,384]{4,3,2,1,0:T(8,128)(2,1)}, u32[]{:S(2)}, u32[]{:S(2)}) collective-permute-start(bf16[2,2,2,208,384]{4,3,2,1,0:T(8,128)(2,1)} %get-tuple-element.267), channel_id=1, source_target_pairs={{0,16},{16,0},{1,17},{17,1},{2,18},{18,2},{3,19},{19,3},{4,20},{20... | collective-permute-start | bytes 3833864 | tf_op jit(solution)/shard_map/ppermute | solution.py:1070
  126.8 15.3 %collective-permute-start.26 = (bf16[2,2,2,208,384]{4,3,2,1,0:T(8,128)(2,1)}, bf16[2,2,2,208,384]{4,3,2,1,0:T(8,128)(2,1)S(1)}, u32[]{:S(2)}, u32[]{:S(2)}) collective-permute-start(bf16[2,2,2,208,384]{4,3,2,1,0:T(8,128)(2,1)} %get-tuple-element.268), channel_id=1, source_target_pairs={{0,16},{16,0},{1,17},{17,1},{2,18},{18,2},{3,19},{19,3},{4,20},{20... | collective-permute-start | bytes 3833864 | tf_op jit(solution)/shard_map/ppermute | solution.py:1070
  127.3 11.4 %collective-permute-start.22 = (bf16[2,2,1,1,128,384]{5,4,2,1,0,3:T(8,128)(2,1)}, bf16[2,2,1,1,128,384]{5,4,2,1,0,3:T(8,128)(2,1)}, u32[]{:S(2)}, u32[]{:S(2)}) collective-permute-start(bf16[2,2,1,1,128,384]{5,4,2,1,0,3:T(8,128)(2,1)} %slice.417), channel_id=1, source_target_pairs={{0,2},{1,3},{2,0},{3,1},{4,6},{5,7},{6,4},{7,5},{8,10},{9,11},{10,... | collective-permute-start | bytes 1179656 | tf_op jit(solution)/shard_map/ppermute | solution.py:651
  128.6 11.2 %collective-permute-start.23 = (bf16[2,1,1,2,128,384]{5,4,3,1,0,2:T(8,128)(2,1)S(1)}, bf16[2,1,1,2,128,384]{5,4,3,1,0,2:T(8,128)(2,1)}, u32[]{:S(2)}, u32[]{:S(2)}) collective-permute-start(bf16[2,1,1,2,128,384]{5,4,3,1,0,2:T(8,128)(2,1)S(1)} %slice.418), channel_id=1, source_target_pairs={{0,4},{1,5},{2,6},{3,7},{4,0},{5,1},{6,2},{7,3},{8,12},{9,13},{10,... | collective-permute-start | bytes 1179656 | tf_op jit(solution)/shard_map/ppermute | solution.py:651
  129.3 11.7 %collective-permute-start.24 = (bf16[2,1,2,1,128,384]{5,4,3,2,1,0:T(8,128)(2,1)}, bf16[2,1,2,1,128,384]{5,4,3,2,1,0:T(8,128)(2,1)}, u32[]{:S(2)}, u32[]{:S(2)}) collective-permute-start(bf16[2,1,2,1,128,384]{5,4,3,2,1,0:T(8,128)(2,1)} %slice.419), channel_id=1, source_target_pairs={{0,1},{1,0},{2,3},{3,2},{4,5},{5,4},{6,7},{7,6},{8,9},{9,8},{10,11... | collective-permute-start | bytes 1179656 | tf_op jit(solution)/shard_map/ppermute | solution.py:651
  153.6 26.8 %collective-permute-start.31 = (bf16[1,1,1,1,768,384]{5,4,3,2,1,0:T(8,128)(2,1)S(1)}, bf16[1,1,1,1,768,384]{5,4,3,2,1,0:T(8,128)(2,1)S(1)}, u32[]{:S(2)}, u32[]{:S(2)}) collective-permute-start(bf16[1,1,1,1,768,384]{5,4,3,2,1,0:T(8,128)(2,1)S(1)} %slice_dynamic-update-slice_fusion), channel_id=1, source_target_pairs={{0,8},{1,9},{2,10},{3,11},{4,12},{5,13},{6,14},{7,15},{8,0},{9,1},... | collective-permute-start | bytes 1769480 | tf_op jit(solution)/shard_map/ppermute | solution.py:651
  156.9 26.7 %collective-permute-start.33 = (bf16[2,1,2,2,112,384]{5,4,3,2,1,0:T(8,128)(2,1)S(1)}, bf16[2,1,2,2,112,384]{5,4,3,2,1,0:T(8,128)(2,1)S(1)}, u32[]{:S(2)}, u32[]{:S(2)}) collective-permute-start(bf16[2,1,2,2,112,384]{5,4,3,2,1,0:T(8,128)(2,1)S(1)} %maximum_bitcast_fusion.4), channel_id=1, source_target_pairs={{0,4},{1,5},{2,6},{3,7},{4,0},{5,1},{6,2},{7,3},{8,12},{9,13},{10,... | collective-permute-start | bytes 2064392 | tf_op jit(solution)/shard_map/ppermute | solution.py:651
  158.3 25.6 %collective-permute-start.30 = (bf16[2,2,2,1,176,384]{5,4,3,2,1,0:T(8,128)(2,1)S(1)}, bf16[2,2,2,1,176,384]{5,4,3,2,1,0:T(8,128)(2,1)S(1)}, u32[]{:S(2)}, u32[]{:S(2)}) collective-permute-start(bf16[2,2,2,1,176,384]{5,4,3,2,1,0:T(8,128)(2,1)S(1)} %maximum_bitcast_fusion.1), channel_id=1, source_target_pairs={{0,1},{1,0},{2,3},{3,2},{4,5},{5,4},{6,7},{7,6},{8,9},{9,8},{10,11... | collective-permute-start | bytes 3244040 | tf_op jit(solution)/shard_map/ppermute | solution.py:651
  158.9 25.3 %collective-permute-start.32 = (bf16[2,2,1,2,176,384]{5,4,3,2,1,0:T(8,128)(2,1)S(1)}, bf16[2,2,1,2,176,384]{5,4,3,2,1,0:T(8,128)(2,1)S(1)}, u32[]{:S(2)}, u32[]{:S(2)}) collective-permute-start(bf16[2,2,1,2,176,384]{5,4,3,2,1,0:T(8,128)(2,1)S(1)} %maximum_bitcast_fusion.2), channel_id=1, source_target_pairs={{0,2},{1,3},{2,0},{3,1},{4,6},{5,7},{6,4},{7,5},{8,10},{9,11},{10,... | collective-permute-start | bytes 3244040 | tf_op jit(solution)/shard_map/ppermute | solution.py:651
  187.7 14.4 %collective-permute-start.34 = (bf16[2,2,1,1,176,384]{5,4,3,2,1,0:T(8,128)(2,1)S(1)}, bf16[2,2,1,1,176,384]{5,4,3,2,1,0:T(8,128)(2,1)S(1)}, u32[]{:S(2)}, u32[]{:S(2)}) collective-permute-start(bf16[2,2,1,1,176,384]{5,4,3,2,1,0:T(8,128)(2,1)S(1)} %slice.442), channel_id=1, source_target_pairs={{0,2},{1,3},{2,0},{3,1},{4,6},{5,7},{6,4},{7,5},{8,10},{9,11},{10,... | collective-permute-start | bytes 1622024 | tf_op jit(solution)/shard_map/ppermute | solution.py:651
  216.7 22.1 %collective-permute-start.46 = (bf16[1,1,1,1,672,384]{5,4,3,2,1,0:T(8,128)(2,1)S(1)}, bf16[1,1,1,1,672,384]{5,4,3,2,1,0:T(8,128)(2,1)S(1)}, u32[]{:S(2)}, u32[]{:S(2)}) collective-permute-start(bf16[1,1,1,1,672,384]{5,4,3,2,1,0:T(8,128)(2,1)S(1)} %slice_dynamic-update-slice_fusion.8), channel_id=1, source_target_pairs={{0,8},{1,9},{2,10},{3,11},{4,12},{5,13},{6,14},{7,15},{8,0},{9,1},... | collective-permute-start | bytes 1548296 | tf_op jit(solution)/shard_map/ppermute | solution.py:651
  221.4 28.0 %collective-permute-start.50 = (bf16[2,2,2,1,128,384]{5,4,2,1,0,3:T(8,128)(2,1)S(1)}, bf16[2,2,2,1,128,384]{5,4,2,1,0,3:T(8,128)(2,1)S(1)}, u32[]{:S(2)}, u32[]{:S(2)}) collective-permute-start(bf16[2,2,2,1,128,384]{5,4,2,1,0,3:T(8,128)(2,1)S(1)} %pad_maximum_fusion), channel_id=1, source_target_pairs={{0,1},{1,0},{2,3},{3,2},{4,5},{5,4},{6,7},{7,6},{8,9},{9,8},{10,11... | collective-permute-start | bytes 2359304 | tf_op jit(solution)/shard_map/ppermute | solution.py:651
  222.2 27.1 %collective-permute-start.51 = (bf16[2,2,1,2,128,384]{5,4,3,1,0,2:T(8,128)(2,1)S(1)}, bf16[2,2,1,2,128,384]{5,4,3,1,0,2:T(8,128)(2,1)S(1)}, u32[]{:S(2)}, u32[]{:S(2)}) collective-permute-start(bf16[2,2,1,2,128,384]{5,4,3,1,0,2:T(8,128)(2,1)S(1)} %pad_maximum_fusion.1), channel_id=1, source_target_pairs={{0,2},{1,3},{2,0},{3,1},{4,6},{5,7},{6,4},{7,5},{8,10},{9,11},{10,... | collective-permute-start | bytes 2359304 | tf_op jit(solution)/shard_map/ppermute | solution.py:651
  223.3 26.1 %collective-permute-start.52 = (bf16[2,1,2,2,128,384]{5,4,3,2,1,0:T(8,128)(2,1)S(1)}, bf16[2,1,2,2,128,384]{5,4,3,2,1,0:T(8,128)(2,1)S(1)}, u32[]{:S(2)}, u32[]{:S(2)}) collective-permute-start(bf16[2,1,2,2,128,384]{5,4,3,2,1,0:T(8,128)(2,1)S(1)} %pad_maximum_fusion.2.refs_4_), channel_id=1, source_target_pairs={{0,4},{1,5},{2,6},{3,7},{4,0},{5,1},{6,2},{7,3},{8,12},{9,13},{10,... | collective-permute-start | bytes 2359304 | tf_op jit(solution)/shard_map/ppermute | solution.py:651
  (69 other events, 602.9 us)

commit v5 on v4

--- a/solution.py
+++ b/solution.py
@@ -86,7 +86,7 @@
     parts = refs[: 2 * len(columns)]
     refs = refs[2 * len(columns) :]
     key_weights, value_weights = refs[:pieces], refs[pieces : 2 * pieces]
-    path, keys, values, found, full_key, full_value, tree, sems, tree_sems = refs[2 * pieces :]
+    path, keys, values, found, full_key, full_value, tree, sems, tree_sems, prefetch = refs[2 * pieces :]
     shard = scalars[0]
     total = len(tree.shape) - 2
     moves = []
@@ -103,6 +103,7 @@
         copy.start()
     for copy in moves:
         copy.wait()
+    prefetch()
     micro_count = path.shape[0]
     content_rows = micro_count * run
     facts = [
@@ -132,6 +133,84 @@
         values[micro * span : (micro + 1) * span, :] = mm(rows, full_value[...]).astype(low)
 
 
+def start_all(groups):
+    for group in groups:
+        for copy in group:
+            copy.start()
+
+
+def forward_kernel(pieces, columns, lasts, run, slots, scalars, table, *refs):
+    query_low, query_segment, rows, cotangent, vectors, inner_bias = refs[:6]
+    parts, refs = refs[6 : 6 + 2 * len(columns)], refs[6 + 2 * len(columns) :]
+    pair_weights, feed_weights, refs = refs[: 2 * pieces], refs[2 * pieces : 5 * pieces], refs[5 * pieces :]
+    path_out, keys_out, values_out, probs_out, found, attended = refs[:6]
+    refs = refs[6:]
+    feed_outs = refs[: 6 + (4 if pieces == 2 else 2)]
+    refs = refs[len(feed_outs) :]
+    path, keys, values, probs, full_key, full_value, tree, out_sems, pair_sems, tree_sems = refs[:10]
+    feed_scratch = refs[10:]
+    sems = feed_scratch[6] if pieces == 2 else feed_scratch[5]
+    copies = [
+        weight_copies(feed_weights[i * pieces : (i + 1) * pieces], feed_scratch[i], sems, i * pieces, scalars[0])
+        for i in range(3)
+    ]
+    keys_kernel(
+        pieces,
+        columns,
+        lasts,
+        run,
+        slots,
+        scalars,
+        *parts,
+        *pair_weights,
+        path,
+        keys,
+        values,
+        found,
+        full_key,
+        full_value,
+        tree,
+        pair_sems,
+        tree_sems,
+        lambda: start_all(copies),
+    )
+    leaving = [
+        pltpu.make_async_copy(path, path_out, out_sems.at[0]),
+        pltpu.make_async_copy(keys, keys_out, out_sems.at[1]),
+        pltpu.make_async_copy(values, values_out, out_sems.at[2]),
+    ]
+    for copy in leaving:
+        copy.start()
+    micro_count = path.shape[0]
+
+    def attend(pair, carry):
+        lanes = pl.ds(pl.multiple_of(pair * 128, 128), 128)
+        attend_kernel(
+            run,
+            slots,
+            pair,
+            scalars,
+            table,
+            query_low.at[:, lanes],
+            query_segment.at[:, lanes],
+            keys.at[:, lanes],
+            values.at[:, lanes],
+            vectors.at[:, lanes],
+            probs.at[pl.ds(pair * micro_count, micro_count)],
+            attended.at[:, lanes],
+        )
+        return carry
+
+    lax.fori_loop(0, rows.shape[1] // 128, attend, 0)
+    leaving.append(pltpu.make_async_copy(probs, probs_out, out_sems.at[3]))
+    leaving[-1].start()
+    feed_kernel(
+        pieces, run, copies, scalars, rows, attended, cotangent, vectors, inner_bias, *feed_outs, *feed_scratch
+    )
+    for copy in leaving:
+        copy.wait()
+
+
 def head_masks():
     lane = lax.broadcasted_iota(jnp.int32, (1, 128), 1)
     first = lane < 64
@@ -157,8 +236,7 @@
     return base + row - column, column
 
 
-def attend_kernel(run, slots, scalars, table, query_low, query_segment, keys, values, vectors, probs, attended):
-    pair = pl.program_id(0)
+def attend_kernel(run, slots, pair, scalars, table, query_low, query_segment, keys, values, vectors, probs, attended):
     span = slots * run
     first, mask_a, mask_b = head_masks()
     for micro in range(probs.shape[0]):
@@ -226,9 +304,7 @@
     return ((0, step), (step, step), (2 * step, height - 2 * step))
 
 
-def feed_kernel(pieces, run, scalars, rows, attended, cotangent, vectors, inner_bias, *refs):
-    out_weights, inner_weights, outer_weights = (refs[i * pieces : (i + 1) * pieces] for i in range(3))
-    refs = refs[3 * pieces :]
+def feed_kernel(pieces, run, copies, scalars, rows, attended, cotangent, vectors, inner_bias, *refs):
     out_content, out_query, d_mid_in, d_branch_out, d_att, small = refs[:6]
     routes = feed_cuts(pieces, rows.shape[1])
     outputs = 4 if pieces == 2 else 2
@@ -236,17 +312,7 @@
     full_out, full_inner, full_outer, act_low, slope = refs[6 + outputs : 11 + outputs]
     if pieces == 2:
         held, sems, grad_sems = refs[11 + outputs :]
-    else:
-        (sems,) = refs[11 + outputs :]
     shard, place = scalars[0], scalars[1]
-    copies = [
-        weight_copies(out_weights, full_out, sems, 0, shard),
-        weight_copies(inner_weights, full_inner, sems, pieces, shard),
-        weight_copies(outer_weights, full_outer, sems, 2 * pieces, shard),
-    ]
-    for group in copies:
-        for copy in group:
-            copy.start()
     model = rows.shape[1]
     hidden = full_inner.shape[1]
     att_low = attended[...].astype(low)
@@ -892,29 +958,6 @@
         cost_estimate=cost(1),
     )(early, rows, vectors, *query_weights)
 
-    path, keys, values, found = pl.pallas_call(
-        functools.partial(keys_kernel, pieces, columns, [route[0] for route in routes_out], run, slots),
-        out_shape=(
-            shape((micro_count, span, model), low),
-            shape((micro_count * span, model), low),
-            shape((micro_count * span, model), low),
-            shape((micro_count * slots,), jnp.int32),
-        ),
-        in_specs=[smem_space] + [any_space] * (2 * len(columns) + 2 * pieces),
-        out_specs=(vmem_space,) * 3 + (smem_space,),
-        scratch_shapes=[
-            pltpu.VMEM((model, model), low),
-            pltpu.VMEM((model, model), low),
-            pltpu.VMEM((2,) * total_bits + (content_rows + 16, model), low),
-            dma((2 * pieces,)),
-            dma((2 * len(columns),)),
-        ],
-        compiler_params=grown,
-        name="path_keys",
-        cost_estimate=cost(6),
-    )(scalars, *tree_parts, *key_weights, *value_weights)
-    path = path.reshape(micro_count * span, model)
-
     def blocks_at(first):
         return (
             pl.BlockSpec((rows_total, 128), lambda pair: (0, pair + first)),
@@ -924,20 +967,6 @@
         )
 
     row_block, key_block, prob_block, vector_block = blocks_at(0)
-    probs, attended = pl.pallas_call(
-        functools.partial(attend_kernel, run, slots),
-        grid=(pairs,),
-        out_shape=(
-            shape((pairs * micro_count, 4 * run, span), low),
-            shape((rows_total, model), f32),
-        ),
-        in_specs=[smem_space, smem_space, row_block, row_block, key_block, key_block, vector_block],
-        out_specs=(prob_block, row_block),
-        compiler_params=grown,
-        name="attend",
-        cost_estimate=cost(11),
-    )(scalars, table, query_low, query_segment, keys, values, vectors)
-
     half = model // 2
     if pieces == 2:
         grad_shapes = [shape((2,) * (total_bits - 1) + (half, half), low)] * 4
@@ -947,9 +976,15 @@
         grad_shapes = [shape((hidden, model), low), shape((model, hidden), low)]
         grad_specs = [vmem_space] * 2
         grad_scratch = []
-    results = pl.pallas_call(
-        functools.partial(feed_kernel, pieces, run),
+    path, keys, values, probs, found, attended, *results = pl.pallas_call(
+        functools.partial(forward_kernel, pieces, columns, [route[0] for route in routes_out], run, slots),
         out_shape=[
+            shape((micro_count, span, model), low),
+            shape((micro_count * span, model), low),
+            shape((micro_count * span, model), low),
+            shape((pairs * micro_count, 4 * run, span), low),
+            shape((micro_count * slots,), jnp.int32),
+            shape((rows_total, model), f32),
             shape((micro_count, run, model), low),
             shape((micro_count, run, model), low),
             shape((rows_total, model), f32),
@@ -958,9 +993,19 @@
             shape((16, model), f32),
         ]
         + grad_shapes,
-        in_specs=[smem_space] + [vmem_space] * 5 + [any_space] * (3 * pieces),
-        out_specs=[vmem_space] * 6 + grad_specs,
+        in_specs=[smem_space] * 2 + [vmem_space] * 6 + [any_space] * (2 * len(columns) + 5 * pieces),
+        out_specs=[any_space] * 4 + [smem_space] + [vmem_space] * 7 + grad_specs,
         scratch_shapes=[
+            pltpu.VMEM((micro_count, span, model), low),
+            pltpu.VMEM((micro_count * span, model), low),
+            pltpu.VMEM((micro_count * span, model), low),
+            pltpu.VMEM((pairs * micro_count, 4 * run, span), low),
+            pltpu.VMEM((model, model), low),
+            pltpu.VMEM((model, model), low),
+            pltpu.VMEM((2,) * total_bits + (content_rows + 16, model), low),
+            dma((4,)),
+            dma((2 * pieces,)),
+            dma((2 * len(columns),)),
             pltpu.VMEM((model, model), low),
             pltpu.VMEM((model, hidden), low),
             pltpu.VMEM((hidden, model), low),
@@ -971,9 +1016,25 @@
         + [dma((3 * pieces,))]
         + ([dma((12,))] if pieces == 2 else []),
         compiler_params=grown,
-        name="feed_forward",
-        cost_estimate=cost(21),
-    )(scalars, rows, attended, cotangent, vectors, inner_bias, *out_weights, *inner_weights, *outer_weights)
+        name="forward",
+        cost_estimate=cost(36),
+    )(
+        scalars,
+        table,
+        query_low,
+        query_segment,
+        rows,
+        cotangent,
+        vectors,
+        inner_bias,
+        *tree_parts,
+        *key_weights,
+        *value_weights,
+        *out_weights,
+        *inner_weights,
+        *outer_weights,
+    )
+    path = path.reshape(micro_count * span, model)
     out_content, out_query, d_mid_in, d_branch, d_att, small_first = results[:6]
 
     swap = [(0, 1), (1, 0)]

time: 277 us -> 271 us (0.978)
  Pallas kernels: 82.6 us -> 76.7 us
    pallas_call x3 -> x1, Pallas kernels: 35.4 us -> 29.5 us  [shards(): pl.pallas_call(functools.partial(forward_kernel, pieces, columns, [route[...]
  transfers between devices with their start and end apart: 59 -> 59, of which waited for: 33 -> 33; matrix products, arithmetic and copies ran while one was open for 9% -> 9% of each run, Pallas kernels for 15% -> 16%
where the time goes in v5:
time: 271 us; the launch traced here: 270 us
  waiting for transfers between devices  99.1 us (37%)
  Pallas kernels  76.7 us (28%)
  starting transfers between devices  55.6 us (21%)
  other arithmetic  20 us (7%)
  local copies, waits for them, and re-layouts  16.9 us (6%)
    ppermute x48, waiting for transfers between devices, send(): return lax.ppermute(inputs, 'dp', [(i, i ^ 1 << bit) for i in range(count)])  99 us
    ppermute x48, starting transfers between devices, send(): return lax.ppermute(inputs, 'dp', [(i, i ^ 1 << bit) for i in range(count)])  53.6 us
    pallas_call x1, Pallas kernels, shards(): pl.pallas_call(functools.partial(forward_kernel, pieces, columns, [route[...  29.5 us
    pallas_call x2, Pallas kernels, attend_back(): pl.pallas_call(functools.partial(back_kernel, run, slots), grid=(pair_cou...  13.7 us
    pallas_call x1, Pallas kernels, shards(): pl.pallas_call(functools.partial(weights_kernel, pieces), out_shape=grad_...  8.96 us
    pallas_call x1, Pallas kernels, shards(): pl.pallas_call(functools.partial(tree_kernel, pieces, run, slots), out_sh...  8.76 us
    pallas_call x1, Pallas kernels, shards(): pl.pallas_call(feed_spread_kernel, out_shape=(shape(w_outer.shape, f32),...  7.36 us
    concatenate x1, local copies, waits for them, and re-layouts, shards(): jnp.concatenate(flat + [jnp.zeros((fill,), low)]).reshape(16, part_width)  5.61 us
  transfers between devices with their start and end apart: 59, of which 33 were waited for; matrix products, arithmetic and copies ran while one was open for 9% of the time, Pallas kernels for 16%

profile of v5, /device:TPU:0, one launch (start us, length us, event | category | flops | bytes accessed | tf_op | source)
XLA Modules:
  0.0 270.2 jit_solution(4919492964366302365)
XLA Ops:
  4.2 4.0 %collective-permute-start = (bf16[1,1,1,1,144,768]{5,4,3,2,1,0:T(8,128)(2,1)S(1)}, bf16[1,1,1,1,144,768]{5,4,3,2,1,0:T(8,128)(2,1)S(1)}, u32[]{:S(2)}, u32[]{:S(2)}) collective-permute-start(bf16[1,1,1,1,144,768]{5,4,3,2,1,0:T(8,128)(2,1)S(1)} %bitcast.74), channel_id=1, source_target_pairs={{0,8},{1,9},{2,10},{3,11},{4,12},{5,13},{6,14},{7,15},{8,0},{9,1},... | collective-permute-start | bytes 663560 | tf_op jit(solution)/shard_map/ppermute | solution.py:717
  9.8 5.6 %concatenate.123 = bf16[6144]{0:T(1024)(128)(2,1)S(1)} concatenate(bf16[1536]{0:T(1024)(128)(2,1)} %param.34, bf16[384]{0:T(512)(128)(2,1)} %param.35, bf16[384]{0:T(512)(128)(2,1)} %param.36, bf16[384]{0:T(512)(128)(2,1)} %param.37, bf16[384]{0:T(512)(128)(2,1)} %param.38, bf16[384]{0:T(512)(128)(2,1)} %param.39, bf16[384]{0:T(512)(128)(2,1)} %param.40, bf16[384]{0:T(512)(128)(2,1)} %param.41, ...), dimensions={0} | concatenate | bytes 24576 | tf_op jit(solution)/shard_map/concatenate | solution.py:899
  15.5 3.2 %collective-permute-done = bf16[1,1,1,1,144,768]{5,4,3,2,1,0:T(8,128)(2,1)S(1)} collective-permute-done((bf16[1,1,1,1,144,768]{5,4,3,2,1,0:T(8,128)(2,1)S(1)}, bf16[1,1,1,1,144,768]{5,4,3,2,1,0:T(8,128)(2,1)S(1)}, u32[]{:S(2)}, u32[]{:S(2)}) %collective-permute-start) | collective-permute-done | bytes 221216 | tf_op jit(solution)/shard_map/ppermute | solution.py:717
  32.4 4.8 %collective-permute-done.9 = bf16[2,1,1,2,128,256]{5,4,3,2,1,0:T(8,128)(2,1)S(1)} collective-permute-done((bf16[2,1,1,2,128,256]{5,4,3,2,1,0:T(8,128)(2,1)S(1)}, bf16[2,1,1,2,128,256]{5,4,3,2,1,0:T(8,128)(2,1)S(1)}, u32[]{:S(2)}, u32[]{:S(2)}) %collective-permute-start.9) | collective-permute-done | bytes 262176 | tf_op jit(solution)/shard_map/ppermute | solution.py:717
  43.1 3.7 %query_projection.1 = (bf16[256,768]{1,0:T(8,128)(2,1)}, bf16[256,768]{1,0:T(8,128)(2,1)}) custom-call(s32[2]{0:T(128)} %pad_add_fusion.1.scalars, bf16[256,768]{1,0:T(8,128)(2,1)} %bitcast.84, f32[16,768]{1,0:T(8,128)} %bitcast.90, bf16[384,768]{1,0:T(8,128)(2,1)} %refs_6_, bf16[384,768]{1,0:T(8,128)(2,1)} %copy-done.27), custom_call_target="tpu_custom_call" | custom-call | flops 1000000000 | tf_op jit(solution)/shard_map/query_projection/pallas_call | solution.py:950
  46.8 7.8 %collective-permute-done.14.refs_9_ = bf16[2,2,1,2,128,256]{5,4,3,2,1,0:T(8,128)(2,1)S(1)} collective-permute-done((bf16[2,2,1,2,128,256]{5,4,3,2,1,0:T(8,128)(2,1)S(1)}, bf16[2,2,1,2,128,256]{5,4,3,2,1,0:T(8,128)(2,1)S(1)}, u32[]{:S(2)}, u32[]{:S(2)}) %collective-permute-start.14) | collective-permute-done | bytes 524320 | tf_op jit(solution)/shard_map/ppermute | solution.py:717
  55.8 29.5 %forward.1 = (bf16[2,384,768]{2,1,0:T(8,128)(2,1)}, bf16[768,768]{1,0:T(8,128)(2,1)}, bf16[768,768]{1,0:T(8,128)(2,1)}, bf16[12,256,384]{2,1,0:T(8,128)(2,1)}, s...) custom-call(s32[12]{0:T(128)} %pad_add_fusion.scalars, ...), custom_call_target="tpu_custom_call" | custom-call | flops 35999997952 | tf_op jit(solution)/shard_map/forward/pallas_call | solution.py:979
  85.9 5.3 %attend_back.2 = (bf16[256,256]{1,0:T(8,128)(2,1)}, bf16[768,256]{1,0:T(8,128)(2,1)}, bf16[768,256]{1,0:T(8,128)(2,1)}, f32[8,256]{1,0:T(8,128)}, f32[4,16,384]{2,1,0:T(8,128)}) custom-call(s32[12]{0:T(128)} %pad_add_fusion.scalars, bf16[256,768]{1,0:T(8,128)(2,1)} %get-tuple-element.204.refs_0_.query_low, ...), custom_call_target="tpu_custom_call" | custom-call | flops 3000000000 | tf_op jit(solution)/shard_map/attend_back/pallas_call | solution.py:1047
  97.4 8.4 %attend_back.3 = (bf16[256,512]{1,0:T(8,128)(2,1)}, bf16[768,512]{1,0:T(8,128)(2,1)}, bf16[768,512]{1,0:T(8,128)(2,1)}, f32[8,512]{1,0:T(8,128)}, f32[8,16,384]{2,1,0:T(8,128)}) custom-call(s32[12]{0:T(128)} %pad_add_fusion.scalars, bf16[256,768]{1,0:T(8,128)(2,1)} %get-tuple-element.204.refs_0_.query_low, ...), custom_call_target="tpu_custom_call" | custom-call | flops 3000000000 | tf_op jit(solution)/shard_map/attend_back/pallas_call | solution.py:1047
  105.8 9.0 %weight_gradients.1 = (bf16[2,2,2,208,384]{4,3,2,1,0:T(8,128)(2,1)}, bf16[2,2,2,208,384]{4,3,2,1,0:T(8,128)(2,1)}, bf16[2,2,2,208,384]{4,3,2,1,0:T(8,128)(2,1)}, bf16[2,2,2,208,384]{4,3,2,1,0:T(8,128)(2,1)}) custom-call(s32[12]{0:T(128)} %pad_add_fusion.scalars, bf16[256,768]{1,0:T(8,128)(2,1)} %bitcast.86, bf16[768,768]{1,0:T(8,128)(2,1)} %bitcast.102, ...), custom_call_target="tpu_custom_call" | custom-call | flops 3000000000 | tf_op jit(solution)/shard_map/weight_gradients/pallas_call | solution.py:1100
  124.2 8.8 %tree_gradients.1 = (f32[2,64,768]{2,1,0:T(8,128)}, f32[2,64,768]{2,1,0:T(8,128)}, bf16[2,2,2,256,384]{4,3,2,1,0:T(8,128)(2,1)}, bf16[2,2,2,256,384]{4,3,2,1,0:T(8,128)(2,1)}) custom-call(s32[12]{0:T(128)} %pad_add_fusion.scalars, s32[12]{0:T(128)} %get-tuple-element.225.found, f32[256,768]{1,0:T(8,128)} %get-tuple-element.261.d_mid_in, ...), custom_call_target="tpu_custom_call" | custom-call | flops 3000000000 | tf_op jit(solution)/shard_map/tree_gradients/pallas_call | solution.py:1114
  147.8 2.8 %collective-permute-start.31 = (bf16[1,1,1,1,768,384]{5,4,3,2,1,0:T(8,128)(2,1)S(1)}, bf16[1,1,1,1,768,384]{5,4,3,2,1,0:T(8,128)(2,1)S(1)}, u32[]{:S(2)}, u32[]{:S(2)}) collective-permute-start(bf16[1,1,1,1,768,384]{5,4,3,2,1,0:T(8,128)(2,1)S(1)} %slice_dynamic-update-slice_fusion), channel_id=1, source_target_pairs={{0,8},{1,9},{2,10},{3,11},{4,12},{5,13},{6,14},{7,15},{8,0},{9,1},... | collective-permute-start | bytes 1769480 | tf_op jit(solution)/shard_map/ppermute | solution.py:717
  154.6 20.0 %collective-permute-done.31 = bf16[1,1,1,1,768,384]{5,4,3,2,1,0:T(8,128)(2,1)S(1)} collective-permute-done((bf16[1,1,1,1,768,384]{5,4,3,2,1,0:T(8,128)(2,1)S(1)}, bf16[1,1,1,1,768,384]{5,4,3,2,1,0:T(8,128)(2,1)S(1)}, u32[]{:S(2)}, u32[]{:S(2)}) %collective-permute-start.31) | collective-permute-done | bytes 589856 | tf_op jit(solution)/shard_map/ppermute | solution.py:717
  174.8 3.0 %collective-permute-done.33 = bf16[2,1,2,2,112,384]{5,4,3,2,1,0:T(8,128)(2,1)S(1)} collective-permute-done((bf16[2,1,2,2,112,384]{5,4,3,2,1,0:T(8,128)(2,1)S(1)}, bf16[2,1,2,2,112,384]{5,4,3,2,1,0:T(8,128)(2,1)S(1)}, u32[]{:S(2)}, u32[]{:S(2)}) %collective-permute-start.33) | collective-permute-done | bytes 688160 | tf_op jit(solution)/shard_map/ppermute | solution.py:717
  183.4 3.1 %collective-permute-done.35 = bf16[2,1,1,1,128,384]{5,4,2,1,0,3:T(8,128)(2,1)S(1)} collective-permute-done((bf16[2,1,1,1,128,384]{5,4,2,1,0,3:T(8,128)(2,1)S(1)}, bf16[2,1,1,1,128,384]{5,4,2,1,0,3:T(8,128)(2,1)S(1)}, u32[]{:S(2)}, u32[]{:S(2)}) %collective-permute-start.35) | collective-permute-done | bytes 196640 | tf_op jit(solution)/shard_map/ppermute | solution.py:717
  190.2 6.0 %collective-permute-done.34 = bf16[2,2,1,1,176,384]{5,4,3,2,1,0:T(8,128)(2,1)S(1)} collective-permute-done((bf16[2,2,1,1,176,384]{5,4,3,2,1,0:T(8,128)(2,1)S(1)}, bf16[2,2,1,1,176,384]{5,4,3,2,1,0:T(8,128)(2,1)S(1)}, u32[]{:S(2)}, u32[]{:S(2)}) %collective-permute-start.34) | collective-permute-done | bytes 540704 | tf_op jit(solution)/shard_map/ppermute | solution.py:717
  210.8 4.7 %collective-permute-start.46 = (bf16[1,1,1,1,672,384]{5,4,3,2,1,0:T(8,128)(2,1)S(1)}, bf16[1,1,1,1,672,384]{5,4,3,2,1,0:T(8,128)(2,1)S(1)}, u32[]{:S(2)}, u32[]{:S(2)}) collective-permute-start(bf16[1,1,1,1,672,384]{5,4,3,2,1,0:T(8,128)(2,1)S(1)} %slice_dynamic-update-slice_fusion.8), channel_id=1, source_target_pairs={{0,8},{1,9},{2,10},{3,11},{4,12},{5,13},{6,14},{7,15},{8,0},{9,1},... | collective-permute-start | bytes 1548296 | tf_op jit(solution)/shard_map/ppermute | solution.py:717
  219.0 13.9 %collective-permute-done.46 = bf16[1,1,1,1,672,384]{5,4,3,2,1,0:T(8,128)(2,1)S(1)} collective-permute-done((bf16[1,1,1,1,672,384]{5,4,3,2,1,0:T(8,128)(2,1)S(1)}, bf16[1,1,1,1,672,384]{5,4,3,2,1,0:T(8,128)(2,1)S(1)}, u32[]{:S(2)}, u32[]{:S(2)}) %collective-permute-start.46) | collective-permute-done | bytes 516128 | tf_op jit(solution)/shard_map/ppermute | solution.py:717
  234.0 3.5 %collective-permute-done.49 = bf16[2,1,1,1,48,384]{5,4,3,2,1,0:T(8,128)(2,1)S(1)} collective-permute-done((bf16[2,1,1,1,48,384]{5,4,3,2,1,0:T(8,128)(2,1)S(1)}, bf16[2,1,1,1,48,384]{5,4,3,2,1,0:T(8,128)(2,1)S(1)}, u32[]{:S(2)}, u32[]{:S(2)}) %collective-permute-start.49) | collective-permute-done | bytes 73760 | tf_op jit(solution)/shard_map/ppermute | solution.py:717
  238.0 4.7 %collective-permute-done.47 = bf16[2,1,1,1,80,384]{5,4,3,2,1,0:T(8,128)(2,1)S(1)} collective-permute-done((bf16[2,1,1,1,80,384]{5,4,3,2,1,0:T(8,128)(2,1)S(1)}, bf16[2,1,1,1,80,384]{5,4,3,2,1,0:T(8,128)(2,1)S(1)}, u32[]{:S(2)}, u32[]{:S(2)}) %collective-permute-start.47) | collective-permute-done | bytes 122912 | tf_op jit(solution)/shard_map/ppermute | solution.py:717
  246.3 3.1 %collective-permute-done.55 = bf16[2,1,2,1,48,384]{5,4,3,2,1,0:T(8,128)(2,1)S(1)} collective-permute-done((bf16[2,1,2,1,48,384]{5,4,3,2,1,0:T(8,128)(2,1)S(1)}, bf16[2,1,2,1,48,384]{5,4,3,2,1,0:T(8,128)(2,1)S(1)}, u32[]{:S(2)}, u32[]{:S(2)}) %collective-permute-start.55) | collective-permute-done | bytes 147488 | tf_op jit(solution)/shard_map/ppermute | solution.py:717
  249.5 2.8 %collective-permute-done.53 = bf16[2,2,1,1,80,384]{5,4,3,2,1,0:T(8,128)(2,1)S(1)} collective-permute-done((bf16[2,2,1,1,80,384]{5,4,3,2,1,0:T(8,128)(2,1)S(1)}, bf16[2,2,1,1,80,384]{5,4,3,2,1,0:T(8,128)(2,1)S(1)}, u32[]{:S(2)}, u32[]{:S(2)}) %collective-permute-start.53) | collective-permute-done | bytes 245792 | tf_op jit(solution)/shard_map/ppermute | solution.py:717
  256.2 7.4 %feed_spread.1 = (f32[1536,768]{1,0:T(8,128)}, f32[384,3072]{1,0:T(8,128)}) custom-call(s32[2]{0:T(128)} %pad_add_fusion.1.scalars, bf16[2,2,2,1,128,384]{5,4,3,2,1,0:T(8,128)(2,1)} %bitcast.78, bf16[2,2,2,1,128,384]{5,4,3,2,1,0:T(8,128)(2,1)} %bitcast.99, bf16[2,2,1,2,128,384]{5,4,3,2,1,0:T(8,128)(2,1)} %bitcast.79, ...), custom_call_target="tpu_custom_call" | custom-call | flops 7000000000 | tf_op jit(solution)/shard_map/feed_spread/pallas_call | solution.py:1155
  265.3 4.8 %later_spread.1 = (f32[384,768]{1,0:T(8,128)}, f32[384,768]{1,0:T(8,128)}, f32[384,768]{1,0:T(8,128)}, f32[384,768]{1,0:T(8,128)}, f32[1536]{0:T(1024)}, /*index...) custom-call(s32[2]{0:T(128)} %pad_add_fusion.1.scalars, ...), custom_call_target="tpu_custom_call" | custom-call | flops 4000000000 | tf_op jit(solution)/shard_map/later_spread/pallas_call | solution.py:1168
  (296 shorter events, 98.5 us)
Async XLA Ops:
  3.6 15.1 %collective-permute-start.1 = (bf16[384,768]{1,0:T(8,128)(2,1)}, bf16[384,768]{1,0:T(8,128)(2,1)S(1)}, u32[]{:S(2)}, u32[]{:S(2)}) collective-permute-start(bf16[384,768]{1,0:T(8,128)(2,1)} %refs_6_), channel_id=1, source_target_pairs={{0,16},{16,0},{1,17},{17,1},{2,18},{18,2},{3,19},{19,3},{4,20},{20... | collective-permute-start | bytes 1769480 | tf_op jit(solution)/shard_map/ppermute | solution.py:876
  4.2 14.6 %collective-permute-start.2 = (bf16[384,768]{1,0:T(8,128)(2,1)}, bf16[384,768]{1,0:T(8,128)(2,1)}, u32[]{:S(2)}, u32[]{:S(2)}) collective-permute-start(bf16[384,768]{1,0:T(8,128)(2,1)} %refs_8_), channel_id=1, source_target_pairs={{0,16},{16,0},{1,17},{17,1},{2,18},{18,2},{3,19},{19,3},{4,20},{20... | collective-permute-start | bytes 1769480 | tf_op jit(solution)/shard_map/ppermute | solution.py:876
  4.2 14.4 %collective-permute-start = (bf16[1,1,1,1,144,768]{5,4,3,2,1,0:T(8,128)(2,1)S(1)}, bf16[1,1,1,1,144,768]{5,4,3,2,1,0:T(8,128)(2,1)S(1)}, u32[]{:S(2)}, u32[]{:S(2)}) collective-permute-start(bf16[1,1,1,1,144,768]{5,4,3,2,1,0:T(8,128)(2,1)S(1)} %bitcast.74), channel_id=1, source_target_pairs={{0,8},{1,9},{2,10},{3,11},{4,12},{5,13},{6,14},{7,15},{8,0},{9,1},... | collective-permute-start | bytes 663560 | tf_op jit(solution)/shard_map/ppermute | solution.py:717
  39.0 16.0 %collective-permute-start.16 = (bf16[1536,768]{1,0:T(8,128)(2,1)}, bf16[1536,768]{1,0:T(8,128)(2,1)}, u32[]{:S(2)}, u32[]{:S(2)}) collective-permute-start(bf16[1536,768]{1,0:T(8,128)(2,1)} %refs_20_), channel_id=1, source_target_pairs={{0,16},{16,0},{1,17},{17,1},{2,18},{18,2},{3,19},{19,3},{4,20},{20... | collective-permute-start | bytes 7077896 | tf_op jit(solution)/shard_map/ppermute | solution.py:876
  39.1 15.9 %collective-permute-start.13 = (bf16[2,2,2,1,144,256]{5,4,3,2,1,0:T(8,128)(2,1)S(1)}, bf16[2,2,2,1,144,256]{5,4,3,2,1,0:T(8,128)(2,1)S(1)}, u32[]{:S(2)}, u32[]{:S(2)}) collective-permute-start(bf16[2,2,2,1,144,256]{5,4,3,2,1,0:T(8,128)(2,1)S(1)} %pad_maximum_fusion.3.refs_6_), channel_id=1, source_target_pairs={{0,1},{1,0},{2,3},{3,2},{4,5},{5,4},{6,7},{7,6},{8,9},{9,8},{10,11... | collective-permute-start | bytes 1769480 | tf_op jit(solution)/shard_map/ppermute | solution.py:717
  40.6 14.0 %collective-permute-start.14 = (bf16[2,2,1,2,128,256]{5,4,3,2,1,0:T(8,128)(2,1)S(1)}, bf16[2,2,1,2,128,256]{5,4,3,2,1,0:T(8,128)(2,1)S(1)}, u32[]{:S(2)}, u32[]{:S(2)}) collective-permute-start(bf16[2,2,1,2,128,256]{5,4,3,2,1,0:T(8,128)(2,1)S(1)} %pad_maximum_fusion.4.refs_8_), channel_id=1, source_target_pairs={{0,2},{1,3},{2,0},{3,1},{4,6},{5,7},{6,4},{7,5},{8,10},{9,11},{10,... | collective-permute-start | bytes 1572872 | tf_op jit(solution)/shard_map/ppermute | solution.py:717
  41.1 13.8 %collective-permute-start.15 = (bf16[2,1,2,2,128,256]{5,4,3,2,1,0:T(8,128)(2,1)S(1)}, bf16[2,1,2,2,128,256]{5,4,3,2,1,0:T(8,128)(2,1)}, u32[]{:S(2)}, u32[]{:S(2)}) collective-permute-start(bf16[2,1,2,2,128,256]{5,4,3,2,1,0:T(8,128)(2,1)S(1)} %pad_maximum_fusion.5.refs_10_), channel_id=1, source_target_pairs={{0,4},{1,5},{2,6},{3,7},{4,0},{5,1},{6,2},{7,3},{8,12},{9,13},{10,... | collective-permute-start | bytes 1572872 | tf_op jit(solution)/shard_map/ppermute | solution.py:717
  94.0 20.8 %collective-permute-start.19 = (bf16[2,2,2,1,128,384]{5,4,2,1,0,3:T(8,128)(2,1)}, bf16[2,2,2,1,128,384]{5,4,2,1,0,3:T(8,128)(2,1)S(1)}, u32[]{:S(2)}, u32[]{:S(2)}) collective-permute-start(bf16[2,2,2,1,128,384]{5,4,2,1,0,3:T(8,128)(2,1)} %get-tuple-element.237), channel_id=1, source_target_pairs={{0,1},{1,0},{2,3},{3,2},{4,5},{5,4},{6,7},{7,6},{8,9},{9,8},{10,11... | collective-permute-start | bytes 2359304 | tf_op jit(solution)/shard_map/ppermute | solution.py:717
  95.4 21.9 %collective-permute-start.20 = (bf16[2,2,1,2,128,384]{5,4,3,1,0,2:T(8,128)(2,1)S(1)}, bf16[2,2,1,2,128,384]{5,4,3,1,0,2:T(8,128)(2,1)S(1)}, u32[]{:S(2)}, u32[]{:S(2)}) collective-permute-start(bf16[2,2,1,2,128,384]{5,4,3,1,0,2:T(8,128)(2,1)S(1)} %get-tuple-element.238), channel_id=1, source_target_pairs={{0,2},{1,3},{2,0},{3,1},{4,6},{5,7},{6,4},{7,5},{8,10},{9,11},{10,... | collective-permute-start | bytes 2359304 | tf_op jit(solution)/shard_map/ppermute | solution.py:717
  96.1 22.6 %collective-permute-start.21 = (bf16[2,1,2,2,128,384]{5,4,3,2,1,0:T(8,128)(2,1)S(1)}, bf16[2,1,2,2,128,384]{5,4,3,2,1,0:T(8,128)(2,1)}, u32[]{:S(2)}, u32[]{:S(2)}) collective-permute-start(bf16[2,1,2,2,128,384]{5,4,3,2,1,0:T(8,128)(2,1)S(1)} %get-tuple-element.239), channel_id=1, source_target_pairs={{0,4},{1,5},{2,6},{3,7},{4,0},{5,1},{6,2},{7,3},{8,12},{9,13},{10,... | collective-permute-start | bytes 2359304 | tf_op jit(solution)/shard_map/ppermute | solution.py:717
  121.0 15.3 %collective-permute-start.25 = (bf16[2,2,2,208,384]{4,3,2,1,0:T(8,128)(2,1)}, bf16[2,2,2,208,384]{4,3,2,1,0:T(8,128)(2,1)}, u32[]{:S(2)}, u32[]{:S(2)}) collective-permute-start(bf16[2,2,2,208,384]{4,3,2,1,0:T(8,128)(2,1)} %get-tuple-element.267), channel_id=1, source_target_pairs={{0,16},{16,0},{1,17},{17,1},{2,18},{18,2},{3,19},{19,3},{4,20},{20... | collective-permute-start | bytes 3833864 | tf_op jit(solution)/shard_map/ppermute | solution.py:1131
  121.0 15.3 %collective-permute-start.26 = (bf16[2,2,2,208,384]{4,3,2,1,0:T(8,128)(2,1)}, bf16[2,2,2,208,384]{4,3,2,1,0:T(8,128)(2,1)S(1)}, u32[]{:S(2)}, u32[]{:S(2)}) collective-permute-start(bf16[2,2,2,208,384]{4,3,2,1,0:T(8,128)(2,1)} %get-tuple-element.268), channel_id=1, source_target_pairs={{0,16},{16,0},{1,17},{17,1},{2,18},{18,2},{3,19},{19,3},{4,20},{20... | collective-permute-start | bytes 3833864 | tf_op jit(solution)/shard_map/ppermute | solution.py:1131
  121.5 11.4 %collective-permute-start.22 = (bf16[2,2,1,1,128,384]{5,4,2,1,0,3:T(8,128)(2,1)}, bf16[2,2,1,1,128,384]{5,4,2,1,0,3:T(8,128)(2,1)}, u32[]{:S(2)}, u32[]{:S(2)}) collective-permute-start(bf16[2,2,1,1,128,384]{5,4,2,1,0,3:T(8,128)(2,1)} %slice.417), channel_id=1, source_target_pairs={{0,2},{1,3},{2,0},{3,1},{4,6},{5,7},{6,4},{7,5},{8,10},{9,11},{10,... | collective-permute-start | bytes 1179656 | tf_op jit(solution)/shard_map/ppermute | solution.py:717
  122.8 11.2 %collective-permute-start.23 = (bf16[2,1,1,2,128,384]{5,4,3,1,0,2:T(8,128)(2,1)S(1)}, bf16[2,1,1,2,128,384]{5,4,3,1,0,2:T(8,128)(2,1)}, u32[]{:S(2)}, u32[]{:S(2)}) collective-permute-start(bf16[2,1,1,2,128,384]{5,4,3,1,0,2:T(8,128)(2,1)S(1)} %slice.418), channel_id=1, source_target_pairs={{0,4},{1,5},{2,6},{3,7},{4,0},{5,1},{6,2},{7,3},{8,12},{9,13},{10,... | collective-permute-start | bytes 1179656 | tf_op jit(solution)/shard_map/ppermute | solution.py:717
  123.5 11.7 %collective-permute-start.24 = (bf16[2,1,2,1,128,384]{5,4,3,2,1,0:T(8,128)(2,1)}, bf16[2,1,2,1,128,384]{5,4,3,2,1,0:T(8,128)(2,1)}, u32[]{:S(2)}, u32[]{:S(2)}) collective-permute-start(bf16[2,1,2,1,128,384]{5,4,3,2,1,0:T(8,128)(2,1)} %slice.419), channel_id=1, source_target_pairs={{0,1},{1,0},{2,3},{3,2},{4,5},{5,4},{6,7},{7,6},{8,9},{9,8},{10,11... | collective-permute-start | bytes 1179656 | tf_op jit(solution)/shard_map/ppermute | solution.py:717
  147.8 26.8 %collective-permute-start.31 = (bf16[1,1,1,1,768,384]{5,4,3,2,1,0:T(8,128)(2,1)S(1)}, bf16[1,1,1,1,768,384]{5,4,3,2,1,0:T(8,128)(2,1)S(1)}, u32[]{:S(2)}, u32[]{:S(2)}) collective-permute-start(bf16[1,1,1,1,768,384]{5,4,3,2,1,0:T(8,128)(2,1)S(1)} %slice_dynamic-update-slice_fusion), channel_id=1, source_target_pairs={{0,8},{1,9},{2,10},{3,11},{4,12},{5,13},{6,14},{7,15},{8,0},{9,1},... | collective-permute-start | bytes 1769480 | tf_op jit(solution)/shard_map/ppermute | solution.py:717
  151.1 26.7 %collective-permute-start.33 = (bf16[2,1,2,2,112,384]{5,4,3,2,1,0:T(8,128)(2,1)S(1)}, bf16[2,1,2,2,112,384]{5,4,3,2,1,0:T(8,128)(2,1)S(1)}, u32[]{:S(2)}, u32[]{:S(2)}) collective-permute-start(bf16[2,1,2,2,112,384]{5,4,3,2,1,0:T(8,128)(2,1)S(1)} %maximum_bitcast_fusion.4), channel_id=1, source_target_pairs={{0,4},{1,5},{2,6},{3,7},{4,0},{5,1},{6,2},{7,3},{8,12},{9,13},{10,... | collective-permute-start | bytes 2064392 | tf_op jit(solution)/shard_map/ppermute | solution.py:717
  152.4 25.6 %collective-permute-start.30 = (bf16[2,2,2,1,176,384]{5,4,3,2,1,0:T(8,128)(2,1)S(1)}, bf16[2,2,2,1,176,384]{5,4,3,2,1,0:T(8,128)(2,1)S(1)}, u32[]{:S(2)}, u32[]{:S(2)}) collective-permute-start(bf16[2,2,2,1,176,384]{5,4,3,2,1,0:T(8,128)(2,1)S(1)} %maximum_bitcast_fusion.1), channel_id=1, source_target_pairs={{0,1},{1,0},{2,3},{3,2},{4,5},{5,4},{6,7},{7,6},{8,9},{9,8},{10,11... | collective-permute-start | bytes 3244040 | tf_op jit(solution)/shard_map/ppermute | solution.py:717
  153.1 25.2 %collective-permute-start.32 = (bf16[2,2,1,2,176,384]{5,4,3,2,1,0:T(8,128)(2,1)S(1)}, bf16[2,2,1,2,176,384]{5,4,3,2,1,0:T(8,128)(2,1)S(1)}, u32[]{:S(2)}, u32[]{:S(2)}) collective-permute-start(bf16[2,2,1,2,176,384]{5,4,3,2,1,0:T(8,128)(2,1)S(1)} %maximum_bitcast_fusion.2), channel_id=1, source_target_pairs={{0,2},{1,3},{2,0},{3,1},{4,6},{5,7},{6,4},{7,5},{8,10},{9,11},{10,... | collective-permute-start | bytes 3244040 | tf_op jit(solution)/shard_map/ppermute | solution.py:717
  181.9 14.4 %collective-permute-start.34 = (bf16[2,2,1,1,176,384]{5,4,3,2,1,0:T(8,128)(2,1)S(1)}, bf16[2,2,1,1,176,384]{5,4,3,2,1,0:T(8,128)(2,1)S(1)}, u32[]{:S(2)}, u32[]{:S(2)}) collective-permute-start(bf16[2,2,1,1,176,384]{5,4,3,2,1,0:T(8,128)(2,1)S(1)} %slice.442), channel_id=1, source_target_pairs={{0,2},{1,3},{2,0},{3,1},{4,6},{5,7},{6,4},{7,5},{8,10},{9,11},{10,... | collective-permute-start | bytes 1622024 | tf_op jit(solution)/shard_map/ppermute | solution.py:717
  210.8 22.1 %collective-permute-start.46 = (bf16[1,1,1,1,672,384]{5,4,3,2,1,0:T(8,128)(2,1)S(1)}, bf16[1,1,1,1,672,384]{5,4,3,2,1,0:T(8,128)(2,1)S(1)}, u32[]{:S(2)}, u32[]{:S(2)}) collective-permute-start(bf16[1,1,1,1,672,384]{5,4,3,2,1,0:T(8,128)(2,1)S(1)} %slice_dynamic-update-slice_fusion.8), channel_id=1, source_target_pairs={{0,8},{1,9},{2,10},{3,11},{4,12},{5,13},{6,14},{7,15},{8,0},{9,1},... | collective-permute-start | bytes 1548296 | tf_op jit(solution)/shard_map/ppermute | solution.py:717
  215.5 28.0 %collective-permute-start.50 = (bf16[2,2,2,1,128,384]{5,4,2,1,0,3:T(8,128)(2,1)S(1)}, bf16[2,2,2,1,128,384]{5,4,2,1,0,3:T(8,128)(2,1)S(1)}, u32[]{:S(2)}, u32[]{:S(2)}) collective-permute-start(bf16[2,2,2,1,128,384]{5,4,2,1,0,3:T(8,128)(2,1)S(1)} %pad_maximum_fusion), channel_id=1, source_target_pairs={{0,1},{1,0},{2,3},{3,2},{4,5},{5,4},{6,7},{7,6},{8,9},{9,8},{10,11... | collective-permute-start | bytes 2359304 | tf_op jit(solution)/shard_map/ppermute | solution.py:717
  216.4 27.1 %collective-permute-start.51 = (bf16[2,2,1,2,128,384]{5,4,3,1,0,2:T(8,128)(2,1)S(1)}, bf16[2,2,1,2,128,384]{5,4,3,1,0,2:T(8,128)(2,1)S(1)}, u32[]{:S(2)}, u32[]{:S(2)}) collective-permute-start(bf16[2,2,1,2,128,384]{5,4,3,1,0,2:T(8,128)(2,1)S(1)} %pad_maximum_fusion.1), channel_id=1, source_target_pairs={{0,2},{1,3},{2,0},{3,1},{4,6},{5,7},{6,4},{7,5},{8,10},{9,11},{10,... | collective-permute-start | bytes 2359304 | tf_op jit(solution)/shard_map/ppermute | solution.py:717
  217.5 26.1 %collective-permute-start.52 = (bf16[2,1,2,2,128,384]{5,4,3,2,1,0:T(8,128)(2,1)S(1)}, bf16[2,1,2,2,128,384]{5,4,3,2,1,0:T(8,128)(2,1)S(1)}, u32[]{:S(2)}, u32[]{:S(2)}) collective-permute-start(bf16[2,1,2,2,128,384]{5,4,3,2,1,0:T(8,128)(2,1)S(1)} %pad_maximum_fusion.2.refs_4_), channel_id=1, source_target_pairs={{0,4},{1,5},{2,6},{3,7},{4,0},{5,1},{6,2},{7,3},{8,12},{9,13},{10,... | collective-permute-start | bytes 2359304 | tf_op jit(solution)/shard_map/ppermute | solution.py:717
  (69 other events, 603.4 us)

commit v6 on v5

--- a/solution.py
+++ b/solution.py
@@ -184,7 +184,7 @@
     micro_count = path.shape[0]
 
     def attend(pair, carry):
-        lanes = pl.ds(pl.multiple_of(pair * 128, 128), 128)
+        lanes = pl.ds(pair * 128, 128)
         attend_kernel(
             run,
             slots,
@@ -201,7 +201,8 @@
         )
         return carry
 
-    lax.fori_loop(0, rows.shape[1] // 128, attend, 0)
+    for pair in range(rows.shape[1] // 128):
+        attend(pair, 0)
     leaving.append(pltpu.make_async_copy(probs, probs_out, out_sems.at[3]))
     leaving[-1].start()
     feed_kernel(
@@ -680,33 +681,38 @@
 
 
 def later_spread_kernel(scalars, *refs):
-    weights, inner_bias, vectors, embed, table, sources, sems = refs[6:10], refs[10], refs[11:18], *refs[18:20], refs[20:23], refs[23]
-    collect_pieces(refs[:6], sources, sems)
+    weights, inner_bias, vectors, embed, table, small = refs[6:10], refs[10], refs[11:18], *refs[18:21]
     place = scalars[1]
-    side = sources[0].shape[-1]
+    side = refs[0].shape[-1]
     rows = weights[0].shape[0] // 8
     cuts = later_cuts(2 * side)
-    for chunk in range(16):
-        at = block_index(chunk ^ place, 4)
-        down, across = (chunk // 2) * rows, (chunk % 2) * side
-        for source, (start, height) in zip(sources, cuts):
-            value = source[at].astype(f32)
+    for relative in range(16):
+        chunk = relative ^ place
+        down = pl.multiple_of((chunk // 2) * rows, 16)
+        across = pl.ds(pl.multiple_of((chunk % 2) * side, 128), side)
+        at = block_index(relative, 4)
+        for part, (start, height) in enumerate(cuts):
+            axis = 3 - routes_out[part][0]
+            inside = tuple(0 if i == axis else bit for i, bit in enumerate(at))
+            value = refs[2 * part + at[axis]][inside].astype(f32)
             for which in range(4):
                 begin, end = max(start, which * rows), min(start + height, (which + 1) * rows)
                 if begin < end:
-                    top = down + begin - which * rows
-                    weights[which][top : top + end - begin, across : across + side] = value[begin - start : end - start]
+                    here = pl.ds(pl.multiple_of(down + begin - which * rows, 16), end - begin)
+                    weights[which][here, across] = value[begin - start : end - start]
             begin = 4 * rows
             if start <= begin < start + height:
-                line = value[begin - start : begin - start + 1]
-                if chunk < 4:
-                    inner_bias[chunk * side : (chunk + 1) * side] = line.reshape(side)
-                elif chunk < 11:
-                    vectors[chunk - 4][...] = line.reshape(side)
-                elif chunk < 13:
-                    embed[chunk - 11 : chunk - 10, :] = line
-                elif chunk == 13:
-                    table[...] = value[begin - start : begin - start + table.shape[0], : table.shape[1]]
+                small[chunk] = value[begin - start : begin - start + 16]
+    for chunk in range(14):
+        line = small[chunk, :1]
+        if chunk < 4:
+            inner_bias[chunk * side : (chunk + 1) * side] = line.reshape(side)
+        elif chunk < 11:
+            vectors[chunk - 4][...] = line.reshape(side)
+        elif chunk < 13:
+            embed[chunk - 11 : chunk - 10, :] = line
+        else:
+            table[...] = small[chunk, : table.shape[0], : table.shape[1]]
 
 
 routes_out = ((0, 1, 2), (1, 2, 0), (2, 0, 1))
@@ -943,6 +949,10 @@
 
     grown = pltpu.CompilerParams(vmem_limit_bytes=vmem_bytes)
 
+    def granted(mebibytes):
+        return pltpu.CompilerParams(vmem_limit_bytes=mebibytes * 1024 * 1024)
+
+
     def shape(dims, kind):
         return jax.ShapeDtypeStruct(dims, kind)
 
@@ -953,7 +963,7 @@
         in_specs=[smem_space, vmem_space, vmem_space] + [any_space] * pieces,
         out_specs=(vmem_space,) * 2,
         scratch_shapes=[pltpu.VMEM((model, model), low), dma((pieces,))],
-        compiler_params=grown,
+        compiler_params=granted(16),
         name="query_projection",
         cost_estimate=cost(1),
     )(early, rows, vectors, *query_weights)
@@ -1062,7 +1072,7 @@
                 pl.BlockSpec((8, 128), lambda pair: (0, pair)),
                 pl.BlockSpec((2, 16, span), lambda pair: (pair, 0, 0)),
             ),
-            compiler_params=grown,
+            compiler_params=granted(24),
             name="attend_back",
             cost_estimate=cost(3),
         )(scalars, query_low, query_segment, keys, values, probs, gradient, attended, vectors)
@@ -1103,7 +1113,7 @@
         in_specs=[smem_space] + [vmem_space] * 15,
         out_specs=grad_specs,
         scratch_shapes=extra,
-        compiler_params=grown,
+        compiler_params=granted(40),
         name="weight_gradients",
         cost_estimate=cost(3),
     )(scalars, rows, path, attended, d_branch, small_first, *back_first, *back_second)
@@ -1122,7 +1132,7 @@
             dma((3 * pieces,)),
             dma((6,)),
         ],
-        compiler_params=grown,
+        compiler_params=granted(40),
         name="tree_gradients",
         cost_estimate=cost(3),
     )(scalars, found, d_mid_in, *back_first[:3], *back_second[:3], *query_weights, *key_weights, *value_weights)
@@ -1158,7 +1168,7 @@
             in_specs=[smem_space] + [any_space] * 6,
             out_specs=(vmem_space,) * 2,
             scratch_shapes=pieces_scratch([height for _, height in feed_cuts(pieces, model)]),
-            compiler_params=grown,
+            compiler_params=granted(32),
             name="feed_spread",
             cost_estimate=cost(7),
         )(early, *feed_done)
@@ -1171,10 +1181,10 @@
             + [shape(b_inner.shape, f32)]
             + [shape(b_outer.shape, f32)] * 7
             + [shape(seg_embed.shape, f32), shape(rel_table.shape, f32)],
-            in_specs=[smem_space] + [any_space] * 6,
+            in_specs=[smem_space] + [vmem_space] * 6,
             out_specs=[vmem_space] * 14,
-            scratch_shapes=pieces_scratch(heights),
-            compiler_params=grown,
+            scratch_shapes=[pltpu.VMEM((dp_count, 16, half), f32)],
+            compiler_params=granted(20),
             name="later_spread",
             cost_estimate=cost(4),
         )(early, *later_done)

time: 271 us -> 265 us (0.978)
  Pallas kernels: 76.7 us -> 62.5 us
  waiting for transfers between devices: 99.1 us -> 106 us
  other arithmetic: 20 us -> 13.4 us
  local copies, waits for them, and re-layouts: 16.9 us -> 21.6 us
    unnamed x83 -> x111, local copies, waits for them, and re-layouts: 4.7 us -> 11.5 us
    ppermute x48, waiting for transfers between devices: 99 us -> 106 us  [send(): return lax.ppermute(inputs, 'dp', [(i, i ^ 1 << bit) for i in range(count)])]
    concatenate x8, other arithmetic: 0.28 us -> 6.35 us  [grow(): return jnp.concatenate([held, send(held, bit)], axis=bit_total() - 1 - bit)]
    add x6, other arithmetic: 5.25 us -> 1.2 us  [sum_rounds(): own + send(entry, route[0])]
    pallas_call x1, Pallas kernels: 8.96 us -> 5.15 us  [shards(): pl.pallas_call(functools.partial(weights_kernel, pieces), out_shape=grad_...]
    add x12, other arithmetic: 3.63 us -> 0.52 us  [sum_rounds(): part_of(entry, route[step], 0) + send(other, route[step])]
    pallas_call x1, Pallas kernels: 8.76 us -> 5.75 us  [shards(): pl.pallas_call(functools.partial(tree_kernel, pieces, run, slots), out_sh...]
  transfers between devices with their start and end apart: 59 -> 59, of which waited for: 33 -> 38; matrix products, arithmetic and copies ran while one was open for 9% -> 8% of each run, Pallas kernels for 16% -> 12%
where the time goes in v6:
time: 265 us; the launch traced here: 262 us
  waiting for transfers between devices  106 us (40%)
  Pallas kernels  62.5 us (24%)
  starting transfers between devices  56.4 us (21%)
  local copies, waits for them, and re-layouts  21.6 us (8%)
  other arithmetic  13.4 us (5%)
    ppermute x48, waiting for transfers between devices, send(): return lax.ppermute(inputs, 'dp', [(i, i ^ 1 << bit) for i in range(count)])  106 us
    ppermute x48, starting transfers between devices, send(): return lax.ppermute(inputs, 'dp', [(i, i ^ 1 << bit) for i in range(count)])  54.4 us
    pallas_call x1, Pallas kernels, shards(): pl.pallas_call(functools.partial(forward_kernel, pieces, columns, [route[...  28.7 us
    pallas_call x2, Pallas kernels, attend_back(): pl.pallas_call(functools.partial(back_kernel, run, slots), grid=(pair_cou...  12.9 us
    unnamed x111, local copies, waits for them, and re-layouts  11.5 us
    concatenate x8, other arithmetic, grow(): return jnp.concatenate([held, send(held, bit)], axis=bit_total() - 1 - bit)  6.35 us
    pallas_call x1, Pallas kernels, shards(): pl.pallas_call(functools.partial(tree_kernel, pieces, run, slots), out_sh...  5.75 us
    concatenate x1, local copies, waits for them, and re-layouts, shards(): jnp.concatenate(flat + [jnp.zeros((fill,), low)]).reshape(16, part_width)  5.61 us
  transfers between devices with their start and end apart: 59, of which 38 were waited for; matrix products, arithmetic and copies ran while one was open for 8% of the time, Pallas kernels for 12%

profile of v6, /device:TPU:0, one launch (start us, length us, event | category | flops | bytes accessed | tf_op | source)
XLA Modules:
  0.0 261.7 jit_solution(7476733996001680764)
XLA Ops:
  4.2 4.0 %collective-permute-start = (bf16[1,1,1,1,144,768]{5,4,3,2,1,0:T(8,128)(2,1)S(1)}, bf16[1,1,1,1,144,768]{5,4,3,2,1,0:T(8,128)(2,1)S(1)}, u32[]{:S(2)}, u32[]{:S(2)}) collective-permute-start(bf16[1,1,1,1,144,768]{5,4,3,2,1,0:T(8,128)(2,1)S(1)} %bitcast.86), channel_id=1, source_target_pairs={{0,8},{1,9},{2,10},{3,11},{4,12},{5,13},{6,14},{7,15},{8,0},{9,1},... | collective-permute-start | bytes 663560 | tf_op jit(solution)/shard_map/ppermute | solution.py:723
  9.8 5.6 %concatenate.123 = bf16[6144]{0:T(1024)(128)(2,1)S(1)} concatenate(bf16[1536]{0:T(1024)(128)(2,1)} %param.34, bf16[384]{0:T(512)(128)(2,1)} %param.35, bf16[384]{0:T(512)(128)(2,1)} %param.36, bf16[384]{0:T(512)(128)(2,1)} %param.37, bf16[384]{0:T(512)(128)(2,1)} %param.38, bf16[384]{0:T(512)(128)(2,1)} %param.39, bf16[384]{0:T(512)(128)(2,1)} %param.40, bf16[384]{0:T(512)(128)(2,1)} %param.41, ...), dimensions={0} | concatenate | bytes 24576 | tf_op jit(solution)/shard_map/concatenate | solution.py:905
  15.4 3.2 %collective-permute-done = bf16[1,1,1,1,144,768]{5,4,3,2,1,0:T(8,128)(2,1)S(1)} collective-permute-done((bf16[1,1,1,1,144,768]{5,4,3,2,1,0:T(8,128)(2,1)S(1)}, bf16[1,1,1,1,144,768]{5,4,3,2,1,0:T(8,128)(2,1)S(1)}, u32[]{:S(2)}, u32[]{:S(2)}) %collective-permute-start) | collective-permute-done | bytes 221216 | tf_op jit(solution)/shard_map/ppermute | solution.py:723
  34.6 3.7 %collective-permute-done.9 = bf16[2,1,1,2,128,256]{5,4,3,2,1,0:T(8,128)(2,1)S(1)} collective-permute-done((bf16[2,1,1,2,128,256]{5,4,3,2,1,0:T(8,128)(2,1)S(1)}, bf16[2,1,1,2,128,256]{5,4,3,2,1,0:T(8,128)(2,1)S(1)}, u32[]{:S(2)}, u32[]{:S(2)}) %collective-permute-start.9) | collective-permute-done | bytes 262176 | tf_op jit(solution)/shard_map/ppermute | solution.py:723
  49.3 8.2 %collective-permute-done.14.refs_9_ = bf16[2,2,1,2,128,256]{5,4,3,2,1,0:T(8,128)(2,1)S(1)} collective-permute-done((bf16[2,2,1,2,128,256]{5,4,3,2,1,0:T(8,128)(2,1)S(1)}, bf16[2,2,1,2,128,256]{5,4,3,2,1,0:T(8,128)(2,1)S(1)}, u32[]{:S(2)}, u32[]{:S(2)}) %collective-permute-start.14) | collective-permute-done | bytes 524320 | tf_op jit(solution)/shard_map/ppermute | solution.py:723
  60.1 28.7 %forward.1 = (bf16[2,384,768]{2,1,0:T(8,128)(2,1)}, bf16[768,768]{1,0:T(8,128)(2,1)}, bf16[768,768]{1,0:T(8,128)(2,1)}, bf16[12,256,384]{2,1,0:T(8,128)(2,1)}, s...) custom-call(s32[12]{0:T(128)} %pad_add_fusion.scalars, ...), custom_call_target="tpu_custom_call" | custom-call | flops 35999997952 | tf_op jit(solution)/shard_map/forward/pallas_call | solution.py:989
  95.7 4.3 %attend_back.2 = (bf16[256,256]{1,0:T(8,128)(2,1)S(1)}, bf16[768,256]{1,0:T(8,128)(2,1)S(1)}, bf16[768,256]{1,0:T(8,128)(2,1)S(1)}, f32[8,256]{1,0:T(8,128)S(1)}, f32[4,16,384]{2,1,0:T(8,128)S(1)}) custom-call(s32[12]{0:T(128)S(1)} %copy-done.4, bf16[256,768]{1,0:T(8,128)(2,1)S(1)} %copy-done.16, bf16[256,768]{1,0:T(8,128)(2,1)S(1)} %copy-done.18, ...), custom_call_target="tpu_custom_call" | custom-call | flops 3000000000 | tf_op jit(solution)/shard_map/attend_back/pallas_call | solution.py:1057
  103.6 8.5 %attend_back.3 = (bf16[256,512]{1,0:T(8,128)(2,1)S(1)}, bf16[768,512]{1,0:T(8,128)(2,1)S(1)}, bf16[768,512]{1,0:T(8,128)(2,1)S(1)}, f32[8,512]{1,0:T(8,128)S(1)}, f32[8,16,384]{2,1,0:T(8,128)S(1)}) custom-call(s32[12]{0:T(128)S(1)} %copy-done.4, bf16[256,768]{1,0:T(8,128)(2,1)S(1)} %copy-done.16, bf16[256,768]{1,0:T(8,128)(2,1)S(1)} %copy-done.18, ...), custom_call_target="tpu_custom_call" | custom-call | flops 3000000000 | tf_op jit(solution)/shard_map/attend_back/pallas_call | solution.py:1057
  112.2 5.2 %weight_gradients.1 = (bf16[2,2,2,208,384]{4,3,2,1,0:T(8,128)(2,1)S(1)}, bf16[2,2,2,208,384]{4,3,2,1,0:T(8,128)(2,1)S(1)}, bf16[2,2,2,208,384]{4,3,2,1,0:T(8,128)(2,1)S(1)}, bf16[2,2,2,208,384]{4,3,2,1,0:T(8,128)(2,1)S(1)}) custom-call(s32[12]{0:T(128)S(1)} %copy-done.4, bf16[256,768]{1,0:T(8,128)(2,1)S(1)} %bitcast.78, bf16[768,768]{1,0:T(8,128)(2,1)S(1)} %bitcast.85, ...), custom_call_target="tpu_custom_call" | custom-call | flops 3000000000 | tf_op jit(solution)/shard_map/weight_gradients/pallas_call | solution.py:1110
  117.4 2.7 %collective-permute-done.19 = bf16[2,2,2,1,128,384]{5,4,2,1,0,3:T(8,128)(2,1)S(1)} collective-permute-done((bf16[2,2,2,1,128,384]{5,4,2,1,0,3:T(8,128)(2,1)S(1)}, bf16[2,2,2,1,128,384]{5,4,2,1,0,3:T(8,128)(2,1)S(1)}, u32[]{:S(2)}, u32[]{:S(2)}) %collective-permute-start.19) | collective-permute-done | bytes 786464 | tf_op jit(solution)/shard_map/ppermute | solution.py:723
  125.6 5.7 %tree_gradients.1 = (f32[2,64,768]{2,1,0:T(8,128)S(1)}, f32[2,64,768]{2,1,0:T(8,128)}, bf16[2,2,2,256,384]{4,3,2,1,0:T(8,128)(2,1)S(1)}, bf16[2,2,2,256,384]{4,3,2,1,0:T(8,128)(2,1)S(1)}) custom-call(s32[12]{0:T(128)S(1)} %copy-done.4, s32[12]{0:T(128)S(1)} %copy-done.29, f32[256,768]{1,0:T(8,128)S(1)} %copy-done.23, ...), custom_call_target="tpu_custom_call" | custom-call | flops 3000000000 | tf_op jit(solution)/shard_map/tree_gradients/pallas_call | solution.py:1124
  138.6 2.9 %collective-permute-done.27 = bf16[2,1,1,1,128,384]{5,4,2,1,0,3:T(8,128)(2,1)S(1)} collective-permute-done((bf16[2,1,1,1,128,384]{5,4,2,1,0,3:T(8,128)(2,1)S(1)}, bf16[2,1,1,1,128,384]{5,4,2,1,0,3:T(8,128)(2,1)S(1)}, u32[]{:S(2)}, u32[]{:S(2)}) %collective-permute-start.27) | collective-permute-done | bytes 196640 | tf_op jit(solution)/shard_map/ppermute | solution.py:723
  143.2 3.3 %collective-permute-start.31 = (bf16[1,1,1,1,768,384]{5,4,3,2,1,0:T(8,128)(2,1)S(1)}, bf16[1,1,1,1,768,384]{5,4,3,2,1,0:T(8,128)(2,1)S(1)}, u32[]{:S(2)}, u32[]{:S(2)}) collective-permute-start(bf16[1,1,1,1,768,384]{5,4,3,2,1,0:T(8,128)(2,1)S(1)} %slice_dynamic-update-slice_fusion), channel_id=1, source_target_pairs={{0,8},{1,9},{2,10},{3,11},{4,12},{5,13},{6,14},{7,15},{8,0},{9,1},... | collective-permute-start | bytes 1769480 | tf_op jit(solution)/shard_map/ppermute | solution.py:723
  149.4 20.5 %collective-permute-done.31 = bf16[1,1,1,1,768,384]{5,4,3,2,1,0:T(8,128)(2,1)S(1)} collective-permute-done((bf16[1,1,1,1,768,384]{5,4,3,2,1,0:T(8,128)(2,1)S(1)}, bf16[1,1,1,1,768,384]{5,4,3,2,1,0:T(8,128)(2,1)S(1)}, u32[]{:S(2)}, u32[]{:S(2)}) %collective-permute-start.31) | collective-permute-done | bytes 589856 | tf_op jit(solution)/shard_map/ppermute | solution.py:723
  170.2 3.5 %collective-permute-done.33 = bf16[2,1,2,2,112,384]{5,4,3,2,1,0:T(8,128)(2,1)S(1)} collective-permute-done((bf16[2,1,2,2,112,384]{5,4,3,2,1,0:T(8,128)(2,1)S(1)}, bf16[2,1,2,2,112,384]{5,4,3,2,1,0:T(8,128)(2,1)S(1)}, u32[]{:S(2)}, u32[]{:S(2)}) %collective-permute-start.33) | collective-permute-done | bytes 688160 | tf_op jit(solution)/shard_map/ppermute | solution.py:723
  178.9 3.6 %collective-permute-done.35 = bf16[2,1,1,1,128,384]{5,4,2,1,0,3:T(8,128)(2,1)S(1)} collective-permute-done((bf16[2,1,1,1,128,384]{5,4,2,1,0,3:T(8,128)(2,1)S(1)}, bf16[2,1,1,1,128,384]{5,4,2,1,0,3:T(8,128)(2,1)S(1)}, u32[]{:S(2)}, u32[]{:S(2)}) %collective-permute-start.35) | collective-permute-done | bytes 196640 | tf_op jit(solution)/shard_map/ppermute | solution.py:723
  185.4 6.5 %collective-permute-done.34 = bf16[2,2,1,1,176,384]{5,4,3,2,1,0:T(8,128)(2,1)S(1)} collective-permute-done((bf16[2,2,1,1,176,384]{5,4,3,2,1,0:T(8,128)(2,1)S(1)}, bf16[2,2,1,1,176,384]{5,4,3,2,1,0:T(8,128)(2,1)S(1)}, u32[]{:S(2)}, u32[]{:S(2)}) %collective-permute-start.34) | collective-permute-done | bytes 540704 | tf_op jit(solution)/shard_map/ppermute | solution.py:723
  204.3 2.7 %collective-permute-done.42 = bf16[2,1,1,2,128,384]{5,4,3,1,0,2:T(8,128)(2,1)S(1)} collective-permute-done((bf16[2,1,1,2,128,384]{5,4,3,1,0,2:T(8,128)(2,1)S(1)}, bf16[2,1,1,2,128,384]{5,4,3,1,0,2:T(8,128)(2,1)S(1)}, u32[]{:S(2)}, u32[]{:S(2)}) %collective-permute-start.42) | collective-permute-done | bytes 393248 | tf_op jit(solution)/shard_map/ppermute | solution.py:723
  214.5 12.3 %collective-permute-done.46 = bf16[1,1,1,1,672,384]{5,4,3,2,1,0:T(8,128)(2,1)S(1)} collective-permute-done((bf16[1,1,1,1,672,384]{5,4,3,2,1,0:T(8,128)(2,1)S(1)}, bf16[1,1,1,1,672,384]{5,4,3,2,1,0:T(8,128)(2,1)S(1)}, u32[]{:S(2)}, u32[]{:S(2)}) %collective-permute-start.46) | collective-permute-done | bytes 516128 | tf_op jit(solution)/shard_map/ppermute | solution.py:723
  227.9 3.5 %collective-permute-done.49 = bf16[2,1,1,1,48,384]{5,4,3,2,1,0:T(8,128)(2,1)S(1)} collective-permute-done((bf16[2,1,1,1,48,384]{5,4,3,2,1,0:T(8,128)(2,1)S(1)}, bf16[2,1,1,1,48,384]{5,4,3,2,1,0:T(8,128)(2,1)S(1)}, u32[]{:S(2)}, u32[]{:S(2)}) %collective-permute-start.49) | collective-permute-done | bytes 73760 | tf_op jit(solution)/shard_map/ppermute | solution.py:723
  232.1 4.9 %collective-permute-done.47 = bf16[2,1,1,1,80,384]{5,4,3,2,1,0:T(8,128)(2,1)S(1)} collective-permute-done((bf16[2,1,1,1,80,384]{5,4,3,2,1,0:T(8,128)(2,1)S(1)}, bf16[2,1,1,1,80,384]{5,4,3,2,1,0:T(8,128)(2,1)S(1)}, u32[]{:S(2)}, u32[]{:S(2)}) %collective-permute-start.47) | collective-permute-done | bytes 122912 | tf_op jit(solution)/shard_map/ppermute | solution.py:723
  244.7 2.9 %collective-permute-done.54 = bf16[2,1,1,2,80,384]{5,4,3,2,1,0:T(8,128)(2,1)S(1)} collective-permute-done((bf16[2,1,1,2,80,384]{5,4,3,2,1,0:T(8,128)(2,1)S(1)}, bf16[2,1,1,2,80,384]{5,4,3,2,1,0:T(8,128)(2,1)S(1)}, u32[]{:S(2)}, u32[]{:S(2)}) %collective-permute-start.54) | collective-permute-done | bytes 245792 | tf_op jit(solution)/shard_map/ppermute | solution.py:723
  250.7 5.3 %feed_spread.1 = (f32[1536,768]{1,0:T(8,128)}, f32[384,3072]{1,0:T(8,128)}) custom-call(s32[2]{0:T(128)S(1)} %pad_add_fusion.1.scalars, bf16[2,2,2,1,128,384]{5,4,3,2,1,0:T(8,128)(2,1)S(1)} %bitcast.74, bf16[2,2,2,1,128,384]{5,4,3,2,1,0:T(8,128)(2,1)S(1)} %bitcast.83, bf16[2,2,1,2,128,384]{5,4,3,2,1,0:T(8,128)(2,1)S(1)} %bitcast.75, ...), custom_call_target="tpu_custom_call" | custom-call | flops 7000000000 | tf_op jit(solution)/shard_map/feed_spread/pallas_call | solution.py:1165
  258.5 3.0 %later_spread.1 = (f32[384,768]{1,0:T(8,128)}, f32[384,768]{1,0:T(8,128)}, f32[384,768]{1,0:T(8,128)}, f32[384,768]{1,0:T(8,128)}, f32[1536]{0:T(1024)}, /*index...) custom-call(s32[2]{0:T(128)S(1)} %pad_add_fusion.1.scalars, ...), custom_call_target="tpu_custom_call" | custom-call | flops 4000000000 | tf_op jit(solution)/shard_map/later_spread/pallas_call | solution.py:1178
  (324 shorter events, 104.9 us)
Async XLA Ops:
  3.6 15.1 %collective-permute-start.1 = (bf16[384,768]{1,0:T(8,128)(2,1)}, bf16[384,768]{1,0:T(8,128)(2,1)S(1)}, u32[]{:S(2)}, u32[]{:S(2)}) collective-permute-start(bf16[384,768]{1,0:T(8,128)(2,1)} %refs_6_), channel_id=1, source_target_pairs={{0,16},{16,0},{1,17},{17,1},{2,18},{18,2},{3,19},{19,3},{4,20},{20... | collective-permute-start | bytes 1769480 | tf_op jit(solution)/shard_map/ppermute | solution.py:882
  4.1 14.6 %collective-permute-start.2 = (bf16[384,768]{1,0:T(8,128)(2,1)}, bf16[384,768]{1,0:T(8,128)(2,1)S(1)}, u32[]{:S(2)}, u32[]{:S(2)}) collective-permute-start(bf16[384,768]{1,0:T(8,128)(2,1)} %refs_8_), channel_id=1, source_target_pairs={{0,16},{16,0},{1,17},{17,1},{2,18},{18,2},{3,19},{19,3},{4,20},{20... | collective-permute-start | bytes 1769480 | tf_op jit(solution)/shard_map/ppermute | solution.py:882
  4.2 14.4 %collective-permute-start = (bf16[1,1,1,1,144,768]{5,4,3,2,1,0:T(8,128)(2,1)S(1)}, bf16[1,1,1,1,144,768]{5,4,3,2,1,0:T(8,128)(2,1)S(1)}, u32[]{:S(2)}, u32[]{:S(2)}) collective-permute-start(bf16[1,1,1,1,144,768]{5,4,3,2,1,0:T(8,128)(2,1)S(1)} %bitcast.86), channel_id=1, source_target_pairs={{0,8},{1,9},{2,10},{3,11},{4,12},{5,13},{6,14},{7,15},{8,0},{9,1},... | collective-permute-start | bytes 663560 | tf_op jit(solution)/shard_map/ppermute | solution.py:723
  29.5 12.5 %collective-permute-start.12 = (bf16[384,3072]{1,0:T(8,128)(2,1)}, bf16[384,3072]{1,0:T(8,128)(2,1)}, u32[]{:S(2)}, u32[]{:S(2)}) collective-permute-start(bf16[384,3072]{1,0:T(8,128)(2,1)} %refs_18_), channel_id=1, source_target_pairs={{0,16},{16,0},{1,17},{17,1},{2,18},{18,2},{3,19},{19,3},{4,20},{20... | collective-permute-start | bytes 7077896 | tf_op jit(solution)/shard_map/ppermute | solution.py:882
  42.1 16.3 %collective-permute-start.16 = (bf16[1536,768]{1,0:T(8,128)(2,1)S(1)}, bf16[1536,768]{1,0:T(8,128)(2,1)S(1)}, u32[]{:S(2)}, u32[]{:S(2)}) collective-permute-start(bf16[1536,768]{1,0:T(8,128)(2,1)S(1)} %copy-done.43), channel_id=1, source_target_pairs={{0,16},{16,0},{1,17},{17,1},{2,18},{18,2},{3,19},{19,3},{4,20},{20... | collective-permute-start | bytes 7077896 | tf_op jit(solution)/shard_map/ppermute | solution.py:882
  42.1 16.2 %collective-permute-start.13 = (bf16[2,2,2,1,144,256]{5,4,3,2,1,0:T(8,128)(2,1)S(1)}, bf16[2,2,2,1,144,256]{5,4,3,2,1,0:T(8,128)(2,1)S(1)}, u32[]{:S(2)}, u32[]{:S(2)}) collective-permute-start(bf16[2,2,2,1,144,256]{5,4,3,2,1,0:T(8,128)(2,1)S(1)} %pad_maximum_fusion.3.refs_6_), channel_id=1, source_target_pairs={{0,1},{1,0},{2,3},{3,2},{4,5},{5,4},{6,7},{7,6},{8,9},{9,8},{10,11... | collective-permute-start | bytes 1769480 | tf_op jit(solution)/shard_map/ppermute | solution.py:723
  43.4 14.0 %collective-permute-start.14 = (bf16[2,2,1,2,128,256]{5,4,3,2,1,0:T(8,128)(2,1)S(1)}, bf16[2,2,1,2,128,256]{5,4,3,2,1,0:T(8,128)(2,1)S(1)}, u32[]{:S(2)}, u32[]{:S(2)}) collective-permute-start(bf16[2,2,1,2,128,256]{5,4,3,2,1,0:T(8,128)(2,1)S(1)} %pad_maximum_fusion.4.refs_8_), channel_id=1, source_target_pairs={{0,2},{1,3},{2,0},{3,1},{4,6},{5,7},{6,4},{7,5},{8,10},{9,11},{10,... | collective-permute-start | bytes 1572872 | tf_op jit(solution)/shard_map/ppermute | solution.py:723
  44.6 13.7 %collective-permute-start.15 = (bf16[2,1,2,2,128,256]{5,4,3,2,1,0:T(8,128)(2,1)S(1)}, bf16[2,1,2,2,128,256]{5,4,3,2,1,0:T(8,128)(2,1)S(1)}, u32[]{:S(2)}, u32[]{:S(2)}) collective-permute-start(bf16[2,1,2,2,128,256]{5,4,3,2,1,0:T(8,128)(2,1)S(1)} %pad_maximum_fusion.5.refs_10_), channel_id=1, source_target_pairs={{0,4},{1,5},{2,6},{3,7},{4,0},{5,1},{6,2},{7,3},{8,12},{9,13},{10,... | collective-permute-start | bytes 1572872 | tf_op jit(solution)/shard_map/ppermute | solution.py:723
  88.9 11.5 %collective-permute-start.18 = (bf16[2,2,2,384,384]{4,3,2,1,0:T(8,128)(2,1)}, bf16[2,2,2,384,384]{4,3,2,1,0:T(8,128)(2,1)S(1)}, u32[]{:S(2)}, u32[]{:S(2)}) collective-permute-start(bf16[2,2,2,384,384]{4,3,2,1,0:T(8,128)(2,1)} %get-tuple-element.229), channel_id=1, source_target_pairs={{0,16},{16,0},{1,17},{17,1},{2,18},{18,2},{3,19},{19,3},{4,20},{20... | collective-permute-start | bytes 7077896 | tf_op jit(solution)/shard_map/ppermute | solution.py:1053
  100.5 19.6 %collective-permute-start.19 = (bf16[2,2,2,1,128,384]{5,4,2,1,0,3:T(8,128)(2,1)S(1)}, bf16[2,2,2,1,128,384]{5,4,2,1,0,3:T(8,128)(2,1)S(1)}, u32[]{:S(2)}, u32[]{:S(2)}) collective-permute-start(bf16[2,2,2,1,128,384]{5,4,2,1,0,3:T(8,128)(2,1)S(1)} %get-tuple-element.237), channel_id=1, source_target_pairs={{0,1},{1,0},{2,3},{3,2},{4,5},{5,4},{6,7},{7,6},{8,9},{9,8},{10,11... | collective-permute-start | bytes 2359304 | tf_op jit(solution)/shard_map/ppermute | solution.py:723
  101.7 19.2 %collective-permute-start.20 = (bf16[2,2,1,2,128,384]{5,4,3,1,0,2:T(8,128)(2,1)S(1)}, bf16[2,2,1,2,128,384]{5,4,3,1,0,2:T(8,128)(2,1)S(1)}, u32[]{:S(2)}, u32[]{:S(2)}) collective-permute-start(bf16[2,2,1,2,128,384]{5,4,3,1,0,2:T(8,128)(2,1)S(1)} %get-tuple-element.238), channel_id=1, source_target_pairs={{0,2},{1,3},{2,0},{3,1},{4,6},{5,7},{6,4},{7,5},{8,10},{9,11},{10,... | collective-permute-start | bytes 2359304 | tf_op jit(solution)/shard_map/ppermute | solution.py:723
  102.4 19.0 %collective-permute-start.21 = (bf16[2,1,2,2,128,384]{5,4,3,2,1,0:T(8,128)(2,1)S(1)}, bf16[2,1,2,2,128,384]{5,4,3,2,1,0:T(8,128)(2,1)S(1)}, u32[]{:S(2)}, u32[]{:S(2)}) collective-permute-start(bf16[2,1,2,2,128,384]{5,4,3,2,1,0:T(8,128)(2,1)S(1)} %get-tuple-element.239), channel_id=1, source_target_pairs={{0,4},{1,5},{2,6},{3,7},{4,0},{5,1},{6,2},{7,3},{8,12},{9,13},{10,... | collective-permute-start | bytes 2359304 | tf_op jit(solution)/shard_map/ppermute | solution.py:723
  121.5 13.9 %collective-permute-start.25 = (bf16[2,2,2,208,384]{4,3,2,1,0:T(8,128)(2,1)S(1)}, bf16[2,2,2,208,384]{4,3,2,1,0:T(8,128)(2,1)S(1)}, u32[]{:S(2)}, u32[]{:S(2)}) collective-permute-start(bf16[2,2,2,208,384]{4,3,2,1,0:T(8,128)(2,1)S(1)} %get-tuple-element.267), channel_id=1, source_target_pairs={{0,16},{16,0},{1,17},{17,1},{2,18},{18,2},{3,19},{19,3},{4,20},{20... | collective-permute-start | bytes 3833864 | tf_op jit(solution)/shard_map/ppermute | solution.py:1141
  121.6 13.8 %collective-permute-start.26 = (bf16[2,2,2,208,384]{4,3,2,1,0:T(8,128)(2,1)S(1)}, bf16[2,2,2,208,384]{4,3,2,1,0:T(8,128)(2,1)S(1)}, u32[]{:S(2)}, u32[]{:S(2)}) collective-permute-start(bf16[2,2,2,208,384]{4,3,2,1,0:T(8,128)(2,1)S(1)} %get-tuple-element.268), channel_id=1, source_target_pairs={{0,16},{16,0},{1,17},{17,1},{2,18},{18,2},{3,19},{19,3},{4,20},{20... | collective-permute-start | bytes 3833864 | tf_op jit(solution)/shard_map/ppermute | solution.py:1141
  143.2 26.8 %collective-permute-start.31 = (bf16[1,1,1,1,768,384]{5,4,3,2,1,0:T(8,128)(2,1)S(1)}, bf16[1,1,1,1,768,384]{5,4,3,2,1,0:T(8,128)(2,1)S(1)}, u32[]{:S(2)}, u32[]{:S(2)}) collective-permute-start(bf16[1,1,1,1,768,384]{5,4,3,2,1,0:T(8,128)(2,1)S(1)} %slice_dynamic-update-slice_fusion), channel_id=1, source_target_pairs={{0,8},{1,9},{2,10},{3,11},{4,12},{5,13},{6,14},{7,15},{8,0},{9,1},... | collective-permute-start | bytes 1769480 | tf_op jit(solution)/shard_map/ppermute | solution.py:723
  146.9 26.7 %collective-permute-start.33 = (bf16[2,1,2,2,112,384]{5,4,3,2,1,0:T(8,128)(2,1)S(1)}, bf16[2,1,2,2,112,384]{5,4,3,2,1,0:T(8,128)(2,1)S(1)}, u32[]{:S(2)}, u32[]{:S(2)}) collective-permute-start(bf16[2,1,2,2,112,384]{5,4,3,2,1,0:T(8,128)(2,1)S(1)} %maximum_bitcast_fusion.4), channel_id=1, source_target_pairs={{0,4},{1,5},{2,6},{3,7},{4,0},{5,1},{6,2},{7,3},{8,12},{9,13},{10,... | collective-permute-start | bytes 2064392 | tf_op jit(solution)/shard_map/ppermute | solution.py:723
  147.4 26.5 %collective-permute-start.30 = (bf16[2,2,2,1,176,384]{5,4,3,2,1,0:T(8,128)(2,1)S(1)}, bf16[2,2,2,1,176,384]{5,4,3,2,1,0:T(8,128)(2,1)S(1)}, u32[]{:S(2)}, u32[]{:S(2)}) collective-permute-start(bf16[2,2,2,1,176,384]{5,4,3,2,1,0:T(8,128)(2,1)S(1)} %maximum_bitcast_fusion.1), channel_id=1, source_target_pairs={{0,1},{1,0},{2,3},{3,2},{4,5},{5,4},{6,7},{7,6},{8,9},{9,8},{10,11... | collective-permute-start | bytes 3244040 | tf_op jit(solution)/shard_map/ppermute | solution.py:723
  148.6 25.7 %collective-permute-start.32 = (bf16[2,2,1,2,176,384]{5,4,3,2,1,0:T(8,128)(2,1)S(1)}, bf16[2,2,1,2,176,384]{5,4,3,2,1,0:T(8,128)(2,1)S(1)}, u32[]{:S(2)}, u32[]{:S(2)}) collective-permute-start(bf16[2,2,1,2,176,384]{5,4,3,2,1,0:T(8,128)(2,1)S(1)} %maximum_bitcast_fusion.2), channel_id=1, source_target_pairs={{0,2},{1,3},{2,0},{3,1},{4,6},{5,7},{6,4},{7,5},{8,10},{9,11},{10,... | collective-permute-start | bytes 3244040 | tf_op jit(solution)/shard_map/ppermute | solution.py:723
  177.9 14.1 %collective-permute-start.34 = (bf16[2,2,1,1,176,384]{5,4,3,2,1,0:T(8,128)(2,1)S(1)}, bf16[2,2,1,1,176,384]{5,4,3,2,1,0:T(8,128)(2,1)S(1)}, u32[]{:S(2)}, u32[]{:S(2)}) collective-permute-start(bf16[2,2,1,1,176,384]{5,4,3,2,1,0:T(8,128)(2,1)S(1)} %slice.442), channel_id=1, source_target_pairs={{0,2},{1,3},{2,0},{3,1},{4,6},{5,7},{6,4},{7,5},{8,10},{9,11},{10,... | collective-permute-start | bytes 1622024 | tf_op jit(solution)/shard_map/ppermute | solution.py:723
  182.5 11.5 %collective-permute-start.38 = (bf16[2,1,1,2,176,384]{5,4,3,2,1,0:T(8,128)(2,1)S(1)}, bf16[2,1,1,2,176,384]{5,4,3,2,1,0:T(8,128)(2,1)S(1)}, u32[]{:S(2)}, u32[]{:S(2)}) collective-permute-start(bf16[2,1,1,2,176,384]{5,4,3,2,1,0:T(8,128)(2,1)S(1)} %slice.443), channel_id=1, source_target_pairs={{0,4},{1,5},{2,6},{3,7},{4,0},{5,1},{6,2},{7,3},{8,12},{9,13},{10,... | collective-permute-start | bytes 1622024 | tf_op jit(solution)/shard_map/ppermute | solution.py:723
  209.0 17.8 %collective-permute-start.46 = (bf16[1,1,1,1,672,384]{5,4,3,2,1,0:T(8,128)(2,1)S(1)}, bf16[1,1,1,1,672,384]{5,4,3,2,1,0:T(8,128)(2,1)S(1)}, u32[]{:S(2)}, u32[]{:S(2)}) collective-permute-start(bf16[1,1,1,1,672,384]{5,4,3,2,1,0:T(8,128)(2,1)S(1)} %slice_dynamic-update-slice_fusion.8), channel_id=1, source_target_pairs={{0,8},{1,9},{2,10},{3,11},{4,12},{5,13},{6,14},{7,15},{8,0},{9,1},... | collective-permute-start | bytes 1548296 | tf_op jit(solution)/shard_map/ppermute | solution.py:723
  209.9 27.4 %collective-permute-start.50 = (bf16[2,2,2,1,128,384]{5,4,2,1,0,3:T(8,128)(2,1)S(1)}, bf16[2,2,2,1,128,384]{5,4,2,1,0,3:T(8,128)(2,1)S(1)}, u32[]{:S(2)}, u32[]{:S(2)}) collective-permute-start(bf16[2,2,2,1,128,384]{5,4,2,1,0,3:T(8,128)(2,1)S(1)} %pad_maximum_fusion), channel_id=1, source_target_pairs={{0,1},{1,0},{2,3},{3,2},{4,5},{5,4},{6,7},{7,6},{8,9},{9,8},{10,11... | collective-permute-start | bytes 2359304 | tf_op jit(solution)/shard_map/ppermute | solution.py:723
  211.2 26.1 %collective-permute-start.51 = (bf16[2,2,1,2,128,384]{5,4,3,1,0,2:T(8,128)(2,1)S(1)}, bf16[2,2,1,2,128,384]{5,4,3,1,0,2:T(8,128)(2,1)S(1)}, u32[]{:S(2)}, u32[]{:S(2)}) collective-permute-start(bf16[2,2,1,2,128,384]{5,4,3,1,0,2:T(8,128)(2,1)S(1)} %pad_maximum_fusion.1), channel_id=1, source_target_pairs={{0,2},{1,3},{2,0},{3,1},{4,6},{5,7},{6,4},{7,5},{8,10},{9,11},{10,... | collective-permute-start | bytes 2359304 | tf_op jit(solution)/shard_map/ppermute | solution.py:723
  212.0 25.3 %collective-permute-start.52 = (bf16[2,1,2,2,128,384]{5,4,3,2,1,0:T(8,128)(2,1)S(1)}, bf16[2,1,2,2,128,384]{5,4,3,2,1,0:T(8,128)(2,1)S(1)}, u32[]{:S(2)}, u32[]{:S(2)}) collective-permute-start(bf16[2,1,2,2,128,384]{5,4,3,2,1,0:T(8,128)(2,1)S(1)} %pad_maximum_fusion.2.refs_4_), channel_id=1, source_target_pairs={{0,4},{1,5},{2,6},{3,7},{4,0},{5,1},{6,2},{7,3},{8,12},{9,13},{10,... | collective-permute-start | bytes 2359304 | tf_op jit(solution)/shard_map/ppermute | solution.py:723
  (83 other events, 710.1 us)
